TPU v7x, 32 devices: a whole 2x2x4 slice. The times are simulated.
32 devices in a mesh: member: 2 (over x), lat: 16 (over z, y, core).
Axes of the slice: x: 2, y: 2, z: 4, core: 2. Of those that a mesh axis runs over, the one named last changes fastest.
Arguments:
- state: float32 [10, 128, 128, 256], P('member', None, 'lat'), parts along dimension 0, may hold values from -6 to 6
- wind: float32 [256, 128, 256], P('member', 'lat'), parts along dimension 0, may hold values from -0.9 to 0.9
- sunlight: float32 [256, 256], P(('member', 'lat')), parts along dimension 0, may hold values from 0.1 to 1
- day_list: int32 [32, 16], P(('member', 'lat')), parts along dimension 0, may hold values from -1 to 15, as said below
- w_first: bfloat16 [640, 2048], replicated, may hold values from -0.25 to 0.25
- bias: float32 [2048], replicated, may hold values from -3 to 3
- w_second: bfloat16 [2048, 128], replicated, may hold values from -0.125 to 0.125
- remap: float32 [128, 128], replicated, may hold values from -1.5 to 2
Outputs:
- new_state: float32 [10, 128, 128, 256], P('member', None, 'lat'), parts along dimension 0
There are 2 independent parts, one for each index of `member`. A program takes and returns all parts, laid end to end along the dimension named above; an argument that names none is the same for every part. Nothing has to cross between parts.
Inputs may be any that keep to these rules, and one draw needn't show every extreme that they name: `day_list`: row d names the daylit blocks of band d, each once, as a cyclic run of consecutive numbers placed first, then -1; every row names at least one block. Rows d and d + 8 together name at most 20 blocks; row 0 names all 16 and row 8 exactly 4.
All inputs are finite; a program needn't handle non-finite values.
Results may differ from a plain program's by a relative error of at most 0.00062.
Values may be sent and summed in bfloat16 or wider, within the bound.
No kernel may reach another device: no remote copies, remote signals or barrier semaphores. Data moves between devices by JAX's collectives and lax.ppermute only.
A program may use at most 128 MiB of HBM per device.

v0:
```python
import jax
import jax.numpy as jnp
from jax import lax
from jax.sharding import PartitionSpec as P

STEPS = 2


def shifted(block, axis, distance):
    devices = range(lax.axis_size(axis))
    route = [(i - distance, i) for i in devices if i - distance in devices]
    return lax.ppermute(block, axis, route)


def padded_2(x, sides, width):
    for axis, dim in sides:
        count, length = (lax.axis_size(axis), x.shape[dim])
        up = [(i, (i + 1) % count) for i in range(count - 1)]
        down = [(j, i) for i, j in up]
        last = lax.slice_in_dim(x, length - width, length, axis=dim)
        leading = lax.slice_in_dim(x, 0, width, axis=dim)
        before = lax.ppermute(last, axis, up)
        after = lax.ppermute(leading, axis, down)
        x = jnp.concatenate([before, x, after], axis=dim)
    return x


def min_mod(left, right):
    return 0.5 * (jnp.sign(left) + jnp.sign(right)) * jnp.minimum(jnp.abs(left), jnp.abs(right))


def advance(padded, courant):
    length = padded.shape[2] - 4
    slopes = min_mod(padded[:, :, 2:] - padded[:, :, 1:-1], padded[:, :, 1:-1] - padded[:, :, :-2])
    upper_q = padded[:, :, 1 : length + 2]
    upper_s = slopes[:, :, 0 : length + 1]
    lower_q = padded[:, :, 2 : length + 3]
    lower_s = slopes[:, :, 1 : length + 2]
    speed = courant[None]
    fluxes = jnp.where(
        speed > 0.0,
        speed * (upper_q + 0.5 * (1.0 - speed) * upper_s),
        speed * (lower_q - 0.5 * (1.0 + speed) * lower_s),
    )
    return padded[:, :, 2 : length + 2] - (fluxes[:, :, 1:] - fluxes[:, :, :-1])


def radiate(sources, slot_index, w_shaped, bias, w_second):
    picked = jnp.take(sources, slot_index, axis=2)
    hidden = (
        jnp.einsum("flkc,flh->kch", picked, w_shaped, preferred_element_type=jnp.float32) + bias
    )
    hidden = jax.nn.gelu(hidden, approximate=True).astype(jnp.bfloat16)
    return jnp.einsum("kch,hl->klc", hidden, w_second, preferred_element_type=jnp.float32)


def place_blocks(listed, results, block_ids):
    owner = (listed[None, :] == block_ids[:, None]).astype(jnp.float32)
    return jnp.einsum("bs,slc->lbc", owner, results, precision=lax.Precision.HIGHEST)


def shards(state, wind, sunlight, day_list, w_first, bias, w_second, remap):
    fields, levels, rows, lons = state.shape
    next_row = shifted(wind[:, :1, :], "lat", -1)
    courant = jnp.concatenate([wind, next_row], axis=1)
    current = state
    for step in range(STEPS):
        padded = padded_2(current, (("lat", 2),), 2)
        current = advance(padded, courant)
    columns = current.reshape(fields, levels, rows * lons)
    remapped = jnp.einsum("km,fmc->fkc", remap, columns, precision=lax.Precision.HIGHEST)
    blocks = day_list.shape[1]
    block_width = rows * lons // blocks
    inputs = remapped.astype(jnp.bfloat16).reshape(fields, levels, blocks, block_width)
    w_shaped = w_first.reshape(fields, levels, w_first.shape[1])
    listed = day_list[0]
    block_ids = jnp.arange(blocks, dtype=jnp.int32)
    safe_ids = jnp.maximum(listed, 0)
    results = radiate(inputs, safe_ids, w_shaped, bias, w_second)
    heating = place_blocks(listed, results, block_ids)
    heating = heating.reshape(levels, rows * lons) * sunlight.reshape(1, rows * lons)
    output = jnp.concatenate([remapped[:1] + heating[None], remapped[1:]], axis=0)
    return output.reshape(fields, levels, rows, lons)


def solution(mesh):
    placed = (
        P("member", None, "lat", None),
        P("member", "lat", None),
        P(("member", "lat"), None),
        P(("member", "lat"), None),
        P(),
        P(),
        P(),
        P(),
    )
    return jax.shard_map(
        shards,
        mesh=mesh,
        in_specs=placed,
        out_specs=P("member", None, "lat", None),
        check_vma=False,
    )
```

profile of v0, /device:TPU:22, one launch (start us, length us, event | category | flops | bytes accessed | tf_op | source)
XLA Modules:
  0.0 197.0 jit_solution(10704786735371431547)
XLA Ops:
  0.0 5.2 %fusion.57 = (f32[5,128,2,256]{3,2,1,0:T(2,128)S(1)}, f32[5,128,2,256]{3,2,1,0:T(2,128)S(1)}) fusion(f32[5,128,8,256]{3,2,1,0:T(8,128)} %param.8), kind=kLoop, calls=%fused_computation.86 | loop fusion | bytes 5242880 | tf_op jit(solution)/shard_map/slice | solution.py:20
  5.2 1.2 copy.77
  6.4 1.9 collective-permute-start.1
  8.3 1.2 copy.78
  9.5 3.6 %collective-permute-start.2 = (f32[5,128,2,256]{3,1,2,0:T(8,128)}, f32[5,128,2,256]{3,1,2,0:T(8,128)}, u32[]{:S(2)}, u32[]{:S(2)}) collective-permute-start(f32[5,128,2,256]{3,1,2,0:T(8,128)} %copy.78), channel_id=1, source_target_pairs={{1,0},{2,1},{3,2},{4,3},{5,4},{6,5},{7,6},{8,7},{9,8},{10,9},{11,1... | collective-permute-start | bytes 3932168 | tf_op jit(solution)/shard_map/ppermute | solution.py:23
  13.2 1.9 collective-permute-start
  15.2 1.4 constant_dynamic-update-slice_fusion.1
  16.5 6.1 %copy.66 = f32[5,128,8,256]{1,3,2,0:T(8,128)} copy(f32[5,128,8,256]{3,2,1,0:T(8,128)} %param.8) | data formatting | bytes 10485760 | tf_op args[0]
  22.6 17.3 %collective-permute-done = f32[128,1,256]{2,0,1:T(8,128)S(1)} collective-permute-done((f32[128,1,256]{2,0,1:T(8,128)S(1)}, f32[128,1,256]{2,0,1:T(8,128)S(1)}, u32[]{:S(2)}, u32[]{:S(2)}) %collective-permute-start) | collective-permute-done | bytes 131104 | tf_op jit(solution)/shard_map/ppermute | solution.py:12
  39.9 0.6 constant_dynamic-update-slice_fusion
  40.6 2.7 %copy.54 = f32[128,9,256]{0,2,1:T(8,128)} copy(f32[128,9,256]{2,0,1:T(8,128)} %constant_dynamic-update-slice_fusion) | data formatting | bytes 2359296 | tf_op jit(solution)/shard_map/concatenate | solution.py:65
  43.2 2.9 %subtract_multiply_fusion = (f32[128,9,256]{2,0,1:T(8,128)}, f32[128,9,256]{2,0,1:T(8,128)}) fusion(f32[128,9,256]{2,0,1:T(8,128)} %constant_dynamic-update-slice_fusion), kind=kLoop, calls=%fused_computation.66 | loop fusion | flops 1179648 | bytes 3538944 | tf_op jit(solution)/shard_map/mul | solution.py:42
  46.2 2.6 %copy.58 = f32[128,9,256]{0,2,1:T(8,128)} copy(f32[128,9,256]{2,0,1:T(8,128)} %get-tuple-element.9) | data formatting | bytes 2359296 | tf_op jit(solution)/shard_map/mul | solution.py:42
  48.8 2.6 %copy.65 = f32[128,9,256]{0,2,1:T(8,128)} copy(f32[128,9,256]{2,0,1:T(8,128)} %get-tuple-element.10) | data formatting | bytes 2359296 | tf_op jit(solution)/shard_map/mul | solution.py:43
  51.5 1.4 broadcast_compare_fusion
  52.9 1.1 copy.53
  54.0 2.8 %copy.56 = f32[5,128,2,256]{1,3,2,0:T(8,128)} copy(f32[5,128,2,256]{3,1,2,0:T(8,128)} %collective-permute-done.1) | data formatting | bytes 2621440 | tf_op jit(solution)/shard_map/ppermute | solution.py:22
  56.8 2.9 %copy.61 = f32[5,128,2,256]{1,3,2,0:T(8,128)} copy(f32[5,128,2,256]{3,1,2,0:T(8,128)} %collective-permute-done.2) | data formatting | bytes 2621440 | tf_op jit(solution)/shard_map/ppermute | solution.py:23
  59.7 9.1 %minimum_multiply_fusion.1 = f32[5,128,10,256]{1,3,2,0:T(8,128)S(1)} fusion(f32[5,128,8,256]{1,3,2,0:T(8,128)} %copy.66, f32[5,128,2,256]{1,3,2,0:T(8,128)} %copy.56, f32[5,128,2,256]{1,3,2,0:T(8,128)} %copy.61), kind=kLoop, calls=%fused_computation.33 | loop fusion | flops 22937600 | bytes 14417920 | tf_op jit(solution)/shard_map/mul | solution.py:29
  68.8 0.0 slice-start.3
  68.8 8.7 %fusion.24 = f32[5,128,9,256]{1,3,2,0:T(8,128)} fusion(f32[5,128,8,256]{1,3,2,0:T(8,128)} %copy.66, f32[5,128,2,256]{1,3,2,0:T(8,128)} %copy.61, f32[5,128,2,256]{1,3,2,0:T(8,128)} %copy.56, f32[5,128,10,256]{1,3,2,0:T(8,128)S(1)} %minimum_multiply_fusion.1, f32[128,9,256]{0,2,1:T(8,128)} %copy.65, f32[128,9,256]{0,2,1:T(8,128)} %copy.58, ...), kind=kLoop, calls=%fused_computation.44 | loop fusion | flops 13271040 | bytes 29392896 | tf_op jit(solution)/shard_map/jit(_where)/select_n | solution.py:40
  77.5 5.5 %fusion.29 = f32[5,128,8,256]{1,3,2,0:T(8,128)S(1)} fusion(f32[5,128,8,256]{1,3,2,0:T(8,128)S(1)} %bitcast.54, f32[5,128,9,256]{1,3,2,0:T(8,128)} %fusion.24), kind=kLoop, calls=%fused_computation.55 | loop fusion | flops 2621440 | bytes 20971520 | tf_op jit(solution)/shard_map/sub | solution.py:45
  83.0 0.0 copy-start.1
  83.0 2.3 %copy-done.1 = f32[5,128,8,256]{1,3,2,0:T(8,128)} copy-done((f32[5,128,8,256]{1,3,2,0:T(8,128)}, f32[5,128,8,256]{1,3,2,0:T(8,128)S(1)}, u32[]{:S(2)}) %copy-start.1) | copy-done | bytes 5242904
  85.3 1.7 fusion.56
  87.0 2.8 %copy.67 = f32[5,128,2,256]{3,1,2,0:T(8,128)} copy(f32[5,128,2,256]{1,3,2,0:T(8,128)} %get-tuple-element.5) | data formatting | bytes 2621440 | tf_op jit(solution)/shard_map/slice | solution.py:20
  89.8 1.9 collective-permute-start.3
  91.8 2.8 %copy.69 = f32[5,128,2,256]{3,1,2,0:T(8,128)} copy(f32[5,128,2,256]{1,3,2,0:T(8,128)} %get-tuple-element.6) | data formatting | bytes 2621440 | tf_op jit(solution)/shard_map/slice | solution.py:21
  94.5 4.0 %collective-permute-start.4 = (f32[5,128,2,256]{3,1,2,0:T(8,128)}, f32[5,128,2,256]{3,1,2,0:T(8,128)}, u32[]{:S(2)}, u32[]{:S(2)}) collective-permute-start(f32[5,128,2,256]{3,1,2,0:T(8,128)} %copy.69), channel_id=1, source_target_pairs={{1,0},{2,1},{3,2},{4,3},{5,4},{6,5},{7,6},{8,7},{9,8},{10,9},{11,1... | collective-permute-start | bytes 3932168 | tf_op jit(solution)/shard_map/ppermute | solution.py:23
  98.6 24.7 %collective-permute-done.3 = f32[5,128,2,256]{3,1,2,0:T(8,128)} collective-permute-done((f32[5,128,2,256]{3,1,2,0:T(8,128)}, f32[5,128,2,256]{3,1,2,0:T(8,128)}, u32[]{:S(2)}, u32[]{:S(2)}) %collective-permute-start.3) | collective-permute-done | bytes 1310752 | tf_op jit(solution)/shard_map/ppermute | solution.py:22
  123.3 2.8 %copy.68 = f32[5,128,2,256]{1,3,2,0:T(8,128)} copy(f32[5,128,2,256]{3,1,2,0:T(8,128)} %collective-permute-done.3) | data formatting | bytes 2621440 | tf_op jit(solution)/shard_map/ppermute | solution.py:22
  126.1 2.9 %copy.70 = f32[5,128,2,256]{1,3,2,0:T(8,128)} copy(f32[5,128,2,256]{3,1,2,0:T(8,128)} %collective-permute-done.4) | data formatting | bytes 2621440 | tf_op jit(solution)/shard_map/ppermute | solution.py:23
  129.0 9.1 %minimum_multiply_fusion = f32[5,128,10,256]{1,3,2,0:T(8,128)S(1)} fusion(f32[5,128,8,256]{1,3,2,0:T(8,128)} %copy-done.1, f32[5,128,2,256]{1,3,2,0:T(8,128)} %copy.68, f32[5,128,2,256]{1,3,2,0:T(8,128)} %copy.70), kind=kLoop, calls=%fused_computation.32 | loop fusion | flops 22937600 | bytes 14417920 | tf_op jit(solution)/shard_map/mul | solution.py:29
  138.1 0.0 slice-start.1
  138.1 8.7 %fusion.17 = f32[5,128,9,256]{1,3,2,0:T(8,128)} fusion(f32[5,128,8,256]{1,3,2,0:T(8,128)} %copy-done.1, f32[5,128,2,256]{1,3,2,0:T(8,128)} %copy.70, f32[5,128,2,256]{1,3,2,0:T(8,128)} %copy.68, f32[5,128,10,256]{1,3,2,0:T(8,128)S(1)} %minimum_multiply_fusion, f32[128,9,256]{0,2,1:T(8,128)} %copy.65, f32[128,9,256]{0,2,1:T(8,128)} %copy.58, ...), kind=kLoop, calls=%fused_computation.37 | loop fusion | flops 13271040 | bytes 29392896 | tf_op jit(solution)/shard_map/jit(_where)/select_n | solution.py:40
  146.8 0.0 copy-start.4
  146.8 5.5 %fusion.28 = f32[5,128,8,256]{1,3,2,0:T(8,128)S(1)} fusion(f32[5,128,8,256]{1,3,2,0:T(8,128)S(1)} %bitcast.52, f32[5,128,9,256]{1,3,2,0:T(8,128)} %fusion.17), kind=kLoop, calls=%fused_computation.53 | loop fusion | flops 2621440 | bytes 20971520 | tf_op jit(solution)/shard_map/sub | solution.py:45
  152.3 0.0 copy-start.8
  152.3 6.4 %fusion.58 = (bf16[5,128,2048]{1,2,0:T(8,128)(2,1)}, f32[5,128,2048]{1,2,0:T(8,128)}) fusion(f32[5,128,2048]{1,2,0:T(8,128)S(1)} %bitcast.55, f32[128,128]{1,0:T(8,128)S(1)} %copy-done.4), kind=kOutput, calls=%fused_computation.87 | convolution fusion | flops 2014576640 | bytes 13172736 | tf_op jit(solution)/shard_map/km,fmc->fkc/dot_general | solution.py:71
  158.7 4.1 %gather_fusion = bf16[16,5,128,128]{2,3,1,0:T(8,128)(2,1)} fusion(bf16[5,128,16,128]{1,3,2,0:T(8,128)(2,1)} %bitcast.57, s32[1024]{0:T(1024)S(1)} %pad_clamp_fusion), kind=kCustom, calls=%fused_computation | custom fusion | bytes 5242944 | tf_op jit(solution)/shard_map/jit(_take)/gather | solution.py:49
  162.9 13.2 %fusion.38 = f32[16,128,128]{1,2,0:T(8,128)} fusion(f32[2048]{0:T(1024)S(1)} %copy-done.8, bf16[5,128,2048,1]{2,1,0,3:T(8,128)(2,1)S(1)} %bitcast.50, bf16[16,5,128,128]{2,3,1,0:T(8,128)(2,1)} %gather_fusion, pred[16]{0:T(512)(128)(4,1)S(1)} %maximum_compare_fusion, bf16[2048,128]{1,0:T(8,128)(2,1)S(1)} %copy-done.7), kind=kOutput, calls=%fused_computation.63 | convolution fusion | flops 6485704704 | bytes 6823952 | tf_op jit(solution)/shard_map/kch,hl->klc/dot_general | solution.py:54
  176.1 2.6 %copy.73 = f32[16,128,128]{2,0,1:T(8,128)} copy(f32[16,128,128]{1,2,0:T(8,128)} %fusion.38) | data formatting | bytes 2097152 | tf_op jit(solution)/shard_map/kch,hl->klc/transpose | solution.py:54
  178.7 2.8 %convolution_bitcast_fusion.1 = f32[128,16,128]{2,1,0:T(8,128)} fusion(f32[16,128,128]{2,0,1:T(8,128)} %copy.73, s32[16]{0:T(128)S(1)} %bitcast.60), kind=kOutput, calls=%fused_computation.62 | convolution fusion | flops 50331904 | bytes 2097216 | tf_op jit(solution)/shard_map/bs,slc->lbc/dot_general | solution.py:59
  181.5 2.6 %copy.74 = f32[128,16,128]{0,2,1:T(8,128)} copy(f32[128,16,128]{2,1,0:T(8,128)} %convolution_bitcast_fusion.1) | data formatting | bytes 2097152 | tf_op jit(solution)/shard_map/bs,slc->lbc/transpose | solution.py:59
  184.1 2.5 %slice.120 = f32[4,128,2048]{1,2,0:T(8,128)S(1)} slice(f32[5,128,2048]{1,2,0:T(8,128)} %get-tuple-element.12), slice={[1:5], [0:128], [0:2048]} | slice | bytes 8388608 | tf_op jit(solution)/shard_map/slice | solution.py:82
  186.6 1.6 slice_add_fusion
  188.2 2.7 %pad_maximum_fusion.8 = f32[5,128,2048]{1,2,0:T(8,128)} fusion(f32[4,128,2048]{1,2,0:T(8,128)S(1)} %slice.120, f32[1,128,2048]{1,2,0:T(8,128)S(1)} %slice_add_fusion), kind=kLoop, calls=%fused_computation.56 | loop fusion | flops 1310720 | bytes 10485760 | tf_op jit(solution)/shard_map/concatenate | solution.py:82
  190.9 6.1 %copy.75 = f32[5,128,8,256]{3,2,1,0:T(8,128)} copy(f32[5,128,8,256]{1,3,2,0:T(8,128)} %bitcast.56) | data formatting | bytes 10485760 | tf_op jit(solution)/shard_map/reshape | solution.py:83
  (32 shorter events, 0.1 us)
Async XLA Ops:
  0.0 162.9 %copy-start = (bf16[640,2048]{1,0:T(8,128)(2,1)S(1)}, bf16[640,2048]{1,0:T(8,128)(2,1)}, u32[]{:S(2)}) copy-start(bf16[640,2048]{1,0:T(8,128)(2,1)} %param.12) | copy-start | bytes 7864324
  0.0 13.2 %slice-start.4 = ((f32[128,8,256]{2,1,0:T(8,128)}), f32[128,1,256]{2,1,0:T(1,128)S(1)}, s32[]{:S(2)}) async-start(f32[128,8,256]{2,1,0:T(8,128)} %param.9), calls=%async_computation.4 | async-start | bytes 262144 | tf_op jit(solution)/shard_map/slice | solution.py:64
  0.0 15.1 %copy-start.3 = (f32[128,8,256]{2,1,0:T(8,128)S(1)}, f32[128,8,256]{2,1,0:T(8,128)}, u32[]{:S(2)}) copy-start(f32[128,8,256]{2,1,0:T(8,128)} %param.9) | copy-start | bytes 3145732
  6.4 47.6 %collective-permute-start.1 = (f32[5,128,2,256]{3,1,2,0:T(8,128)}, f32[5,128,2,256]{3,1,2,0:T(8,128)}, u32[]{:S(2)}, u32[]{:S(2)}) collective-permute-start(f32[5,128,2,256]{3,1,2,0:T(8,128)} %copy.77), channel_id=1, source_target_pairs={{0,1},{1,2},{2,3},{3,4},{4,5},{5,6},{6,7},{7,8},{8,9},{9,10},{10,1... | collective-permute-start | bytes 3932168 | tf_op jit(solution)/shard_map/ppermute | solution.py:22
  9.5 47.2 %collective-permute-start.2 = (f32[5,128,2,256]{3,1,2,0:T(8,128)}, f32[5,128,2,256]{3,1,2,0:T(8,128)}, u32[]{:S(2)}, u32[]{:S(2)}) collective-permute-start(f32[5,128,2,256]{3,1,2,0:T(8,128)} %copy.78), channel_id=1, source_target_pairs={{1,0},{2,1},{3,2},{4,3},{5,4},{6,5},{7,6},{8,7},{9,8},{10,9},{11,1... | collective-permute-start | bytes 3932168 | tf_op jit(solution)/shard_map/ppermute | solution.py:23
  13.2 26.7 %collective-permute-start = (f32[128,1,256]{2,0,1:T(8,128)S(1)}, f32[128,1,256]{2,0,1:T(8,128)S(1)}, u32[]{:S(2)}, u32[]{:S(2)}) collective-permute-start(f32[128,1,256]{2,0,1:T(8,128)S(1)} %copy.81), channel_id=1, source_target_pairs={{1,0},{2,1},{3,2},{4,3},{5,4},{6,5},{7,6},{8,7},{9,8},{10,9},{11,1... | collective-permute-start | bytes 393224 | tf_op jit(solution)/shard_map/ppermute | solution.py:12
  59.7 17.8 %slice-start.2 = ((s8[5242880]{0:T(1024)(128)(4,1)}), s8[4194304]{0:T(1024)(128)(4,1)S(1)}, s32[]{:S(2)}) async-start(s8[5242880]{0:T(1024)(128)(4,1)} %bitcast.53), calls=%async_computation.2 | async-start | bytes 8388608
  68.8 8.7 %slice-start.3 = ((s8[5242880]{0:T(1024)(128)(4,1)}), s8[1048576]{0:T(1024)(128)(4,1)S(1)}, s32[]{:S(2)}) async-start(s8[5242880]{0:T(1024)(128)(4,1)} %bitcast.53), calls=%async_computation.3 | async-start | bytes 2097152
  83.0 2.4 %copy-start.1 = (f32[5,128,8,256]{1,3,2,0:T(8,128)}, f32[5,128,8,256]{1,3,2,0:T(8,128)S(1)}, u32[]{:S(2)}) copy-start(f32[5,128,8,256]{1,3,2,0:T(8,128)S(1)} %fusion.29) | copy-start | bytes 15728644
  85.3 13.2 %copy-start.5 = (f32[8,256]{1,0:T(8,128)S(1)}, f32[8,256]{1,0:T(8,128)}, u32[]{:S(2)}) copy-start(f32[8,256]{1,0:T(8,128)} %param.10) | copy-start | bytes 24580
  85.3 13.2 %copy-start.6 = (s32[1,16]{1,0:T(1,128)S(1)}, s32[1,16]{1,0:T(1,128)}, u32[]{:S(2)}) copy-start(s32[1,16]{1,0:T(1,128)} %param.11) | copy-start | bytes 196
  89.8 33.4 %collective-permute-start.3 = (f32[5,128,2,256]{3,1,2,0:T(8,128)}, f32[5,128,2,256]{3,1,2,0:T(8,128)}, u32[]{:S(2)}, u32[]{:S(2)}) collective-permute-start(f32[5,128,2,256]{3,1,2,0:T(8,128)} %copy.67), channel_id=1, source_target_pairs={{0,1},{1,2},{2,3},{3,4},{4,5},{5,6},{6,7},{7,8},{8,9},{9,10},{10,1... | collective-permute-start | bytes 3932168 | tf_op jit(solution)/shard_map/ppermute | solution.py:22
  94.5 31.5 %collective-permute-start.4 = (f32[5,128,2,256]{3,1,2,0:T(8,128)}, f32[5,128,2,256]{3,1,2,0:T(8,128)}, u32[]{:S(2)}, u32[]{:S(2)}) collective-permute-start(f32[5,128,2,256]{3,1,2,0:T(8,128)} %copy.69), channel_id=1, source_target_pairs={{1,0},{2,1},{3,2},{4,3},{5,4},{6,5},{7,6},{8,7},{9,8},{10,9},{11,1... | collective-permute-start | bytes 3932168 | tf_op jit(solution)/shard_map/ppermute | solution.py:23
  129.0 17.8 %slice-start = ((s8[5242880]{0:T(1024)(128)(4,1)}), s8[4194304]{0:T(1024)(128)(4,1)S(1)}, s32[]{:S(2)}) async-start(s8[5242880]{0:T(1024)(128)(4,1)} %bitcast.51), calls=%async_computation | async-start | bytes 8388608
  138.1 8.7 %slice-start.1 = ((s8[5242880]{0:T(1024)(128)(4,1)}), s8[1048576]{0:T(1024)(128)(4,1)S(1)}, s32[]{:S(2)}) async-start(s8[5242880]{0:T(1024)(128)(4,1)} %bitcast.51), calls=%async_computation.1 | async-start | bytes 2097152
  146.8 5.5 %copy-start.4 = (f32[128,128]{1,0:T(8,128)S(1)}, f32[128,128]{1,0:T(8,128)}, u32[]{:S(2)}) copy-start(f32[128,128]{1,0:T(8,128)} %param.15) | copy-start | bytes 196612
  152.3 10.6 %copy-start.7 = (bf16[2048,128]{1,0:T(8,128)(2,1)S(1)}, bf16[2048,128]{1,0:T(8,128)(2,1)}, u32[]{:S(2)}) copy-start(bf16[2048,128]{1,0:T(8,128)(2,1)} %param.14) | copy-start | bytes 1572868
  152.3 10.5 %copy-start.8 = (f32[2048]{0:T(1024)S(1)}, f32[2048]{0:T(1024)}, u32[]{:S(2)}) copy-start(f32[2048]{0:T(1024)} %param.13) | copy-start | bytes 24580
  184.1 2.6 %copy-start.2 = (f32[128,16,128]{0,2,1:T(8,128)S(1)}, f32[128,16,128]{0,2,1:T(8,128)}, u32[]{:S(2)}) copy-start(f32[128,16,128]{0,2,1:T(8,128)} %copy.74) | copy-start | bytes 3145732
where the time goes:
time: 198 us; the launch traced here: 197 us
  local copies, waits for them, and re-layouts  63.8 us (32%)
  other arithmetic  55.2 us (28%)
  waiting for transfers between devices  42 us (21%)
  matrix products  22.3 us (11%)
  starting transfers between devices  13.4 us (7%)
    ppermute x2, waiting for transfers between devices, padded_2(): before = lax.ppermute(last, axis, up)  24.7 us
    mul x2, other arithmetic, min_mod(): 0.5 * (jnp.sign(left) + jnp.sign(right))  18.2 us
    select_n x2, other arithmetic, advance(): jnp.where(speed > 0.0, speed * (upper_q + 0.5 * (1.0 - speed) * upper_s),...  17.4 us
    ppermute x1, waiting for transfers between devices, shifted(): return lax.ppermute(block, axis, route)  17.3 us
    dot_general x1, matrix products, radiate(): jnp.einsum('kch,hl->klc', hidden, w_second, preferred_element_type=jnp.fl...  13.2 us
    unnamed x32, local copies, waits for them, and re-layouts  12.3 us
    sub x2, other arithmetic, advance(): return padded[:, :, 2:length + 2] - (fluxes[:, :, 1:] - fluxes[:, :, :-1])  11 us
    slice x3, local copies, waits for them, and re-layouts, padded_2(): last = lax.slice_in_dim(x, length - width, length, axis=dim)  9.69 us
  transfers between devices with their start and end apart: 5, of which 2 were waited for; matrix products, arithmetic and copies ran while one was open for 16% of the time, Pallas kernels for 0%

commit v1 on v0

v1 whole, which is shorter than its diff:
```python
import functools
import jax
import jax.numpy as jnp
from jax import lax
from jax.experimental import pallas as pl
from jax.experimental.pallas import tpu as pltpu
from jax.sharding import PartitionSpec as P

LANES = 128
KB = 32
GELU_A = 0.7978845608028654
GELU_B = 0.7978845608028654 * 0.044715
ANY = pl.BlockSpec(memory_space=pl.ANY)


def limited(ahead, behind):
    return jnp.maximum(jnp.minimum(ahead, jnp.maximum(behind, 0.0)), jnp.minimum(behind, 0.0))


def face(speed):
    size = jnp.abs(speed)
    return speed > 0.0, speed, size * (0.5 - 0.5 * size)


def rows_after(q, faces):
    diffs = [b - a for a, b in zip(q[:-1], q[1:])]
    slopes = [None] + [limited(b, a) for a, b in zip(diffs[:-1], diffs[1:])]
    fluxes = []
    for j, (mask, speed, half) in enumerate(faces):
        edge = jnp.where(mask, q[j + 1], q[j + 2])
        slope = jnp.where(mask, slopes[j + 1], slopes[j + 2])
        fluxes.append(speed * edge + half * slope)
    return [q[j + 2] - (fluxes[j + 1] - fluxes[j]) for j in range(len(faces) - 1)]


def row_of(ref, start, count, rows):
    return ref[pl.ds(start, count, stride=rows), :]


def pack_kernel(state_ref, wind_ref, up_ref, down_ref):
    fields, levels, rows, lanes = state_ref.shape
    flat = state_ref.reshape(fields * levels * rows, lanes)
    winds = wind_ref.reshape(levels * rows, lanes)
    for f in range(fields):
        for r in range(2):
            first = row_of(flat, f * levels * rows + r, levels, rows)
            down_ref[0, r * fields + f] = first.astype(jnp.bfloat16)
            last = row_of(flat, f * levels * rows + rows - 2 + r, levels, rows)
            up_ref[0, r * fields + f] = last.astype(jnp.bfloat16)
    speed = row_of(winds, 0, levels, rows)
    high = speed.astype(jnp.bfloat16)
    down_ref[0, 2 * fields] = high
    down_ref[0, 2 * fields + 1] = (speed - high.astype(jnp.float32)).astype(jnp.bfloat16)


def pack(state, wind):
    fields, levels, rows, lons = state.shape
    halves = lons // LANES
    return pl.pallas_call(
        pack_kernel,
        grid=(halves, levels // KB),
        in_specs=[
            pl.BlockSpec((fields, KB, rows, LANES), lambda h, k: (0, k, 0, h)),
            pl.BlockSpec((KB, rows, LANES), lambda h, k: (k, 0, h)),
        ],
        out_specs=[
            pl.BlockSpec((1, 2 * fields, KB, LANES), lambda h, k: (h, 0, k, 0)),
            pl.BlockSpec((1, 2 * fields + 2, KB, LANES), lambda h, k: (h, 0, k, 0)),
        ],
        out_shape=[
            jax.ShapeDtypeStruct((halves, 2 * fields, levels, LANES), jnp.bfloat16),
            jax.ShapeDtypeStruct((halves, 2 * fields + 2, levels, LANES), jnp.bfloat16),
        ],
        name="pack",
    )(state, wind)


def inner_kernel(state_ref, wind_ref, out_ref):
    fields, levels, rows, lanes = state_ref.shape
    flat = state_ref.reshape(fields * levels * rows, lanes)
    winds = wind_ref.reshape(levels * rows, lanes)
    step = 8

    @pl.loop(0, levels // step)
    def _(i):
        base = i * (step * rows)
        faces = [face(row_of(winds, base + r, step, rows)) for r in range(2, rows - 1)]
        level = pl.multiple_of(i * step, step)
        for f in range(fields):
            q = [row_of(flat, f * levels * rows + base + r, step, rows) for r in range(rows)]
            for r, value in enumerate(rows_after(q, faces)):
                out_ref[0, r, f, pl.ds(level, step), :] = value


def inner(state, wind):
    fields, levels, rows, lons = state.shape
    halves = lons // LANES
    return pl.pallas_call(
        inner_kernel,
        grid=(halves, levels // KB),
        in_specs=[
            pl.BlockSpec((fields, KB, rows, LANES), lambda h, k: (0, k, 0, h)),
            pl.BlockSpec((KB, rows, LANES), lambda h, k: (k, 0, h)),
        ],
        out_specs=pl.BlockSpec((1, rows - 4, fields, KB, LANES), lambda h, k: (h, 0, 0, k, 0)),
        out_shape=jax.ShapeDtypeStruct((halves, rows - 4, fields, levels, LANES), jnp.float32),
        cost_estimate=pl.CostEstimate(flops=100_000_000, bytes_accessed=8_000_000, transcendentals=0),
        name="inner",
    )(state, wind)


def edge_kernel(state_ref, wind_ref, above_ref, below_ref, out_ref, up_ref, down_ref):
    fields, levels, rows, lanes = state_ref.shape
    flat = state_ref.reshape(fields * levels * rows, lanes)
    winds = wind_ref.reshape(levels * rows, lanes)
    step = 16

    @pl.loop(0, levels // step)
    def _(i):
        base = i * (step * rows)
        level = pl.multiple_of(i * step, step)
        here = pl.ds(level, step)
        wide = lambda ref, index: ref[0, index, here, :].astype(jnp.float32)
        speeds = {r: row_of(winds, base + r, step, rows) for r in (0, 1, 2, rows - 2, rows - 1)}
        speeds[rows] = wide(below_ref, 2 * fields) + wide(below_ref, 2 * fields + 1)
        for side, first in enumerate((0, rows - 2)):
            faces = [face(speeds[first + j]) for j in range(3)]
            for f in range(fields):
                own = lambda r: row_of(flat, f * levels * rows + base + r, step, rows)
                if side == 0:
                    q = [wide(above_ref, f), wide(above_ref, fields + f)] + [own(r) for r in range(4)]
                else:
                    q = [own(r) for r in range(rows - 4, rows)] + [wide(below_ref, f), wide(below_ref, fields + f)]
                sent = (down_ref, up_ref)[side]
                for r, value in enumerate(rows_after(q, faces)):
                    out_ref[0, 2 * side + r, f, here, :] = value
                    sent[0, r * fields + f, here, :] = value.astype(jnp.bfloat16)


def edge(state, wind, above, below):
    fields, levels, rows, lons = state.shape
    halves = lons // LANES
    sent = pl.BlockSpec((1, 2 * fields, KB, LANES), lambda h, k: (h, 0, k, 0))
    return pl.pallas_call(
        edge_kernel,
        grid=(halves, levels // KB),
        in_specs=[
            pl.BlockSpec((fields, KB, rows, LANES), lambda h, k: (0, k, 0, h)),
            pl.BlockSpec((KB, rows, LANES), lambda h, k: (k, 0, h)),
            sent,
            pl.BlockSpec((1, 2 * fields + 2, KB, LANES), lambda h, k: (h, 0, k, 0)),
        ],
        out_specs=[
            pl.BlockSpec((1, 4, fields, KB, LANES), lambda h, k: (h, 0, 0, k, 0)),
            sent,
            sent,
        ],
        out_shape=[
            jax.ShapeDtypeStruct((halves, 4, fields, levels, LANES), jnp.float32),
            jax.ShapeDtypeStruct((halves, 2 * fields, levels, LANES), jnp.bfloat16),
            jax.ShapeDtypeStruct((halves, 2 * fields, levels, LANES), jnp.bfloat16),
        ],
        cost_estimate=pl.CostEstimate(flops=100_000_000, bytes_accessed=10_000_000, transcendentals=0),
        name="edge",
    )(state, wind, above, below)


def weights_kernel(first_ref, bias_ref, second_ref, remap_ref, first_out, second_out, split_out):
    inputs, units = first_ref.shape
    levels = remap_ref.shape[0]
    whole = remap_ref[...]
    r_high = whole.astype(jnp.bfloat16)
    r_low = (whole - r_high.astype(jnp.float32)).astype(jnp.bfloat16)
    for j in range(2):
        split_out[:levels, j * levels : (j + 1) * levels] = r_high
        split_out[levels:, j * levels : (j + 1) * levels] = r_low
    wide = first_ref[...].astype(jnp.float32)
    for j in range(inputs // LANES):
        part = wide[j * LANES : (j + 1) * LANES]
        first_out[:, j * LANES : (j + 1) * LANES] = part.T.astype(jnp.bfloat16)
    bias = bias_ref[...]
    high = bias.astype(jnp.bfloat16).astype(jnp.float32)
    middle = (bias - high).astype(jnp.bfloat16).astype(jnp.float32)
    low = bias - high - middle
    row = lax.broadcasted_iota(jnp.int32, (LANES, units), 0)
    stacked = jnp.where(row == 0, high, jnp.where(row == 1, middle, jnp.where(row == 2, low, 0.0)))
    first_out[:, inputs:] = stacked.T.astype(jnp.bfloat16)
    second_out[...] = second_ref[...].astype(jnp.float32).T.astype(jnp.bfloat16)


def weights(w_first, bias, w_second, remap):
    inputs, hidden = w_first.shape
    levels = remap.shape[0]
    outputs = w_second.shape[1]
    return pl.pallas_call(
        weights_kernel,
        grid=(hidden // LANES,),
        in_specs=[
            pl.BlockSpec((inputs, LANES), lambda i: (0, i)),
            pl.BlockSpec((1, LANES), lambda i: (0, i)),
            pl.BlockSpec((LANES, outputs), lambda i: (i, 0)),
            pl.BlockSpec((levels, levels), lambda i: (0, 0)),
        ],
        out_specs=[
            pl.BlockSpec((LANES, inputs + LANES), lambda i: (i, 0)),
            pl.BlockSpec((outputs, LANES), lambda i: (0, i)),
            pl.BlockSpec((2 * levels, 2 * levels), lambda i: (0, 0)),
        ],
        out_shape=[
            jax.ShapeDtypeStruct((hidden, inputs + LANES), jnp.bfloat16),
            jax.ShapeDtypeStruct((outputs, hidden), jnp.bfloat16),
            jax.ShapeDtypeStruct((2 * levels, 2 * levels), jnp.bfloat16),
        ],
        cost_estimate=pl.CostEstimate(flops=100_000_000, bytes_accessed=7_000_000, transcendentals=0),
        name="weights",
    )(w_first, bias.reshape(1, hidden), w_second, remap)


def network(x, w1_ref, w2_ref):
    hidden = w1_ref.shape[0]
    chunk = 256
    total = None
    for c in range(hidden // chunk):
        v = jnp.dot(w1_ref[c * chunk : (c + 1) * chunk, :], x, preferred_element_type=jnp.float32)
        h = 0.5 * v
        t = jnp.tanh(v * (GELU_A + GELU_B * (v * v)))
        g = (h + h * t).astype(jnp.bfloat16)
        part = jnp.dot(w2_ref[:, c * chunk : (c + 1) * chunk], g, preferred_element_type=jnp.float32)
        total = part if total is None else total + part
    return total


def finish_kernel(edges, halves, *refs):
    if edges:
        (mid_hbm, edge_hbm, wind_hbm, scale_hbm, rcat_hbm, w1_hbm, w2_hbm, above_hbm, below_hbm, first_hbm, old_hbm,
         out_hbm, mid, edg, wnd, scale, rcat, w1, w2, a, x, rem, out, above, below, last, sems) = refs
    else:
        (mid_hbm, edge_hbm, wind_hbm, scale_hbm, rcat_hbm, w1_hbm, w2_hbm,
         out_hbm, mid, edg, wnd, scale, rcat, w1, w2, a, x, rem, out, sems) = refs
    count = len(halves)
    fields, levels, rows = out.shape[1:4]
    counter = iter(range(sems.shape[0]))

    def copy(source, target):
        made = pltpu.make_async_copy(source, target, sems.at[next(counter)])
        made.start()
        return made

    loads = []
    for s, h in enumerate(halves):
        lon = pl.ds(h * LANES, LANES)
        pending = [
            copy(mid_hbm.at[h], mid.at[s]),
            copy(edge_hbm.at[h], edg.at[s]),
            copy(wind_hbm.at[:, :, lon], wnd.at[s]),
        ]
        if edges:
            pending += [
                copy(above_hbm.at[h], above.at[s]),
                copy(below_hbm.at[h], below.at[s]),
                copy(first_hbm.at[h, pl.ds(2 * fields, 2)], last.at[s]),
            ]
        loads.append(pending)
        if s == 0:
            small = [copy(rcat_hbm, rcat), copy(scale_hbm, scale)]
            heavy = [copy(w1_hbm, w1), copy(w2_hbm, w2)]
    olds = []
    if edges:
        for s, h in enumerate(halves):
            olds.append(copy(old_hbm.at[:, :, :, pl.ds(h * LANES, LANES)], out.at[s]))

    inputs = fields * levels
    row = lax.broadcasted_iota(jnp.int32, (x.shape[1] - inputs, x.shape[2]), 0)
    for u in range(2):
        x[u, inputs:, :] = jnp.where(row < 3, 1.0, 0.0).astype(jnp.bfloat16)

    step = 16
    stores = []
    for s, h in enumerate(halves):
        for made in loads[s]:
            made.wait()
        winds = wnd.at[s].reshape(levels * rows, LANES)

        @pl.loop(0, levels // step)
        def _(i):
            here = pl.ds(pl.multiple_of(i * step, step), step)
            there = pl.ds(pl.multiple_of(levels + i * step, step), step)
            base = i * (step * rows)
            if edges:
                wide = lambda ref, index: ref[s, index, here, :].astype(jnp.float32)
                needed = (0, 1, 2, rows - 2, rows - 1)
                speeds = {r: row_of(winds, base + r, step, rows) for r in needed}
                speeds[rows] = wide(last, 0) + wide(last, 1)
                groups = ((0, 2), (rows - 2, 2))
            else:
                speeds = {r: row_of(winds, base + r, step, rows) for r in range(2, rows - 1)}
                groups = ((2, 4),)
            for first, many in groups:
                faces = [face(speeds[first + j]) for j in range(many + 1)]
                for f in range(fields):
                    kept = lambda r: (mid[s, r - 2, f, here, :] if 2 <= r < rows - 2 else
                                      edg[s, r if r < 2 else r - rows + 4, f, here, :])
                    q = []
                    for r in range(first - 2, first + many + 2):
                        if r < 0:
                            q.append(wide(above, (r + 2) * fields + f))
                        elif r >= rows:
                            q.append(wide(below, (r - rows) * fields + f))
                        else:
                            q.append(kept(r))
                    for j, value in enumerate(rows_after(q, faces)):
                        if edges:
                            u, place = (0 if first == 0 else 1), j
                        else:
                            u, place = j // 2, j % 2
                        cols = pl.ds(place * LANES, LANES)
                        high = value.astype(jnp.bfloat16)
                        a[u, f, here, cols] = high
                        a[u, f, there, cols] = (value - high.astype(jnp.float32)).astype(jnp.bfloat16)

        if s == 0:
            for made in small:
                made.wait()
        if edges:
            olds[s].wait()
        flat = out.at[s].reshape(fields * levels * rows, LANES)
        starts = (0, rows - 2) if edges else (2, 4)
        for u in range(2):
            for f in range(fields):
                both = jnp.dot(rcat[...], a[u, f], preferred_element_type=jnp.float32)
                value = both[:levels] + both[levels:]
                x[u, f * levels : (f + 1) * levels, :] = value.astype(jnp.bfloat16)
                if f == 0:
                    rem[u] = value
                else:
                    for place in range(2):
                        flat[pl.ds(f * levels * rows + starts[u] + place, levels, stride=rows), :] = (
                            value[:, place * LANES : (place + 1) * LANES])
        lon = pl.ds(h * LANES, LANES)
        stores.append(copy(out.at[s, pl.ds(1, fields - 1)], out_hbm.at[pl.ds(1, fields - 1), :, :, lon]))
        if s == 0:
            for made in heavy:
                made.wait()

        for u in range(2):
            net = network(x[u], w1, w2)
            for place in range(2):
                r = starts[u] + place
                part = slice(place * LANES, (place + 1) * LANES)
                light = scale[r : r + 1, h * LANES : (h + 1) * LANES]
                flat[pl.ds(r, levels, stride=rows), :] = rem[u, :, part] + net[:, part] * light
        stores.append(copy(out.at[s, 0], out_hbm.at[0, :, :, lon]))
    for made in stores:
        made.wait()


def finish(edges, halves, mid, edge_rows, wind, scale, rcat, w1, w2, *more):
    total_halves, inner_rows, fields, levels, _ = mid.shape
    rows = inner_rows + 4
    lons = total_halves * LANES
    n = len(halves)
    f32, b16 = jnp.float32, jnp.bfloat16
    scratch = [
        pltpu.VMEM((n,) + mid.shape[1:], f32),
        pltpu.VMEM((n,) + edge_rows.shape[1:], f32),
        pltpu.VMEM((n, levels, rows, LANES), f32),
        pltpu.VMEM(scale.shape, f32),
        pltpu.VMEM(rcat.shape, b16),
        pltpu.VMEM(w1.shape, b16),
        pltpu.VMEM(w2.shape, b16),
        pltpu.VMEM((2, fields, 2 * levels, 2 * LANES), b16),
        pltpu.VMEM((2, w1.shape[1], 2 * LANES), b16),
        pltpu.VMEM((2, levels, 2 * LANES), f32),
        pltpu.VMEM((n, fields, levels, rows, LANES), f32),
    ]
    semaphores = 4 + 5 * n
    if edges:
        scratch += [
            pltpu.VMEM((n, 2 * fields, levels, LANES), b16),
            pltpu.VMEM((n, 2 * fields, levels, LANES), b16),
            pltpu.VMEM((n, 2, levels, LANES), b16),
        ]
        semaphores += 4 * n
    scratch.append(pltpu.SemaphoreType.DMA((semaphores,)))
    operands = (mid, edge_rows, wind, scale, rcat, w1, w2) + more
    return pl.pallas_call(
        functools.partial(finish_kernel, edges, halves),
        in_specs=[ANY] * len(operands),
        out_specs=ANY,
        out_shape=jax.ShapeDtypeStruct((fields, levels, rows, lons), f32),
        scratch_shapes=scratch,
        input_output_aliases={len(operands) - 1: 0} if edges else {},
        compiler_params=pltpu.CompilerParams(vmem_limit_bytes=44 * 1024 * 1024),
        cost_estimate=pl.CostEstimate(flops=4_000_000_000, bytes_accessed=12_000_000, transcendentals=2_000_000),
        name="finish_edges" if edges else "finish_inner",
    )(*operands)


def shards(state, wind, sunlight, day_list, w_first, bias, w_second, remap):
    fields, levels, rows, lons = state.shape
    halves = lons // LANES
    count = lax.axis_size("lat")
    forward = [(i, i + 1) for i in range(count - 1)]
    back = [(i + 1, i) for i in range(count - 1)]
    up, down = pack(state, wind)
    above = lax.ppermute(up, "lat", forward)
    below = lax.ppermute(down, "lat", back)

    mid = inner(state, wind)
    w1, w2, rcat = weights(w_first, bias, w_second, remap)
    blocks = day_list.shape[1]
    lit = jnp.any(day_list[0][None, :] == jnp.arange(blocks, dtype=jnp.int32)[:, None], axis=1)
    lit = jnp.broadcast_to(lit.astype(jnp.float32).reshape(rows, halves, 1), (rows, halves, LANES))
    scale = sunlight * lit.reshape(rows, lons)

    edge_rows, up2, down2 = edge(state, wind, above, below)
    above2 = lax.ppermute(up2, "lat", forward)
    below2 = lax.ppermute(down2, "lat", back)
    every = tuple(range(halves))
    partial = finish(False, every, mid, edge_rows, wind, scale, rcat, w1, w2)
    return finish(True, every, mid, edge_rows, wind, scale, rcat, w1, w2, above2, below2, below, partial)


def solution(mesh):
    placed = (
        P("member", None, "lat", None),
        P("member", "lat", None),
        P(("member", "lat"), None),
        P(("member", "lat"), None),
        P(),
        P(),
        P(),
        P(),
    )
    return jax.shard_map(
        shards,
        mesh=mesh,
        in_specs=placed,
        out_specs=P("member", None, "lat", None),
        check_vma=False,
    )
```

time: 198 us -> 96.3 us (0.49)
  the two profiles are of different devices: /device:TPU:22 before, /device:TPU:1 now
where the time goes in v1:
time: 96.3 us; the launch traced here: 95.2 us
  Pallas kernels  57.6 us (60%)
  waiting for transfers between devices  15.2 us (16%)
  starting transfers between devices  12.6 us (13%)
  local copies, waits for them, and re-layouts  9.24 us (10%)
    pallas_call x2, Pallas kernels, finish(): pl.pallas_call(functools.partial(finish_kernel, edges, halves), in_specs=...  24.7 us
    ppermute x1, waiting for transfers between devices, shards(): above = lax.ppermute(up, 'lat', forward)  15.2 us
    pallas_call x1, Pallas kernels, weights(): pl.pallas_call(weights_kernel, grid=(hidden // LANES,), in_specs=[pl.Bloc...  10.9 us
    unnamed x24, local copies, waits for them, and re-layouts  9.07 us
    pallas_call x1, Pallas kernels, edge(): pl.pallas_call(edge_kernel, grid=(halves, levels // KB), in_specs=[pl.Blo...  8.17 us
    pallas_call x1, Pallas kernels, inner(): pl.pallas_call(inner_kernel, grid=(halves, levels // KB), in_specs=[pl.Bl...  7.39 us
    pallas_call x1, Pallas kernels, pack(): pl.pallas_call(pack_kernel, grid=(halves, levels // KB), in_specs=[pl.Blo...  6.43 us
    ppermute x1, starting transfers between devices, shards(): above = lax.ppermute(up, 'lat', forward)  4.52 us
  transfers between devices with their start and end apart: 4, of which 1 were waited for; matrix products, arithmetic and copies ran while one was open for 0% of the time, Pallas kernels for 31%

profile of v1, /device:TPU:1, one launch (start us, length us, event | category | flops | bytes accessed | tf_op | source)
XLA Modules:
  0.0 95.2 jit_solution(10956537636629295835)
XLA Ops:
  0.0 6.4 %pack.1 = (bf16[2,10,128,128]{3,2,1,0:T(8,128)(2,1)}, bf16[2,12,128,128]{3,2,1,0:T(8,128)(2,1)}) custom-call(f32[5,128,8,256]{3,2,1,0:T(8,128)} %state_ref.5, f32[128,8,256]{2,1,0:T(8,128)} %refs_2_.3), custom_call_target="tpu_custom_call" | custom-call | tf_op jit(solution)/shard_map/pack/pallas_call | solution.py:59
  6.4 1.9 %collective-permute-start.1 = (bf16[2,12,128,128]{3,2,1,0:T(8,128)(2,1)}, bf16[2,12,128,128]{3,2,1,0:T(8,128)(2,1)S(1)}, u32[]{:S(2)}, u32[]{:S(2)}) collective-permute-start(bf16[2,12,128,128]{3,2,1,0:T(8,128)(2,1)} %get-tuple-element.14), channel_id=1, source_target_pairs={{1,0},{2,1},{3,2},{4,3},{5,4},{6,5},{7,6},{8,7},{9,8},{10,9},{11,1... | collective-permute-start | bytes 2359304 | tf_op jit(solution)/shard_map/ppermute | solution.py:407
  8.3 0.0 copy-start.11
  8.4 4.5 %collective-permute-start = (bf16[2,10,128,128]{3,2,1,0:T(8,128)(2,1)}, bf16[2,10,128,128]{3,2,1,0:T(8,128)(2,1)S(1)}, u32[]{:S(2)}, u32[]{:S(2)}) collective-permute-start(bf16[2,10,128,128]{3,2,1,0:T(8,128)(2,1)} %get-tuple-element.13), channel_id=1, source_target_pairs={{0,1},{1,2},{2,3},{3,4},{4,5},{5,6},{6,7},{7,8},{8,9},{9,10},{10,1... | collective-permute-start | bytes 1966088 | tf_op jit(solution)/shard_map/ppermute | solution.py:406
  12.9 15.2 %collective-permute-done.above_ref = bf16[2,10,128,128]{3,2,1,0:T(8,128)(2,1)S(1)} collective-permute-done((bf16[2,10,128,128]{3,2,1,0:T(8,128)(2,1)}, bf16[2,10,128,128]{3,2,1,0:T(8,128)(2,1)S(1)}, u32[]{:S(2)}, u32[]{:S(2)}) %collective-permute-start) | collective-permute-done | bytes 655392 | tf_op jit(solution)/shard_map/ppermute | solution.py:406
  28.1 0.0 copy-start.9
  28.1 0.0 collective-permute-done.1.below_ref.refs_9_
  28.1 0.8 copy-done.9
  29.0 0.0 copy-start.5
  29.0 0.9 copy-done.5
  29.9 8.2 %edge.1 = (f32[2,4,5,128,128]{4,3,2,1,0:T(8,128)}, bf16[2,10,128,128]{3,2,1,0:T(8,128)(2,1)}, bf16[2,10,128,128]{3,2,1,0:T(8,128)(2,1)}) custom-call(f32[5,128,8,256]{3,2,1,0:T(8,128)} %state_ref.5, f32[128,8,256]{2,1,0:T(8,128)} %refs_2_.3, bf16[2,10,128,128]{3,2,1,0:T(8,128)(2,1)} %copy-done.9, bf16[2,12,128,128]{3,2,1,0:T(8,128)(2,1)} %copy-done.5), custom_call_target="tpu_custom_call" | custom-call | flops 100000000 | bytes 10000000 | tf_op jit(solution)/shard_map/edge/pallas_call | solution.py:144
  38.0 4.3 %collective-permute-start.2 = (bf16[2,10,128,128]{3,2,1,0:T(8,128)(2,1)}, bf16[2,10,128,128]{3,2,1,0:T(8,128)(2,1)S(1)}, u32[]{:S(2)}, u32[]{:S(2)}) collective-permute-start(bf16[2,10,128,128]{3,2,1,0:T(8,128)(2,1)} %get-tuple-element.19), channel_id=1, source_target_pairs={{0,1},{1,2},{2,3},{3,4},{4,5},{5,6},{6,7},{7,8},{8,9},{9,10},{10,1... | collective-permute-start | bytes 1966088 | tf_op jit(solution)/shard_map/ppermute | solution.py:417
  42.3 1.9 %collective-permute-start.3 = (bf16[2,10,128,128]{3,2,1,0:T(8,128)(2,1)}, bf16[2,10,128,128]{3,2,1,0:T(8,128)(2,1)S(1)}, u32[]{:S(2)}, u32[]{:S(2)}) collective-permute-start(bf16[2,10,128,128]{3,2,1,0:T(8,128)(2,1)} %get-tuple-element.20), channel_id=1, source_target_pairs={{1,0},{2,1},{3,2},{4,3},{5,4},{6,5},{7,6},{8,7},{9,8},{10,9},{11,1... | collective-permute-start | bytes 1966088 | tf_op jit(solution)/shard_map/ppermute | solution.py:418
  44.2 0.0 copy-done.11
  44.2 0.1 fusion
  44.4 0.1 reshape.16
  44.5 0.1 copy.12
  44.5 7.4 %inner.1.refs_0_ = f32[2,4,5,128,128]{4,3,2,1,0:T(8,128)} custom-call(f32[5,128,8,256]{3,2,1,0:T(8,128)} %state_ref.5, f32[128,8,256]{2,1,0:T(8,128)} %refs_2_.3), custom_call_target="tpu_custom_call" | custom-call | flops 100000000 | bytes 8000000 | tf_op jit(solution)/shard_map/inner/pallas_call | solution.py:98
  51.9 0.0 copy-start.10
  51.9 0.0 copy-start
  51.9 10.9 %weights.1 = (bf16[2048,768]{1,0:T(8,128)(2,1)}, bf16[128,2048]{1,0:T(8,128)(2,1)}, bf16[256,256]{1,0:T(8,128)(2,1)}) custom-call(bf16[640,2048]{1,0:T(8,128)(2,1)} %first_ref.1, f32[1,2048]{1,0:T(1,128)} %bitcast.4, bf16[2048,128]{1,0:T(8,128)(2,1)} %second_ref.1, f32[128,128]{1,0:T(8,128)} %remap_ref.1), custom_call_target="tpu_custom_call" | custom-call | flops 100000000 | bytes 7000000 | tf_op jit(solution)/shard_map/weights/pallas_call | solution.py:195
  62.9 0.0 copy-done.10
  62.9 0.1 bitcast_multiply_fusion.refs_3_
  63.0 0.0 copy-done
  63.0 0.0 copy-start.1
  63.0 1.7 %copy-done.1 = f32[2,4,5,128,128]{4,3,2,1,0:T(8,128)S(1)} copy-done((f32[2,4,5,128,128]{4,3,2,1,0:T(8,128)S(1)}, f32[2,4,5,128,128]{4,3,2,1,0:T(8,128)}, u32[]{:S(2)}) %copy-start.1) | copy-done | bytes 2621464
  64.7 0.0 copy-start.2
  64.7 1.9 %copy-done.2 = bf16[2048,768]{1,0:T(8,128)(2,1)S(1)} copy-done((bf16[2048,768]{1,0:T(8,128)(2,1)S(1)}, bf16[2048,768]{1,0:T(8,128)(2,1)}, u32[]{:S(2)}) %copy-start.2) | copy-done | bytes 3145752
  66.6 0.0 copy-start.3
  66.6 1.7 %copy-done.3 = f32[2,4,5,128,128]{4,3,2,1,0:T(8,128)S(1)} copy-done((f32[2,4,5,128,128]{4,3,2,1,0:T(8,128)S(1)}, f32[2,4,5,128,128]{4,3,2,1,0:T(8,128)}, u32[]{:S(2)}) %copy-start.3) | copy-done | bytes 2621464
  68.3 0.0 copy-start.7
  68.3 1.0 %copy-done.7 = bf16[128,2048]{1,0:T(8,128)(2,1)S(1)} copy-done((bf16[128,2048]{1,0:T(8,128)(2,1)S(1)}, bf16[128,2048]{1,0:T(8,128)(2,1)}, u32[]{:S(2)}) %copy-start.7) | copy-done | bytes 524312
  69.4 0.0 copy-start.8
  69.4 0.9 copy-done.8
  70.3 0.0 copy-start.4
  70.3 0.0 copy-start.6
  70.3 11.3 %finish_inner.1.refs_10_ = f32[5,128,8,256]{3,2,1,0:T(8,128)} custom-call(f32[2,4,5,128,128]{4,3,2,1,0:T(8,128)S(1)} %copy-done.1, f32[2,4,5,128,128]{4,3,2,1,0:T(8,128)S(1)} %copy-done.3, f32[128,8,256]{2,1,0:T(8,128)S(1)} %copy-done, f32[8,256]{1,0:T(8,128)S(1)} %bitcast_multiply_fusion.refs_3_, bf16[256,256]{1,0:T(8,128)(2,1)S(1)} %copy-done.8, ...), custom_call_target="tpu_custom_call" | custom-call | flops 4000000000 | bytes 12000000 | tf_op jit(solution)/shard_map/finish_inner/pallas_call | solution.py:386
  81.6 0.0 collective-permute-done.2.refs_7_
  81.6 0.0 collective-permute-done.3.refs_8_
  81.6 0.0 copy-done.4
  81.7 0.0 copy-done.6
  81.7 13.4 %finish_edges.1 = f32[5,128,8,256]{3,2,1,0:T(8,128)} custom-call(f32[2,4,5,128,128]{4,3,2,1,0:T(8,128)S(1)} %copy-done.1, f32[2,4,5,128,128]{4,3,2,1,0:T(8,128)S(1)} %copy-done.4, f32[128,8,256]{2,1,0:T(8,128)S(1)} %copy-done, f32[8,256]{1,0:T(8,128)S(1)} %bitcast_multiply_fusion.refs_3_, ...), custom_call_target="tpu_custom_call", output_to_operand_aliasing={{}: (10, {})} | custom-call | flops 4000000000 | bytes 12000000 | tf_op jit(solution)/shard_map/finish_edges/pallas_call | solution.py:386
  (1 shorter events, 0.0 us)
Async XLA Ops:
  6.4 21.7 %collective-permute-start.1 = (bf16[2,12,128,128]{3,2,1,0:T(8,128)(2,1)}, bf16[2,12,128,128]{3,2,1,0:T(8,128)(2,1)S(1)}, u32[]{:S(2)}, u32[]{:S(2)}) collective-permute-start(bf16[2,12,128,128]{3,2,1,0:T(8,128)(2,1)} %get-tuple-element.14), channel_id=1, source_target_pairs={{1,0},{2,1},{3,2},{4,3},{5,4},{6,5},{7,6},{8,7},{9,8},{10,9},{11,1... | collective-permute-start | bytes 2359304 | tf_op jit(solution)/shard_map/ppermute | solution.py:407
  8.3 35.9 %copy-start.11 = (s32[1,16]{1,0:T(1,128)S(1)}, s32[1,16]{1,0:T(1,128)}, u32[]{:S(2)}) copy-start(s32[1,16]{1,0:T(1,128)} %param.11) | copy-start | bytes 196
  8.4 19.8 %collective-permute-start = (bf16[2,10,128,128]{3,2,1,0:T(8,128)(2,1)}, bf16[2,10,128,128]{3,2,1,0:T(8,128)(2,1)S(1)}, u32[]{:S(2)}, u32[]{:S(2)}) collective-permute-start(bf16[2,10,128,128]{3,2,1,0:T(8,128)(2,1)} %get-tuple-element.13), channel_id=1, source_target_pairs={{0,1},{1,2},{2,3},{3,4},{4,5},{5,6},{6,7},{7,8},{8,9},{9,10},{10,1... | collective-permute-start | bytes 1966088 | tf_op jit(solution)/shard_map/ppermute | solution.py:406
  28.1 0.8 copy-start.9
  29.0 0.9 copy-start.5
  38.0 43.6 %collective-permute-start.2 = (bf16[2,10,128,128]{3,2,1,0:T(8,128)(2,1)}, bf16[2,10,128,128]{3,2,1,0:T(8,128)(2,1)S(1)}, u32[]{:S(2)}, u32[]{:S(2)}) collective-permute-start(bf16[2,10,128,128]{3,2,1,0:T(8,128)(2,1)} %get-tuple-element.19), channel_id=1, source_target_pairs={{0,1},{1,2},{2,3},{3,4},{4,5},{5,6},{6,7},{7,8},{8,9},{9,10},{10,1... | collective-permute-start | bytes 1966088 | tf_op jit(solution)/shard_map/ppermute | solution.py:417
  42.3 39.3 %collective-permute-start.3 = (bf16[2,10,128,128]{3,2,1,0:T(8,128)(2,1)}, bf16[2,10,128,128]{3,2,1,0:T(8,128)(2,1)S(1)}, u32[]{:S(2)}, u32[]{:S(2)}) collective-permute-start(bf16[2,10,128,128]{3,2,1,0:T(8,128)(2,1)} %get-tuple-element.20), channel_id=1, source_target_pairs={{1,0},{2,1},{3,2},{4,3},{5,4},{6,5},{7,6},{8,7},{9,8},{10,9},{11,1... | collective-permute-start | bytes 1966088 | tf_op jit(solution)/shard_map/ppermute | solution.py:418
  51.9 11.0 %copy-start.10 = (f32[8,256]{1,0:T(8,128)S(1)}, f32[8,256]{1,0:T(8,128)}, u32[]{:S(2)}) copy-start(f32[8,256]{1,0:T(8,128)} %param.10) | copy-start | bytes 24580
  51.9 11.0 %copy-start = (f32[128,8,256]{2,1,0:T(8,128)S(1)}, f32[128,8,256]{2,1,0:T(8,128)}, u32[]{:S(2)}) copy-start(f32[128,8,256]{2,1,0:T(8,128)} %refs_2_.3) | copy-start | bytes 3145732
  63.0 1.7 %copy-start.1 = (f32[2,4,5,128,128]{4,3,2,1,0:T(8,128)S(1)}, f32[2,4,5,128,128]{4,3,2,1,0:T(8,128)}, u32[]{:S(2)}) copy-start(f32[2,4,5,128,128]{4,3,2,1,0:T(8,128)} %inner.1.refs_0_) | copy-start | bytes 7864324
  64.7 1.9 %copy-start.2 = (bf16[2048,768]{1,0:T(8,128)(2,1)S(1)}, bf16[2048,768]{1,0:T(8,128)(2,1)}, u32[]{:S(2)}) copy-start(bf16[2048,768]{1,0:T(8,128)(2,1)} %get-tuple-element.17.refs_5_) | copy-start | bytes 9437188
  66.6 1.7 %copy-start.3 = (f32[2,4,5,128,128]{4,3,2,1,0:T(8,128)S(1)}, f32[2,4,5,128,128]{4,3,2,1,0:T(8,128)}, u32[]{:S(2)}) copy-start(f32[2,4,5,128,128]{4,3,2,1,0:T(8,128)} %get-tuple-element.15.refs_1_) | copy-start | bytes 7864324
  68.3 1.0 %copy-start.7 = (bf16[128,2048]{1,0:T(8,128)(2,1)S(1)}, bf16[128,2048]{1,0:T(8,128)(2,1)}, u32[]{:S(2)}) copy-start(bf16[128,2048]{1,0:T(8,128)(2,1)} %get-tuple-element.18.refs_6_) | copy-start | bytes 1572868
  69.4 0.9 copy-start.8
  70.3 11.4 %copy-start.4 = (f32[2,4,5,128,128]{4,3,2,1,0:T(8,128)S(1)}, f32[2,4,5,128,128]{4,3,2,1,0:T(8,128)}, u32[]{:S(2)}) copy-start(f32[2,4,5,128,128]{4,3,2,1,0:T(8,128)} %get-tuple-element.15.refs_1_) | copy-start | bytes 7864324
  70.3 11.4 %copy-start.6 = (bf16[2,12,128,128]{3,2,1,0:T(8,128)(2,1)S(1)}, bf16[2,12,128,128]{3,2,1,0:T(8,128)(2,1)}, u32[]{:S(2)}) copy-start(bf16[2,12,128,128]{3,2,1,0:T(8,128)(2,1)} %copy-done.5) | copy-start | bytes 2359300

commit v2 on v0

v2 whole, which is shorter than its diff:
```python
import functools
import jax
import jax.numpy as jnp
from jax import lax
from jax.experimental import pallas as pl
from jax.experimental.pallas import tpu as pltpu
from jax.sharding import PartitionSpec as P

LANES = 128
GELU_A = 0.7978845608028654
GELU_B = 0.7978845608028654 * 0.044715
HBM = pl.BlockSpec(memory_space=pltpu.HBM)
VMEM = pl.BlockSpec(memory_space=pltpu.VMEM)
MIB = 1024 * 1024


def call(kernel, name, outs, operands, hbm_in=0, hbm_out=0, scratch=(), limit=8, flops=0, moved=0):
    return pl.pallas_call(
        kernel,
        in_specs=[HBM] * hbm_in + [VMEM] * (len(operands) - hbm_in),
        out_specs=[HBM] * hbm_out + [VMEM] * (len(outs) - hbm_out),
        out_shape=outs,
        scratch_shapes=scratch,
        compiler_params=pltpu.CompilerParams(vmem_limit_bytes=limit * MIB),
        cost_estimate=pl.CostEstimate(flops=flops, bytes_accessed=moved, transcendentals=0),
        name=name,
    )(*operands)


def array(shape, dtype=jnp.float32):
    return jax.ShapeDtypeStruct(shape, dtype)


def limited(ahead, behind):
    return jnp.maximum(jnp.minimum(ahead, jnp.maximum(behind, 0.0)), jnp.minimum(behind, 0.0))


def face(speed):
    size = jnp.abs(speed)
    return speed > 0.0, speed, size * (0.5 - 0.5 * size)


def rows_after(q, faces):
    diffs = [b - a for a, b in zip(q[:-1], q[1:])]
    slopes = [None] + [limited(b, a) for a, b in zip(diffs[:-1], diffs[1:])]
    fluxes = []
    for j, (mask, speed, half) in enumerate(faces):
        edge = jnp.where(mask, q[j + 1], q[j + 2])
        slope = jnp.where(mask, slopes[j + 1], slopes[j + 2])
        fluxes.append(speed * edge + half * slope)
    return [q[j + 2] - (fluxes[j + 1] - fluxes[j]) for j in range(len(faces) - 1)]


def row_of(ref, start, count, rows):
    return ref[pl.ds(start, count, stride=rows), :]


def pack_kernel(parts, state_hbm, wind_hbm, kept_ref, winds_ref, up_ref, down_ref, sems):
    halves, fields, levels, rows, lanes = kept_ref.shape
    size = levels // parts
    wind_copies, copies = [], []
    for h in range(halves):
        lon = pl.ds(h * lanes, lanes)
        made = pltpu.make_async_copy(wind_hbm.at[:, :, lon], winds_ref.at[h], sems.at[h])
        wind_copies.append(made)
        for p in range(parts):
            some = pl.ds(p * size, size)
            made = pltpu.make_async_copy(
                state_hbm.at[:, some, :, lon], kept_ref.at[h, :, some], sems.at[halves + h * parts + p])
            made.start()
            copies.append((h, p, made))
        wind_copies[h].start()
    for h, p, made in copies:
        made.wait()
        here = slice(p * size, (p + 1) * size)
        flat = kept_ref.at[h].reshape(fields * levels * rows, lanes)
        for f in range(fields):
            base = (f * levels + p * size) * rows
            for r in range(2):
                first = row_of(flat, base + r, size, rows)
                down_ref[h, r * fields + f, here] = first.astype(jnp.bfloat16)
                last = row_of(flat, base + rows - 2 + r, size, rows)
                up_ref[h, r * fields + f, here] = last.astype(jnp.bfloat16)
    for h in range(halves):
        wind_copies[h].wait()
        speed = row_of(winds_ref.at[h].reshape(levels * rows, lanes), 0, levels, rows)
        high = speed.astype(jnp.bfloat16)
        down_ref[h, 2 * fields] = high
        down_ref[h, 2 * fields + 1] = (speed - high.astype(jnp.float32)).astype(jnp.bfloat16)


def pack(state, wind):
    fields, levels, rows, lons = state.shape
    halves = lons // LANES
    parts = 4
    return call(
        functools.partial(pack_kernel, parts), "pack",
        [
            array((halves, fields, levels, rows, LANES)),
            array((halves, levels, rows, LANES)),
            array((halves, 2 * fields, levels, LANES), jnp.bfloat16),
            array((halves, 2 * fields + 2, levels, LANES), jnp.bfloat16),
        ],
        (state, wind), hbm_in=2, scratch=[pltpu.SemaphoreType.DMA((halves * (parts + 1),))], moved=9_000_000)


def inner_kernel(kept_ref, winds_ref, out_ref):
    halves, fields, levels, rows, lanes = kept_ref.shape
    step = 8
    for h in range(halves):
        flat = kept_ref.at[h].reshape(fields * levels * rows, lanes)
        winds = winds_ref.at[h].reshape(levels * rows, lanes)

        @pl.loop(0, levels // step)
        def _(i):
            base = i * (step * rows)
            faces = [face(row_of(winds, base + r, step, rows)) for r in range(2, rows - 1)]
            level = pl.multiple_of(i * step, step)
            for f in range(fields):
                q = [row_of(flat, f * levels * rows + base + r, step, rows) for r in range(rows)]
                for r, value in enumerate(rows_after(q, faces)):
                    out_ref[h, r, f, pl.ds(level, step), :] = value


def inner(kept, winds):
    halves, fields, levels, rows, lanes = kept.shape
    return call(
        inner_kernel, "inner", [array((halves, rows - 4, fields, levels, lanes))], (kept, winds),
        flops=100_000_000, moved=8_000_000)[0]


def edge_kernel(kept_ref, winds_ref, above_ref, below_ref, out_ref, up_ref, down_ref):
    halves, fields, levels, rows, lanes = kept_ref.shape
    step = 16
    for h in range(halves):
        flat = kept_ref.at[h].reshape(fields * levels * rows, lanes)
        winds = winds_ref.at[h].reshape(levels * rows, lanes)

        @pl.loop(0, levels // step)
        def _(i):
            base = i * (step * rows)
            here = pl.ds(pl.multiple_of(i * step, step), step)
            wide = lambda ref, index: ref[h, index, here, :].astype(jnp.float32)
            speeds = {r: row_of(winds, base + r, step, rows) for r in (0, 1, 2, rows - 2, rows - 1)}
            speeds[rows] = wide(below_ref, 2 * fields) + wide(below_ref, 2 * fields + 1)
            for side, first in enumerate((0, rows - 2)):
                faces = [face(speeds[first + j]) for j in range(3)]
                for f in range(fields):
                    own = lambda r: row_of(flat, f * levels * rows + base + r, step, rows)
                    if side == 0:
                        q = [wide(above_ref, f), wide(above_ref, fields + f)] + [own(r) for r in range(4)]
                    else:
                        q = [own(r) for r in range(rows - 4, rows)] + [wide(below_ref, f), wide(below_ref, fields + f)]
                    sent = (down_ref, up_ref)[side]
                    for r, value in enumerate(rows_after(q, faces)):
                        out_ref[h, 2 * side + r, f, here, :] = value
                        sent[h, r * fields + f, here, :] = value.astype(jnp.bfloat16)


def edge(kept, winds, above, below):
    halves, fields, levels, rows, lanes = kept.shape
    sent = array((halves, 2 * fields, levels, lanes), jnp.bfloat16)
    return call(
        edge_kernel, "edge", [array((halves, 4, fields, levels, lanes)), sent, sent],
        (kept, winds, above, below), flops=100_000_000, moved=10_000_000)


def weights_kernel(first_ref, bias_ref, second_ref, remap_ref, first_out, second_out, split_out):
    inputs, hidden = first_ref.shape
    levels = remap_ref.shape[0]
    whole = remap_ref[...]
    r_high = whole.astype(jnp.bfloat16)
    r_low = (whole - r_high.astype(jnp.float32)).astype(jnp.bfloat16)
    for j in range(2):
        split_out[:levels, j * levels : (j + 1) * levels] = r_high
        split_out[levels:, j * levels : (j + 1) * levels] = r_low
    chunk = 256
    same = lambda d: lax.broadcasted_iota(jnp.int32, (chunk, chunk), d)
    unit = jnp.where(same(0) == same(1), 1.0, 0.0).astype(jnp.bfloat16)
    flip = lambda part: lax.dot_general(
        unit, part, (((1,), (1,)), ((), ())), preferred_element_type=jnp.float32).astype(jnp.bfloat16)
    small = unit[:LANES, :LANES]
    row = lax.broadcasted_iota(jnp.int32, (LANES, chunk), 0)
    for j in range(hidden // chunk):
        here = slice(j * chunk, (j + 1) * chunk)
        first_out[here, :inputs] = flip(first_ref[:, here])
        bias = bias_ref[:, here]
        high = bias.astype(jnp.bfloat16).astype(jnp.float32)
        middle = (bias - high).astype(jnp.bfloat16).astype(jnp.float32)
        low = bias - high - middle
        stacked = jnp.where(row == 0, high, jnp.where(row == 1, middle, jnp.where(row == 2, low, 0.0)))
        first_out[here, inputs:] = flip(stacked.astype(jnp.bfloat16))
        second_out[:, here] = lax.dot_general(
            small, second_ref[here, :], (((1,), (1,)), ((), ())),
            preferred_element_type=jnp.float32).astype(jnp.bfloat16)


def weights(w_first, bias, w_second, remap):
    inputs, hidden = w_first.shape
    levels = remap.shape[0]
    outputs = w_second.shape[1]
    return call(
        weights_kernel, "weights",
        [
            array((hidden, inputs + LANES), jnp.bfloat16),
            array((outputs, hidden), jnp.bfloat16),
            array((2 * levels, 2 * levels), jnp.bfloat16),
        ],
        (w_first, bias.reshape(1, hidden), w_second, remap), flops=100_000_000, moved=7_000_000)


def network(x, w1_ref, w2_ref):
    hidden = w1_ref.shape[0]
    chunk = 256
    total = None
    for c in range(hidden // chunk):
        v = jnp.dot(w1_ref[c * chunk : (c + 1) * chunk, :], x, preferred_element_type=jnp.float32)
        h = 0.5 * v
        t = jnp.tanh(v * (GELU_A + GELU_B * (v * v)))
        g = (h + h * t).astype(jnp.bfloat16)
        part = jnp.dot(w2_ref[:, c * chunk : (c + 1) * chunk], g, preferred_element_type=jnp.float32)
        total = part if total is None else total + part
    return total


def finish_kernel(edges, *refs):
    if edges:
        (mid, edg, wnd, scale, rcat, w1, w2, above, below, last, done, out_hbm, a, x, rem, out, sems) = refs
    else:
        (mid, edg, wnd, scale, rcat, w1, w2, out, a, x, rem) = refs
    halves, _, fields, levels, lanes = mid.shape
    rows = wnd.shape[2]
    inputs = fields * levels
    row = lax.broadcasted_iota(jnp.int32, (x.shape[1] - inputs, x.shape[2]), 0)
    for u in range(2):
        x[u, inputs:, :] = jnp.where(row < 3, 1.0, 0.0).astype(jnp.bfloat16)

    step = 16
    stores = []
    for h in range(halves):
        winds = wnd.at[h].reshape(levels * rows, lanes)

        @pl.loop(0, levels // step)
        def _(i):
            here = pl.ds(pl.multiple_of(i * step, step), step)
            there = pl.ds(pl.multiple_of(levels + i * step, step), step)
            base = i * (step * rows)
            wide = lambda ref, index: ref[h, index, here, :].astype(jnp.float32)
            if edges:
                needed = (0, 1, 2, rows - 2, rows - 1)
                speeds = {r: row_of(winds, base + r, step, rows) for r in needed}
                speeds[rows] = wide(last, 2 * fields) + wide(last, 2 * fields + 1)
                groups = ((0, 2), (rows - 2, 2))
            else:
                speeds = {r: row_of(winds, base + r, step, rows) for r in range(2, rows - 1)}
                groups = ((2, 4),)
            for first, many in groups:
                faces = [face(speeds[first + j]) for j in range(many + 1)]
                for f in range(fields):
                    kept = lambda r: (mid[h, r - 2, f, here, :] if 2 <= r < rows - 2 else
                                      edg[h, r if r < 2 else r - rows + 4, f, here, :])
                    q = []
                    for r in range(first - 2, first + many + 2):
                        if r < 0:
                            q.append(wide(above, (r + 2) * fields + f))
                        elif r >= rows:
                            q.append(wide(below, (r - rows) * fields + f))
                        else:
                            q.append(kept(r))
                    for j, value in enumerate(rows_after(q, faces)):
                        if edges:
                            u, place = (0 if first == 0 else 1), j
                        else:
                            u, place = j // 2, j % 2
                        cols = pl.ds(place * lanes, lanes)
                        high = value.astype(jnp.bfloat16)
                        a[u, f, here, cols] = high
                        a[u, f, there, cols] = (value - high.astype(jnp.float32)).astype(jnp.bfloat16)

        starts = (0, rows - 2) if edges else (2, 4)
        if edges:
            flat = out.at[h].reshape(fields * levels * rows, lanes)

        def put(f, u, place, value):
            if edges:
                flat[pl.ds(f * levels * rows + starts[u] + place, levels, stride=rows), :] = value
            else:
                out[h, 2 * u + place, f] = value

        if edges:
            for f in range(fields):
                for r in range(2, rows - 2):
                    flat[pl.ds(f * levels * rows + r, levels, stride=rows), :] = done[h, r - 2, f]
        for u in range(2):
            for f in range(fields):
                both = jnp.dot(rcat[...], a[u, f], preferred_element_type=jnp.float32)
                value = both[:levels] + both[levels:]
                x[u, f * levels : (f + 1) * levels, :] = value.astype(jnp.bfloat16)
                if f == 0:
                    rem[u] = value
                else:
                    for place in range(2):
                        put(f, u, place, value[:, place * lanes : (place + 1) * lanes])
        if edges:
            lon = pl.ds(h * lanes, lanes)
            made = pltpu.make_async_copy(
                out.at[h, pl.ds(1, fields - 1)], out_hbm.at[pl.ds(1, fields - 1), :, :, lon], sems.at[2 * h])
            made.start()
            stores.append(made)
        for u in range(2):
            net = network(x[u], w1, w2)
            for place in range(2):
                r = starts[u] + place
                part = slice(place * lanes, (place + 1) * lanes)
                light = scale[r : r + 1, h * lanes : (h + 1) * lanes]
                put(0, u, place, rem[u, :, part] + net[:, part] * light)
        if edges:
            made = pltpu.make_async_copy(out.at[h, 0], out_hbm.at[0, :, :, lon], sems.at[2 * h + 1])
            made.start()
            stores.append(made)
    for made in stores:
        made.wait()


def finish(edges, mid, edge_rows, wind, scale, rcat, w1, w2, *more):
    halves, inner_rows, fields, levels, lanes = mid.shape
    rows = inner_rows + 4
    scratch = [
        pltpu.VMEM((2, fields, 2 * levels, 2 * lanes), jnp.bfloat16),
        pltpu.VMEM((2, w1.shape[1], 2 * lanes), jnp.bfloat16),
        pltpu.VMEM((2, levels, 2 * lanes), jnp.float32),
    ]
    if edges:
        scratch += [
            pltpu.VMEM((halves, fields, levels, rows, lanes), jnp.float32),
            pltpu.SemaphoreType.DMA((2 * halves,)),
        ]
        outs = [array((fields, levels, rows, halves * lanes))]
    else:
        outs = [array(mid.shape)]
    return call(
        functools.partial(finish_kernel, edges), "finish_edges" if edges else "finish_inner", outs,
        (mid, edge_rows, wind, scale, rcat, w1, w2) + more, hbm_out=1 if edges else 0, scratch=scratch,
        limit=16, flops=4_000_000_000, moved=12_000_000)[0]


def shards(state, wind, sunlight, day_list, w_first, bias, w_second, remap):
    fields, levels, rows, lons = state.shape
    halves = lons // LANES
    count = lax.axis_size("lat")
    forward = [(i, i + 1) for i in range(count - 1)]
    back = [(i + 1, i) for i in range(count - 1)]
    kept, winds, up, down = pack(state, wind)
    above = lax.ppermute(up, "lat", forward)
    below = lax.ppermute(down, "lat", back)

    mid = inner(kept, winds)
    w1, w2, rcat = weights(w_first, bias, w_second, remap)
    blocks = day_list.shape[1]
    lit = jnp.any(day_list[0][None, :] == jnp.arange(blocks, dtype=jnp.int32)[:, None], axis=1)
    lit = jnp.broadcast_to(lit.astype(jnp.float32).reshape(rows, halves, 1), (rows, halves, LANES))
    scale = sunlight * lit.reshape(rows, lons)

    kept, mid, w1, w2, rcat, scale = lax.optimization_barrier((kept, mid, w1, w2, rcat, scale))
    edge_rows, up2, down2 = edge(kept, winds, above, below)
    above2 = lax.ppermute(up2, "lat", forward)
    below2 = lax.ppermute(down2, "lat", back)
    partial = finish(False, mid, edge_rows, winds, scale, rcat, w1, w2)
    return finish(True, mid, edge_rows, winds, scale, rcat, w1, w2, above2, below2, below, partial)


def solution(mesh):
    placed = (
        P("member", None, "lat", None),
        P("member", "lat", None),
        P(("member", "lat"), None),
        P(("member", "lat"), None),
        P(),
        P(),
        P(),
        P(),
    )
    return jax.shard_map(
        shards,
        mesh=mesh,
        in_specs=placed,
        out_specs=P("member", None, "lat", None),
        check_vma=False,
    )
```

time: 198 us -> 62.7 us (0.32)
  the two profiles are of different devices: /device:TPU:22 before, /device:TPU:1 now
where the time goes in v2:
time: 62.7 us; the launch traced here: 62.4 us
  Pallas kernels  29 us (46%)
  starting transfers between devices  12.8 us (20%)
  waiting for transfers between devices  11.3 us (18%)
  local copies, waits for them, and re-layouts  8.75 us (14%)
    pallas_call x6, Pallas kernels, call(): pl.pallas_call(kernel, in_specs=[HBM] * hbm_in + [VMEM] * (len(operands)...  29 us
    unnamed x22, local copies, waits for them, and re-layouts  8.59 us
    ppermute x1, waiting for transfers between devices, shards(): above = lax.ppermute(up, 'lat', forward)  8.52 us
    ppermute x1, starting transfers between devices, shards(): above = lax.ppermute(up, 'lat', forward)  4.52 us
    ppermute x1, starting transfers between devices, shards(): above2 = lax.ppermute(up2, 'lat', forward)  4.28 us
    ppermute x1, waiting for transfers between devices, shards(): above2 = lax.ppermute(up2, 'lat', forward)  2.83 us
    ppermute x1, starting transfers between devices, shards(): below2 = lax.ppermute(down2, 'lat', back)  2.1 us
    ppermute x1, starting transfers between devices, shards(): below = lax.ppermute(down, 'lat', back)  1.91 us
  transfers between devices with their start and end apart: 4, of which 2 were waited for; matrix products, arithmetic and copies ran while one was open for 1% of the time, Pallas kernels for 21%

profile of v2, /device:TPU:1, one launch (start us, length us, event | category | flops | bytes accessed | tf_op | source)
XLA Modules:
  0.0 62.4 jit_solution(6636183176755983482)
XLA Ops:
  0.0 0.0 copy-start.3
  0.0 2.5 %copy-done.3 = f32[5,128,8,256]{3,2,1,0:T(8,128)S(1)} copy-done((f32[5,128,8,256]{3,2,1,0:T(8,128)S(1)}, f32[5,128,8,256]{3,2,1,0:T(8,128)}, u32[]{:S(2)}) %copy-start.3) | copy-done | bytes 5242904
  2.5 0.0 copy-start.5
  2.5 1.2 %copy-done.5 = f32[128,8,256]{2,1,0:T(8,128)S(1)} copy-done((f32[128,8,256]{2,1,0:T(8,128)S(1)}, f32[128,8,256]{2,1,0:T(8,128)}, u32[]{:S(2)}) %copy-start.5) | copy-done | bytes 1048600
  3.7 0.0 copy-start.10
  3.7 1.8 %pack.1 = (f32[2,5,128,8,128]{4,3,2,1,0:T(8,128)S(1)}, f32[2,128,8,128]{3,2,1,0:T(8,128)S(1)}, bf16[2,10,128,128]{3,2,1,0:T(8,128)(2,1)}, bf16[2,12,128,128]{3,2,1,0:T(8,128)(2,1)S(1)}) custom-call(f32[5,128,8,256]{3,2,1,0:T(8,128)S(1)} %copy-done.3, f32[128,8,256]{2,1,0:T(8,128)S(1)} %copy-done.5), custom_call_target="tpu_custom_call" | custom-call | bytes 9000000 | tf_op jit(solution)/shard_map/pack/pallas_call | solution.py:18
  5.6 0.0 copy-start
  5.6 2.3 %copy-done = f32[2,5,128,8,128]{4,3,2,1,0:T(8,128)} copy-done((f32[2,5,128,8,128]{4,3,2,1,0:T(8,128)}, f32[2,5,128,8,128]{4,3,2,1,0:T(8,128)S(1)}, u32[]{:S(2)}) %copy-start) | copy-done | bytes 5242904
  7.9 1.9 %collective-permute-start.1 = (bf16[2,12,128,128]{3,2,1,0:T(8,128)(2,1)S(1)}, bf16[2,12,128,128]{3,2,1,0:T(8,128)(2,1)S(1)}, u32[]{:S(2)}, u32[]{:S(2)}) collective-permute-start(bf16[2,12,128,128]{3,2,1,0:T(8,128)(2,1)S(1)} %get-tuple-element.29), channel_id=1, source_target_pairs={{1,0},{2,1},{3,2},{4,3},{5,4},{6,5},{7,6},{8,7},{9,8},{10,9},{11,1... | collective-permute-start | bytes 2359304 | tf_op jit(solution)/shard_map/ppermute | solution.py:355
  9.8 4.5 %collective-permute-start = (bf16[2,10,128,128]{3,2,1,0:T(8,128)(2,1)}, bf16[2,10,128,128]{3,2,1,0:T(8,128)(2,1)S(1)}, u32[]{:S(2)}, u32[]{:S(2)}) collective-permute-start(bf16[2,10,128,128]{3,2,1,0:T(8,128)(2,1)} %get-tuple-element.28), channel_id=1, source_target_pairs={{0,1},{1,2},{2,3},{3,4},{4,5},{5,6},{6,7},{7,8},{8,9},{9,10},{10,1... | collective-permute-start | bytes 1966088 | tf_op jit(solution)/shard_map/ppermute | solution.py:354
  14.4 0.0 copy-done.10
  14.4 0.1 fusion
  14.5 0.1 reshape.16
  14.6 0.1 copy.11
  14.7 0.0 copy-start.1
  14.7 2.5 %copy-done.1 = f32[2,5,128,8,128]{4,3,2,1,0:T(8,128)S(1)} copy-done((f32[2,5,128,8,128]{4,3,2,1,0:T(8,128)S(1)}, f32[2,5,128,8,128]{4,3,2,1,0:T(8,128)}, u32[]{:S(2)}) %copy-start.1) | copy-done | bytes 5242904
  17.2 0.0 copy-start.4
  17.2 0.0 copy-start.6
  17.2 0.0 copy-start.7
  17.2 0.0 copy-start.8
  17.2 0.0 copy-start.2
  17.2 1.9 %inner.1.refs_0_ = f32[2,4,5,128,128]{4,3,2,1,0:T(8,128)S(1)} custom-call(f32[2,5,128,8,128]{4,3,2,1,0:T(8,128)S(1)} %copy-done.1, f32[2,128,8,128]{3,2,1,0:T(8,128)S(1)} %get-tuple-element.22.winds_ref.refs_2_), custom_call_target="tpu_custom_call" | custom-call | flops 100000000 | bytes 8000000 | tf_op jit(solution)/shard_map/inner/pallas_call | solution.py:18
  19.1 0.0 copy-start.9
  19.1 0.0 copy-done.4
  19.2 0.0 copy-done.6
  19.2 0.0 copy-done.7
  19.2 0.0 copy-done.8
  19.2 1.6 %weights.1 = (bf16[2048,768]{1,0:T(8,128)(2,1)S(1)}, bf16[128,2048]{1,0:T(8,128)(2,1)S(1)}, bf16[256,256]{1,0:T(8,128)(2,1)S(1)}) custom-call(bf16[640,2048]{1,0:T(8,128)(2,1)S(1)} %copy-done.4, f32[1,2048]{1,0:T(1,128)S(1)} %bitcast.4, bf16[2048,128]{1,0:T(8,128)(2,1)S(1)} %copy-done.6, f32[128,128]{1,0:T(8,128)S(1)} %copy-done.7), custom_call_target="tpu_custom_call" | custom-call | flops 100000000 | bytes 7000000 | tf_op jit(solution)/shard_map/weights/pallas_call | solution.py:18
  20.8 0.0 copy-done.9
  20.8 0.1 bitcast_multiply_fusion.refs_3_
  20.9 8.5 %collective-permute-done.above_ref = bf16[2,10,128,128]{3,2,1,0:T(8,128)(2,1)S(1)} collective-permute-done((bf16[2,10,128,128]{3,2,1,0:T(8,128)(2,1)}, bf16[2,10,128,128]{3,2,1,0:T(8,128)(2,1)S(1)}, u32[]{:S(2)}, u32[]{:S(2)}) %collective-permute-start) | collective-permute-done | bytes 655392 | tf_op jit(solution)/shard_map/ppermute | solution.py:354
  29.4 0.0 collective-permute-done.1.below_ref.refs_9_
  29.4 0.0 copy-done.2
  29.4 2.3 %edge.1 = (f32[2,4,5,128,128]{4,3,2,1,0:T(8,128)S(1)}, bf16[2,10,128,128]{3,2,1,0:T(8,128)(2,1)S(1)}, bf16[2,10,128,128]{3,2,1,0:T(8,128)(2,1)S(1)}) custom-call(f32[2,5,128,8,128]{4,3,2,1,0:T(8,128)S(1)} %copy-done.2, f32[2,128,8,128]{3,2,1,0:T(8,128)S(1)} %get-tuple-element.22.winds_ref.refs_2_, ...), custom_call_target="tpu_custom_call" | custom-call | flops 100000000 | bytes 10000000 | tf_op jit(solution)/shard_map/edge/pallas_call | solution.py:18
  31.7 4.3 %collective-permute-start.2 = (bf16[2,10,128,128]{3,2,1,0:T(8,128)(2,1)S(1)}, bf16[2,10,128,128]{3,2,1,0:T(8,128)(2,1)S(1)}, u32[]{:S(2)}, u32[]{:S(2)}) collective-permute-start(bf16[2,10,128,128]{3,2,1,0:T(8,128)(2,1)S(1)} %get-tuple-element.35), channel_id=1, source_target_pairs={{0,1},{1,2},{2,3},{3,4},{4,5},{5,6},{6,7},{7,8},{8,9},{9,10},{10,1... | collective-permute-start | bytes 1966088 | tf_op jit(solution)/shard_map/ppermute | solution.py:366
  36.0 2.1 %collective-permute-start.3 = (bf16[2,10,128,128]{3,2,1,0:T(8,128)(2,1)S(1)}, bf16[2,10,128,128]{3,2,1,0:T(8,128)(2,1)S(1)}, u32[]{:S(2)}, u32[]{:S(2)}) collective-permute-start(bf16[2,10,128,128]{3,2,1,0:T(8,128)(2,1)S(1)} %get-tuple-element.36), channel_id=1, source_target_pairs={{1,0},{2,1},{3,2},{4,3},{5,4},{6,5},{7,6},{8,7},{9,8},{10,9},{11,1... | collective-permute-start | bytes 1966088 | tf_op jit(solution)/shard_map/ppermute | solution.py:367
  38.1 9.6 %finish_inner.1.refs_10_ = f32[2,4,5,128,128]{4,3,2,1,0:T(8,128)S(1)} custom-call(f32[2,4,5,128,128]{4,3,2,1,0:T(8,128)S(1)} %inner.1.refs_0_, f32[2,4,5,128,128]{4,3,2,1,0:T(8,128)S(1)} %get-tuple-element.30.refs_1_, f32[2,128,8,128]{3,2,1,0:T(8,128)S(1)} %get-tuple-element.22.winds_ref.refs_2_, f32[8,256]{1,0:T(8,128)S(1)} %bitcast_multiply_fusion.refs_3_, ...), custom_call_target="tpu_custom_call" | custom-call | flops 4000000000 | bytes 12000000 | tf_op jit(solution)/shard_map/finish_inner/pallas_call | solution.py:18
  47.7 2.8 %collective-permute-done.2.refs_7_ = bf16[2,10,128,128]{3,2,1,0:T(8,128)(2,1)S(1)} collective-permute-done((bf16[2,10,128,128]{3,2,1,0:T(8,128)(2,1)S(1)}, bf16[2,10,128,128]{3,2,1,0:T(8,128)(2,1)S(1)}, u32[]{:S(2)}, u32[]{:S(2)}) %collective-permute-start.2) | collective-permute-done | bytes 655392 | tf_op jit(solution)/shard_map/ppermute | solution.py:366
  50.5 0.0 collective-permute-done.3.refs_8_
  50.5 11.7 %finish_edges.1 = f32[5,128,8,256]{3,2,1,0:T(8,128)} custom-call(f32[2,4,5,128,128]{4,3,2,1,0:T(8,128)S(1)} %inner.1.refs_0_, f32[2,4,5,128,128]{4,3,2,1,0:T(8,128)S(1)} %get-tuple-element.30.refs_1_, f32[2,128,8,128]{3,2,1,0:T(8,128)S(1)} %get-tuple-element.22.winds_ref.refs_2_, f32[8,256]{1,0:T(8,128)S(1)} %bitcast_multiply_fusion.refs_3_, ...), custom_call_target="tpu_custom_call" | custom-call | flops 4000000000 | bytes 12000000 | tf_op jit(solution)/shard_map/finish_edges/pallas_call | solution.py:18
  (1 shorter events, 0.0 us)
Async XLA Ops:
  0.0 2.5 %copy-start.3 = (f32[5,128,8,256]{3,2,1,0:T(8,128)S(1)}, f32[5,128,8,256]{3,2,1,0:T(8,128)}, u32[]{:S(2)}) copy-start(f32[5,128,8,256]{3,2,1,0:T(8,128)} %state_hbm.1) | copy-start | bytes 15728644
  2.5 1.2 %copy-start.5 = (f32[128,8,256]{2,1,0:T(8,128)S(1)}, f32[128,8,256]{2,1,0:T(8,128)}, u32[]{:S(2)}) copy-start(f32[128,8,256]{2,1,0:T(8,128)} %wind_hbm.1) | copy-start | bytes 3145732
  3.7 10.7 %copy-start.10 = (s32[1,16]{1,0:T(1,128)S(1)}, s32[1,16]{1,0:T(1,128)}, u32[]{:S(2)}) copy-start(s32[1,16]{1,0:T(1,128)} %param.11) | copy-start | bytes 196
  5.6 2.4 %copy-start = (f32[2,5,128,8,128]{4,3,2,1,0:T(8,128)}, f32[2,5,128,8,128]{4,3,2,1,0:T(8,128)S(1)}, u32[]{:S(2)}) copy-start(f32[2,5,128,8,128]{4,3,2,1,0:T(8,128)S(1)} %get-tuple-element.27.kept_ref) | copy-start | bytes 15728644
  7.9 21.5 %collective-permute-start.1 = (bf16[2,12,128,128]{3,2,1,0:T(8,128)(2,1)S(1)}, bf16[2,12,128,128]{3,2,1,0:T(8,128)(2,1)S(1)}, u32[]{:S(2)}, u32[]{:S(2)}) collective-permute-start(bf16[2,12,128,128]{3,2,1,0:T(8,128)(2,1)S(1)} %get-tuple-element.29), channel_id=1, source_target_pairs={{1,0},{2,1},{3,2},{4,3},{5,4},{6,5},{7,6},{8,7},{9,8},{10,9},{11,1... | collective-permute-start | bytes 2359304 | tf_op jit(solution)/shard_map/ppermute | solution.py:355
  9.8 19.6 %collective-permute-start = (bf16[2,10,128,128]{3,2,1,0:T(8,128)(2,1)}, bf16[2,10,128,128]{3,2,1,0:T(8,128)(2,1)S(1)}, u32[]{:S(2)}, u32[]{:S(2)}) collective-permute-start(bf16[2,10,128,128]{3,2,1,0:T(8,128)(2,1)} %get-tuple-element.28), channel_id=1, source_target_pairs={{0,1},{1,2},{2,3},{3,4},{4,5},{5,6},{6,7},{7,8},{8,9},{9,10},{10,1... | collective-permute-start | bytes 1966088 | tf_op jit(solution)/shard_map/ppermute | solution.py:354
  14.7 2.5 %copy-start.1 = (f32[2,5,128,8,128]{4,3,2,1,0:T(8,128)S(1)}, f32[2,5,128,8,128]{4,3,2,1,0:T(8,128)}, u32[]{:S(2)}) copy-start(f32[2,5,128,8,128]{4,3,2,1,0:T(8,128)} %copy-done) | copy-start | bytes 15728644
  17.2 2.0 %copy-start.4 = (bf16[640,2048]{1,0:T(8,128)(2,1)S(1)}, bf16[640,2048]{1,0:T(8,128)(2,1)}, u32[]{:S(2)}) copy-start(bf16[640,2048]{1,0:T(8,128)(2,1)} %first_ref.1) | copy-start | bytes 7864324
  17.2 2.0 %copy-start.6 = (bf16[2048,128]{1,0:T(8,128)(2,1)S(1)}, bf16[2048,128]{1,0:T(8,128)(2,1)}, u32[]{:S(2)}) copy-start(bf16[2048,128]{1,0:T(8,128)(2,1)} %second_ref.1) | copy-start | bytes 1572868
  17.2 2.0 %copy-start.7 = (f32[128,128]{1,0:T(8,128)S(1)}, f32[128,128]{1,0:T(8,128)}, u32[]{:S(2)}) copy-start(f32[128,128]{1,0:T(8,128)} %remap_ref.1) | copy-start | bytes 196612
  17.2 2.0 %copy-start.8 = (f32[2048]{0:T(1024)S(1)}, f32[2048]{0:T(1024)}, u32[]{:S(2)}) copy-start(f32[2048]{0:T(1024)} %param.13) | copy-start | bytes 24580
  17.2 12.2 %copy-start.2 = (f32[2,5,128,8,128]{4,3,2,1,0:T(8,128)S(1)}, f32[2,5,128,8,128]{4,3,2,1,0:T(8,128)}, u32[]{:S(2)}) copy-start(f32[2,5,128,8,128]{4,3,2,1,0:T(8,128)} %copy-done) | copy-start | bytes 15728644
  19.1 1.7 %copy-start.9 = (f32[8,256]{1,0:T(8,128)S(1)}, f32[8,256]{1,0:T(8,128)}, u32[]{:S(2)}) copy-start(f32[8,256]{1,0:T(8,128)} %param.10) | copy-start | bytes 24580
  31.7 18.8 %collective-permute-start.2 = (bf16[2,10,128,128]{3,2,1,0:T(8,128)(2,1)S(1)}, bf16[2,10,128,128]{3,2,1,0:T(8,128)(2,1)S(1)}, u32[]{:S(2)}, u32[]{:S(2)}) collective-permute-start(bf16[2,10,128,128]{3,2,1,0:T(8,128)(2,1)S(1)} %get-tuple-element.35), channel_id=1, source_target_pairs={{0,1},{1,2},{2,3},{3,4},{4,5},{5,6},{6,7},{7,8},{8,9},{9,10},{10,1... | collective-permute-start | bytes 1966088 | tf_op jit(solution)/shard_map/ppermute | solution.py:366
  36.0 14.5 %collective-permute-start.3 = (bf16[2,10,128,128]{3,2,1,0:T(8,128)(2,1)S(1)}, bf16[2,10,128,128]{3,2,1,0:T(8,128)(2,1)S(1)}, u32[]{:S(2)}, u32[]{:S(2)}) collective-permute-start(bf16[2,10,128,128]{3,2,1,0:T(8,128)(2,1)S(1)} %get-tuple-element.36), channel_id=1, source_target_pairs={{1,0},{2,1},{3,2},{4,3},{5,4},{6,5},{7,6},{8,7},{9,8},{10,9},{11,1... | collective-permute-start | bytes 1966088 | tf_op jit(solution)/shard_map/ppermute | solution.py:367

commit v3 on v0

v3 whole, which is shorter than its diff:
```python
import functools
import jax
import jax.numpy as jnp
from jax import lax
from jax.experimental import pallas as pl
from jax.experimental.pallas import tpu as pltpu
from jax.sharding import PartitionSpec as P

LANES = 128
GELU_A = 0.7978845608028654
GELU_B = 0.7978845608028654 * 0.044715
HBM = pl.BlockSpec(memory_space=pltpu.HBM)
VMEM = pl.BlockSpec(memory_space=pltpu.VMEM)
MIB = 1024 * 1024


def call(kernel, name, outs, operands, ins=None, out_specs=None, scratch=(), limit=8, flops=0, moved=0, alias=None):
    return pl.pallas_call(
        kernel,
        in_specs=ins or [VMEM] * len(operands),
        out_specs=out_specs or [VMEM] * len(outs),
        out_shape=outs,
        scratch_shapes=scratch,
        input_output_aliases=alias or {},
        compiler_params=pltpu.CompilerParams(vmem_limit_bytes=limit * MIB),
        cost_estimate=pl.CostEstimate(flops=flops, bytes_accessed=moved, transcendentals=0),
        name=name,
    )(*operands)


def array(shape, dtype=jnp.float32):
    return jax.ShapeDtypeStruct(shape, dtype)


def limited(ahead, behind):
    return jnp.maximum(jnp.minimum(ahead, jnp.maximum(behind, 0.0)), jnp.minimum(behind, 0.0))


def face(speed):
    size = jnp.abs(speed)
    return speed > 0.0, speed, size * (0.5 - 0.5 * size)


def rows_after(q, faces):
    diffs = [b - a for a, b in zip(q[:-1], q[1:])]
    slopes = [None] + [limited(b, a) for a, b in zip(diffs[:-1], diffs[1:])]
    fluxes = []
    for j, (mask, speed, half) in enumerate(faces):
        edge = jnp.where(mask, q[j + 1], q[j + 2])
        slope = jnp.where(mask, slopes[j + 1], slopes[j + 2])
        fluxes.append(speed * edge + half * slope)
    return [q[j + 2] - (fluxes[j + 1] - fluxes[j]) for j in range(len(faces) - 1)]


def row_of(ref, start, count, rows):
    return ref[pl.ds(start, count, stride=rows), :]


def pack_kernel(half, parts, state_hbm, wind_hbm, kept_ref, winds_ref, up_ref, down_ref, sems):
    fields, levels, rows, lanes = kept_ref.shape
    size = levels // parts
    lon = pl.ds(half * lanes, lanes)
    copies = []
    for p in range(parts):
        some = pl.ds(p * size, size)
        made = pltpu.make_async_copy(state_hbm.at[:, some, :, lon], kept_ref.at[:, some], sems.at[p])
        made.start()
        copies.append(made)
    winds = pltpu.make_async_copy(wind_hbm.at[:, :, lon], winds_ref, sems.at[parts])
    winds.start()
    flat = kept_ref.reshape(fields * levels * rows, lanes)
    for p, made in enumerate(copies):
        made.wait()
        here = slice(p * size, (p + 1) * size)
        for f in range(fields):
            base = (f * levels + p * size) * rows
            for r in range(2):
                first = row_of(flat, base + r, size, rows)
                down_ref[r * fields + f, here] = first.astype(jnp.bfloat16)
                last = row_of(flat, base + rows - 2 + r, size, rows)
                up_ref[r * fields + f, here] = last.astype(jnp.bfloat16)
    winds.wait()
    speed = row_of(winds_ref.reshape(levels * rows, lanes), 0, levels, rows)
    high = speed.astype(jnp.bfloat16)
    down_ref[2 * fields] = high
    down_ref[2 * fields + 1] = (speed - high.astype(jnp.float32)).astype(jnp.bfloat16)


def pack(half, state, wind):
    fields, levels, rows, lons = state.shape
    parts = 4
    return call(
        functools.partial(pack_kernel, half, parts), f"pack{half}",
        [
            array((fields, levels, rows, LANES)),
            array((levels, rows, LANES)),
            array((2 * fields, levels, LANES), jnp.bfloat16),
            array((2 * fields + 2, levels, LANES), jnp.bfloat16),
        ],
        (state, wind), ins=[HBM, HBM], scratch=[pltpu.SemaphoreType.DMA((parts + 1,))], moved=5_000_000)


def inner_kernel(kept_ref, winds_ref, out_ref):
    fields, levels, rows, lanes = kept_ref.shape
    step = 8
    flat = kept_ref.reshape(fields * levels * rows, lanes)
    winds = winds_ref.reshape(levels * rows, lanes)

    @pl.loop(0, levels // step)
    def _(i):
        base = i * (step * rows)
        faces = [face(row_of(winds, base + r, step, rows)) for r in range(2, rows - 1)]
        level = pl.multiple_of(i * step, step)
        for f in range(fields):
            q = [row_of(flat, f * levels * rows + base + r, step, rows) for r in range(rows)]
            for r, value in enumerate(rows_after(q, faces)):
                out_ref[r, f, pl.ds(level, step), :] = value


def inner(half, kept, winds):
    fields, levels, rows, lanes = kept.shape
    return call(
        inner_kernel, f"inner{half}", [array((rows - 4, fields, levels, lanes))], (kept, winds),
        flops=50_000_000, moved=4_000_000)[0]


def edge_kernel(kept_ref, winds_ref, above_ref, below_ref, out_ref, up_ref, down_ref):
    fields, levels, rows, lanes = kept_ref.shape
    step = 16
    flat = kept_ref.reshape(fields * levels * rows, lanes)
    winds = winds_ref.reshape(levels * rows, lanes)

    @pl.loop(0, levels // step)
    def _(i):
        base = i * (step * rows)
        here = pl.ds(pl.multiple_of(i * step, step), step)
        wide = lambda ref, index: ref[index, here, :].astype(jnp.float32)
        speeds = {r: row_of(winds, base + r, step, rows) for r in (0, 1, 2, rows - 2, rows - 1)}
        speeds[rows] = wide(below_ref, 2 * fields) + wide(below_ref, 2 * fields + 1)
        for side, first in enumerate((0, rows - 2)):
            faces = [face(speeds[first + j]) for j in range(3)]
            for f in range(fields):
                own = lambda r: row_of(flat, f * levels * rows + base + r, step, rows)
                if side == 0:
                    q = [wide(above_ref, f), wide(above_ref, fields + f)] + [own(r) for r in range(4)]
                else:
                    q = [own(r) for r in range(rows - 4, rows)] + [wide(below_ref, f), wide(below_ref, fields + f)]
                sent = (down_ref, up_ref)[side]
                for r, value in enumerate(rows_after(q, faces)):
                    out_ref[2 * side + r, f, here, :] = value
                    sent[r * fields + f, here, :] = value.astype(jnp.bfloat16)


def edge(half, kept, winds, above, below):
    fields, levels, rows, lanes = kept.shape
    sent = array((2 * fields, levels, lanes), jnp.bfloat16)
    return call(
        edge_kernel, f"edge{half}", [array((4, fields, levels, lanes)), sent, sent],
        (kept, winds, above, below), flops=50_000_000, moved=5_000_000)


def weights_kernel(first_ref, bias_ref, second_ref, remap_ref, first_out, second_out, split_out):
    inputs, hidden = first_ref.shape
    levels = remap_ref.shape[0]
    whole = remap_ref[...]
    r_high = whole.astype(jnp.bfloat16)
    r_low = (whole - r_high.astype(jnp.float32)).astype(jnp.bfloat16)
    for j in range(2):
        split_out[:levels, j * levels : (j + 1) * levels] = r_high
        split_out[levels:, j * levels : (j + 1) * levels] = r_low
    chunk = 256
    same = lambda d: lax.broadcasted_iota(jnp.int32, (chunk, chunk), d)
    unit = jnp.where(same(0) == same(1), 1.0, 0.0).astype(jnp.bfloat16)
    flip = lambda part: lax.dot_general(
        unit, part, (((1,), (1,)), ((), ())), preferred_element_type=jnp.float32).astype(jnp.bfloat16)
    small = unit[:LANES, :LANES]
    row = lax.broadcasted_iota(jnp.int32, (LANES, chunk), 0)
    for j in range(hidden // chunk):
        here = slice(j * chunk, (j + 1) * chunk)
        first_out[here, :inputs] = flip(first_ref[:, here])
        bias = bias_ref[:, here]
        high = bias.astype(jnp.bfloat16).astype(jnp.float32)
        middle = (bias - high).astype(jnp.bfloat16).astype(jnp.float32)
        low = bias - high - middle
        stacked = jnp.where(row == 0, high, jnp.where(row == 1, middle, jnp.where(row == 2, low, 0.0)))
        first_out[here, inputs:] = flip(stacked.astype(jnp.bfloat16))
        second_out[:, here] = lax.dot_general(
            small, second_ref[here, :], (((1,), (1,)), ((), ())),
            preferred_element_type=jnp.float32).astype(jnp.bfloat16)


def weights(w_first, bias, w_second, remap):
    inputs, hidden = w_first.shape
    levels = remap.shape[0]
    outputs = w_second.shape[1]
    return call(
        weights_kernel, "weights",
        [
            array((hidden, inputs + LANES), jnp.bfloat16),
            array((outputs, hidden), jnp.bfloat16),
            array((2 * levels, 2 * levels), jnp.bfloat16),
        ],
        (w_first, bias.reshape(1, hidden), w_second, remap), flops=50_000_000, moved=7_000_000)


def network(x, w1_ref, w2_ref, g_ref):
    hidden = w1_ref.shape[0]
    chunk = 512
    for c in range(hidden // chunk):
        here = slice(c * chunk, (c + 1) * chunk)
        v = jnp.dot(w1_ref[here, :], x, preferred_element_type=jnp.float32)
        h = 0.5 * v
        t = jnp.tanh(v * (GELU_A + GELU_B * (v * v)))
        g_ref[here, :] = (h + h * t).astype(jnp.bfloat16)
    return jnp.dot(w2_ref[...], g_ref[...], preferred_element_type=jnp.float32)


def finish_kernel(edges, half, halves, *refs):
    if edges:
        (days, mid, edg, wnd, sun, rcat, w1, w2, above, below, last, _, *refs) = refs
        (out_hbm, out, a, x, rem, g, sems) = refs[-7:]
    else:
        (days, mid, edg, wnd, sun, rcat, w1, w2, out, a, x, rem, g) = refs
    _, fields, levels, lanes = mid.shape
    rows = wnd.shape[1]
    inputs = fields * levels
    row = lax.broadcasted_iota(jnp.int32, (x.shape[1] - inputs, x.shape[2]), 0)
    for u in range(2):
        x[u, inputs:, :] = jnp.where(row < 3, 1.0, 0.0).astype(jnp.bfloat16)

    step = 16
    winds = wnd.reshape(levels * rows, lanes)

    @pl.loop(0, levels // step)
    def _(i):
        here = pl.ds(pl.multiple_of(i * step, step), step)
        there = pl.ds(pl.multiple_of(levels + i * step, step), step)
        base = i * (step * rows)
        wide = lambda ref, index: ref[index, here, :].astype(jnp.float32)
        if edges:
            needed = (0, 1, 2, rows - 2, rows - 1)
            speeds = {r: row_of(winds, base + r, step, rows) for r in needed}
            speeds[rows] = wide(last, 2 * fields) + wide(last, 2 * fields + 1)
            groups = ((0, 2), (rows - 2, 2))
        else:
            speeds = {r: row_of(winds, base + r, step, rows) for r in range(2, rows - 1)}
            groups = ((2, 4),)
        for first, many in groups:
            faces = [face(speeds[first + j]) for j in range(many + 1)]
            for f in range(fields):
                kept = lambda r: (mid[r - 2, f, here, :] if 2 <= r < rows - 2 else
                                  edg[r if r < 2 else r - rows + 4, f, here, :])
                q = []
                for r in range(first - 2, first + many + 2):
                    if r < 0:
                        q.append(wide(above, (r + 2) * fields + f))
                    elif r >= rows:
                        q.append(wide(below, (r - rows) * fields + f))
                    else:
                        q.append(kept(r))
                for j, value in enumerate(rows_after(q, faces)):
                    if edges:
                        u, place = (0 if first == 0 else 1), j
                    else:
                        u, place = j // 2, j % 2
                    cols = pl.ds(place * lanes, lanes)
                    high = value.astype(jnp.bfloat16)
                    a[u, f, here, cols] = high
                    a[u, f, there, cols] = (value - high.astype(jnp.float32)).astype(jnp.bfloat16)

    starts = (0, rows - 2) if edges else (2, 4)
    flat = out.reshape(fields * levels * rows, lanes)

    def put(f, u, place, value):
        flat[pl.ds(f * levels * rows + starts[u] + place, levels, stride=rows), :] = value

    for u in range(2):
        for f in range(fields):
            both = jnp.dot(rcat[...], a[u, f], preferred_element_type=jnp.float32)
            value = both[:levels] + both[levels:]
            x[u, f * levels : (f + 1) * levels, :] = value.astype(jnp.bfloat16)
            if f == 0:
                rem[u] = value
            else:
                for place in range(2):
                    put(f, u, place, value[:, place * lanes : (place + 1) * lanes])
    stores = []
    lon = pl.ds(half * lanes, lanes)
    if edges:
        most = pl.ds(1, fields - 1)
        made = pltpu.make_async_copy(out.at[most], out_hbm.at[most, :, :, lon], sems.at[0])
        made.start()
        stores.append(made)
    for u in range(2):
        net = network(x[u], w1, w2, g.at[u])
        for place in range(2):
            r = starts[u] + place
            lit = days[0, 0] == r * halves + half
            for i in range(1, days.shape[1]):
                lit = jnp.logical_or(lit, days[0, i] == r * halves + half)
            part = slice(place * lanes, (place + 1) * lanes)
            light = sun[r : r + 1, half * lanes : (half + 1) * lanes] * jnp.where(lit, 1.0, 0.0)
            put(0, u, place, rem[u, :, part] + net[:, part] * light)
    if edges:
        made = pltpu.make_async_copy(out.at[0], out_hbm.at[0, :, :, lon], sems.at[1])
        made.start()
        stores.append(made)
    for made in stores:
        made.wait()


def finish(edges, half, halves, days, mid, edge_rows, wind, sun, rcat, w1, w2, *more):
    _, fields, levels, lanes = mid.shape
    rows = wind.shape[1]
    scratch = [
        pltpu.VMEM((2, fields, 2 * levels, 2 * lanes), jnp.bfloat16),
        pltpu.VMEM((2, w1.shape[1], 2 * lanes), jnp.bfloat16),
        pltpu.VMEM((2, levels, 2 * lanes), jnp.float32),
        pltpu.VMEM((2, w1.shape[0], 2 * lanes), jnp.bfloat16),
    ]
    operands = (days, mid, edge_rows, wind, sun, rcat, w1, w2) + more
    ins = [pl.BlockSpec(memory_space=pltpu.SMEM)] + [VMEM] * (len(operands) - 1)
    outs = [array((fields, levels, rows, lanes))]
    out_specs = [VMEM]
    alias = {}
    if edges:
        scratch.append(pltpu.SemaphoreType.DMA((2,)))
        outs = [array((fields, levels, rows, halves * lanes))] + outs
        out_specs = [HBM, VMEM]
        alias = {11: 1}
        if len(operands) > 12:
            ins[12] = HBM
            alias[12] = 0
    return call(
        functools.partial(finish_kernel, edges, half, halves), f"finish_{'edges' if edges else 'inner'}{half}", outs,
        operands, ins=ins, out_specs=out_specs, scratch=scratch, alias=alias,
        limit=16, flops=2_000_000_000, moved=6_000_000)[0]


def shards(state, wind, sunlight, day_list, w_first, bias, w_second, remap):
    halves = state.shape[3] // LANES
    count = lax.axis_size("lat")
    forward = [(i, i + 1) for i in range(count - 1)]
    back = [(i + 1, i) for i in range(count - 1)]
    every = range(halves)
    state = pltpu.with_memory_space_constraint(state, pltpu.HBM)
    wind = pltpu.with_memory_space_constraint(wind, pltpu.HBM)
    kept, winds, above, below, mid = [], [], [], [], []
    for h in every:
        k, w, up, down = pack(h, state, wind)
        kept.append(k)
        winds.append(w)
        above.append(lax.ppermute(up, "lat", forward))
        below.append(lax.ppermute(down, "lat", back))
    for h in every:
        mid.append(inner(h, kept[h], winds[h]))
    w1, w2, rcat = weights(w_first, bias, w_second, remap)
    mid, w1, w2, rcat, above[0], below[0] = lax.optimization_barrier((mid, w1, w2, rcat, above[0], below[0]))
    edges, above2, below2, partial = [], [], [], []
    for h in every:
        rows, up, down = edge(h, kept[h], winds[h], above[h], below[h])
        edges.append(rows)
        above2.append(lax.ppermute(up, "lat", forward))
        below2.append(lax.ppermute(down, "lat", back))
        partial.append(finish(False, h, halves, day_list, mid[h], rows, winds[h], sunlight, rcat, w1, w2))
        if h + 1 < halves:
            above[h + 1], below[h + 1], partial[h] = lax.optimization_barrier((above[h + 1], below[h + 1], partial[h]))
    above2[0], below2[0], partial = lax.optimization_barrier((above2[0], below2[0], partial))
    out = ()
    for h in every:
        more = (above2[h], below2[h], below[h], partial[h]) + out
        out = (finish(True, h, halves, day_list, mid[h], edges[h], winds[h], sunlight, rcat, w1, w2, *more),)
        if h + 1 < halves:
            above2[h + 1], below2[h + 1], out = lax.optimization_barrier((above2[h + 1], below2[h + 1], out))
    return out[0]


def solution(mesh):
    placed = (
        P("member", None, "lat", None),
        P("member", "lat", None),
        P(("member", "lat"), None),
        P(("member", "lat"), None),
        P(),
        P(),
        P(),
        P(),
    )
    return jax.shard_map(
        shards,
        mesh=mesh,
        in_specs=placed,
        out_specs=P("member", None, "lat", None),
        check_vma=False,
    )
```

time: 198 us -> 55.6 us (0.28)
  the two profiles are of different devices: /device:TPU:22 before, /device:TPU:10 now
where the time goes in v3:
time: 55.6 us; the launch traced here: 55.3 us
  Pallas kernels  29.7 us (53%)
  starting transfers between devices  24.3 us (44%)
  local copies, waits for them, and re-layouts  0.84 us (2%)
    pallas_call x11, Pallas kernels, call(): pl.pallas_call(kernel, in_specs=ins or [VMEM] * len(operands), out_specs=...  29.7 us
    ppermute x2, starting transfers between devices, shards(): below2.append(lax.ppermute(down, 'lat', back))  9.29 us
    ppermute x2, starting transfers between devices, shards(): below.append(lax.ppermute(down, 'lat', back))  7.29 us
    ppermute x2, starting transfers between devices, shards(): above.append(lax.ppermute(up, 'lat', forward))  3.84 us
    ppermute x2, starting transfers between devices, shards(): above2.append(lax.ppermute(up, 'lat', forward))  3.84 us
  transfers between devices with their start and end apart: 8, of which 0 were waited for; matrix products, arithmetic and copies ran while one was open for 0% of the time, Pallas kernels for 40%

profile of v3, /device:TPU:10, one launch (start us, length us, event | category | flops | bytes accessed | tf_op | source)
XLA Modules:
  0.0 55.3 jit_solution(7199016615673050373)
XLA Ops:
  0.0 1.9 %pack0.1 = (f32[5,128,8,128]{3,2,1,0:T(8,128)S(1)}, f32[128,8,128]{2,1,0:T(8,128)S(1)}, bf16[10,128,128]{2,1,0:T(8,128)(2,1)S(1)}, bf16[12,128,128]{2,1,0:T(8,128)(2,1)S(1)}) custom-call(f32[5,128,8,256]{3,2,1,0:T(8,128)} %state_hbm.3, f32[128,8,256]{2,1,0:T(8,128)} %wind_hbm.3), custom_call_target="tpu_custom_call" | custom-call | bytes 5000000 | tf_op jit(solution)/shard_map/pack0/pallas_call | solution.py:18
  1.9 2.8 %collective-permute-start.1 = (bf16[12,128,128]{2,1,0:T(8,128)(2,1)S(1)}, bf16[12,128,128]{2,1,0:T(8,128)(2,1)S(1)}, u32[]{:S(2)}, u32[]{:S(2)}) collective-permute-start(bf16[12,128,128]{2,1,0:T(8,128)(2,1)S(1)} %get-tuple-element.49), channel_id=1, source_target_pairs={{1,0},{2,1},{3,2},{4,3},{5,4},{6,5},{7,6},{8,7},{9,8},{10,9},{11,1... | collective-permute-start | bytes 1179656 | tf_op jit(solution)/shard_map/ppermute | solution.py:354
  4.7 1.9 %collective-permute-start = (bf16[10,128,128]{2,1,0:T(8,128)(2,1)S(1)}, bf16[10,128,128]{2,1,0:T(8,128)(2,1)S(1)}, u32[]{:S(2)}, u32[]{:S(2)}) collective-permute-start(bf16[10,128,128]{2,1,0:T(8,128)(2,1)S(1)} %get-tuple-element.48), channel_id=1, source_target_pairs={{0,1},{1,2},{2,3},{3,4},{4,5},{5,6},{6,7},{7,8},{8,9},{9,10},{10,1... | collective-permute-start | bytes 983048 | tf_op jit(solution)/shard_map/ppermute | solution.py:353
  6.6 1.9 %pack1.1 = (f32[5,128,8,128]{3,2,1,0:T(8,128)S(1)}, f32[128,8,128]{2,1,0:T(8,128)S(1)}, bf16[10,128,128]{2,1,0:T(8,128)(2,1)S(1)}, bf16[12,128,128]{2,1,0:T(8,128)(2,1)S(1)}) custom-call(f32[5,128,8,256]{3,2,1,0:T(8,128)} %state_hbm.3, f32[128,8,256]{2,1,0:T(8,128)} %wind_hbm.3), custom_call_target="tpu_custom_call" | custom-call | bytes 5000000 | tf_op jit(solution)/shard_map/pack1/pallas_call | solution.py:18
  8.6 4.5 %collective-permute-start.3 = (bf16[12,128,128]{2,1,0:T(8,128)(2,1)S(1)}, bf16[12,128,128]{2,1,0:T(8,128)(2,1)S(1)}, u32[]{:S(2)}, u32[]{:S(2)}) collective-permute-start(bf16[12,128,128]{2,1,0:T(8,128)(2,1)S(1)} %get-tuple-element.52), channel_id=1, source_target_pairs={{1,0},{2,1},{3,2},{4,3},{5,4},{6,5},{7,6},{8,7},{9,8},{10,9},{11,1... | collective-permute-start | bytes 1179656 | tf_op jit(solution)/shard_map/ppermute | solution.py:354
  13.1 1.9 %collective-permute-start.2 = (bf16[10,128,128]{2,1,0:T(8,128)(2,1)S(1)}, bf16[10,128,128]{2,1,0:T(8,128)(2,1)S(1)}, u32[]{:S(2)}, u32[]{:S(2)}) collective-permute-start(bf16[10,128,128]{2,1,0:T(8,128)(2,1)S(1)} %get-tuple-element.51), channel_id=1, source_target_pairs={{0,1},{1,2},{2,3},{3,4},{4,5},{5,6},{6,7},{7,8},{8,9},{9,10},{10,1... | collective-permute-start | bytes 983048 | tf_op jit(solution)/shard_map/ppermute | solution.py:353
  15.1 1.0 %inner1.1.refs_1_ = f32[4,5,128,128]{3,2,1,0:T(8,128)S(1)} custom-call(f32[5,128,8,128]{3,2,1,0:T(8,128)S(1)} %get-tuple-element.43.kept_ref, f32[128,8,128]{2,1,0:T(8,128)S(1)} %get-tuple-element.44.winds_ref.refs_3_), custom_call_target="tpu_custom_call" | custom-call | flops 50000000 | bytes 4000000 | tf_op jit(solution)/shard_map/inner1/pallas_call | solution.py:18
  16.0 0.0 copy-start
  16.1 0.0 copy-start.1
  16.1 0.0 copy-start.3
  16.1 0.0 copy-start.4
  16.1 1.0 %inner0.1.refs_1_ = f32[4,5,128,128]{3,2,1,0:T(8,128)S(1)} custom-call(f32[5,128,8,128]{3,2,1,0:T(8,128)S(1)} %get-tuple-element.41.kept_ref, f32[128,8,128]{2,1,0:T(8,128)S(1)} %get-tuple-element.42.winds_ref.refs_3_), custom_call_target="tpu_custom_call" | custom-call | flops 50000000 | bytes 4000000 | tf_op jit(solution)/shard_map/inner0/pallas_call | solution.py:18
  17.1 0.7 %copy-done = bf16[640,2048]{1,0:T(8,128)(2,1)S(1)} copy-done((bf16[640,2048]{1,0:T(8,128)(2,1)S(1)}, bf16[640,2048]{1,0:T(8,128)(2,1)}, u32[]{:S(2)}) %copy-start) | copy-done | bytes 2621464
  17.8 0.1 copy-done.1
  17.9 0.0 copy-done.3
  17.9 0.0 copy-done.4
  17.9 1.6 %weights.1 = (bf16[2048,768]{1,0:T(8,128)(2,1)S(1)}, bf16[128,2048]{1,0:T(8,128)(2,1)S(1)}, bf16[256,256]{1,0:T(8,128)(2,1)S(1)}) custom-call(bf16[640,2048]{1,0:T(8,128)(2,1)S(1)} %copy-done, f32[1,2048]{1,0:T(1,128)S(1)} %bitcast.1, bf16[2048,128]{1,0:T(8,128)(2,1)S(1)} %copy-done.1, f32[128,128]{1,0:T(8,128)S(1)} %copy-done.3), custom_call_target="tpu_custom_call" | custom-call | flops 50000000 | bytes 7000000 | tf_op jit(solution)/shard_map/weights/pallas_call | solution.py:18
  19.5 0.0 copy-start.2
  19.5 0.0 copy-start.5
  19.5 0.0 collective-permute-done.above_ref
  19.5 0.0 collective-permute-done.1.below_ref.refs_10_
  19.5 1.1 %edge0.1 = (f32[4,5,128,128]{3,2,1,0:T(8,128)S(1)}, bf16[10,128,128]{2,1,0:T(8,128)(2,1)S(1)}, bf16[10,128,128]{2,1,0:T(8,128)(2,1)S(1)}) custom-call(f32[5,128,8,128]{3,2,1,0:T(8,128)S(1)} %get-tuple-element.41.kept_ref, f32[128,8,128]{2,1,0:T(8,128)S(1)} %get-tuple-element.42.winds_ref.refs_3_, bf16[10,128,128]{2,1,0:T(8,128)(2,1)S(1)} %collective-permute-done.above_ref, ...), custom_call_target="tpu_custom_call" | custom-call | flops 50000000 | bytes 5000000 | tf_op jit(solution)/shard_map/edge0/pallas_call | solution.py:18
  20.7 1.9 %collective-permute-start.6 = (bf16[10,128,128]{2,1,0:T(8,128)(2,1)S(1)}, bf16[10,128,128]{2,1,0:T(8,128)(2,1)S(1)}, u32[]{:S(2)}, u32[]{:S(2)}) collective-permute-start(bf16[10,128,128]{2,1,0:T(8,128)(2,1)S(1)} %get-tuple-element.65), channel_id=1, source_target_pairs={{0,1},{1,2},{2,3},{3,4},{4,5},{5,6},{6,7},{7,8},{8,9},{9,10},{10,1... | collective-permute-start | bytes 983048 | tf_op jit(solution)/shard_map/ppermute | solution.py:363
  22.6 4.6 %collective-permute-start.7 = (bf16[10,128,128]{2,1,0:T(8,128)(2,1)S(1)}, bf16[10,128,128]{2,1,0:T(8,128)(2,1)S(1)}, u32[]{:S(2)}, u32[]{:S(2)}) collective-permute-start(bf16[10,128,128]{2,1,0:T(8,128)(2,1)S(1)} %get-tuple-element.66), channel_id=1, source_target_pairs={{1,0},{2,1},{3,2},{4,3},{5,4},{6,5},{7,6},{8,7},{9,8},{10,9},{11,1... | collective-permute-start | bytes 983048 | tf_op jit(solution)/shard_map/ppermute | solution.py:364
  27.2 0.0 copy-done.2
  27.2 0.0 copy-done.5
  27.2 4.5 %finish_inner0.1.refs_11_ = f32[5,128,8,128]{3,2,1,0:T(8,128)S(1)} custom-call(s32[1,16]{1,0:T(1,128)S(1)} %copy-done.5, f32[4,5,128,128]{3,2,1,0:T(8,128)S(1)} %inner0.1.refs_1_, f32[4,5,128,128]{3,2,1,0:T(8,128)S(1)} %get-tuple-element.56.refs_2_, f32[128,8,128]{2,1,0:T(8,128)S(1)} %get-tuple-element.42.winds_ref.refs_3_, f32[8,256]{1,0:T(8,128)S(1)} %copy-done.2, ...), custom_call_target="tpu_custom_call" | custom-call | flops 2000000000 | bytes 6000000 | tf_op jit(solution)/shard_map/finish_inner0/pallas_call | solution.py:18
  31.7 0.0 collective-permute-done.2.above_ref
  31.7 0.0 collective-permute-done.3.below_ref.refs_10_
  31.7 1.1 %edge1.1 = (f32[4,5,128,128]{3,2,1,0:T(8,128)S(1)}, bf16[10,128,128]{2,1,0:T(8,128)(2,1)S(1)}, bf16[10,128,128]{2,1,0:T(8,128)(2,1)S(1)}) custom-call(f32[5,128,8,128]{3,2,1,0:T(8,128)S(1)} %get-tuple-element.43.kept_ref, f32[128,8,128]{2,1,0:T(8,128)S(1)} %get-tuple-element.44.winds_ref.refs_3_, bf16[10,128,128]{2,1,0:T(8,128)(2,1)S(1)} %collective-permute-done.2.above_ref, ...), custom_call_target="tpu_custom_call" | custom-call | flops 50000000 | bytes 5000000 | tf_op jit(solution)/shard_map/edge1/pallas_call | solution.py:18
  32.9 1.9 %collective-permute-start.4 = (bf16[10,128,128]{2,1,0:T(8,128)(2,1)S(1)}, bf16[10,128,128]{2,1,0:T(8,128)(2,1)S(1)}, u32[]{:S(2)}, u32[]{:S(2)}) collective-permute-start(bf16[10,128,128]{2,1,0:T(8,128)(2,1)S(1)} %get-tuple-element.63), channel_id=1, source_target_pairs={{0,1},{1,2},{2,3},{3,4},{4,5},{5,6},{6,7},{7,8},{8,9},{9,10},{10,1... | collective-permute-start | bytes 983048 | tf_op jit(solution)/shard_map/ppermute | solution.py:363
  34.8 4.7 %collective-permute-start.5 = (bf16[10,128,128]{2,1,0:T(8,128)(2,1)S(1)}, bf16[10,128,128]{2,1,0:T(8,128)(2,1)S(1)}, u32[]{:S(2)}, u32[]{:S(2)}) collective-permute-start(bf16[10,128,128]{2,1,0:T(8,128)(2,1)S(1)} %get-tuple-element.64), channel_id=1, source_target_pairs={{1,0},{2,1},{3,2},{4,3},{5,4},{6,5},{7,6},{8,7},{9,8},{10,9},{11,1... | collective-permute-start | bytes 983048 | tf_op jit(solution)/shard_map/ppermute | solution.py:364
  39.5 4.5 %finish_inner1.1.refs_11_ = f32[5,128,8,128]{3,2,1,0:T(8,128)S(1)} custom-call(s32[1,16]{1,0:T(1,128)S(1)} %copy-done.5, f32[4,5,128,128]{3,2,1,0:T(8,128)S(1)} %inner1.1.refs_1_, f32[4,5,128,128]{3,2,1,0:T(8,128)S(1)} %get-tuple-element.62.refs_2_, f32[128,8,128]{2,1,0:T(8,128)S(1)} %get-tuple-element.44.winds_ref.refs_3_, f32[8,256]{1,0:T(8,128)S(1)} %copy-done.2, ...), custom_call_target="tpu_custom_call" | custom-call | flops 2000000000 | bytes 6000000 | tf_op jit(solution)/shard_map/finish_inner1/pallas_call | solution.py:18
  44.0 0.0 collective-permute-done.6.refs_8_
  44.1 0.0 collective-permute-done.7.refs_9_
  44.1 5.5 %finish_edges0.1 = (f32[5,128,8,256]{3,2,1,0:T(8,128)}, f32[5,128,8,128]{3,2,1,0:T(8,128)S(1)}) custom-call(s32[1,16]{1,0:T(1,128)S(1)} %copy-done.5, f32[4,5,128,128]{3,2,1,0:T(8,128)S(1)} %inner0.1.refs_1_, f32[4,5,128,128]{3,2,1,0:T(8,128)S(1)} %get-tuple-element.56.refs_2_, ...), custom_call_target="tpu_custom_call", output_to_operand_aliasing={{1}: (11, {})} | custom-call | flops 2000000000 | bytes 6000000 | tf_op jit(solution)/shard_map/finish_edges0/pallas_call | solution.py:18
  49.6 0.0 collective-permute-done.4.refs_8_
  49.6 0.0 collective-permute-done.5.refs_9_
  49.6 5.5 %finish_edges1.1 = (f32[5,128,8,256]{3,2,1,0:T(8,128)}, f32[5,128,8,128]{3,2,1,0:T(8,128)S(1)}) custom-call(s32[1,16]{1,0:T(1,128)S(1)} %copy-done.5, f32[4,5,128,128]{3,2,1,0:T(8,128)S(1)} %inner1.1.refs_1_, f32[4,5,128,128]{3,2,1,0:T(8,128)S(1)} %get-tuple-element.62.refs_2_, ...), custom_call_target="tpu_custom_call", output_to_operand_aliasing={{1}: (11, {}), {0}: (12, {})} | custom-call | flops 2000000000 | bytes 6000000 | tf_op jit(solution)/shard_map/finish_edges1/pallas_call | solution.py:18
Async XLA Ops:
  1.9 17.6 %collective-permute-start.1 = (bf16[12,128,128]{2,1,0:T(8,128)(2,1)S(1)}, bf16[12,128,128]{2,1,0:T(8,128)(2,1)S(1)}, u32[]{:S(2)}, u32[]{:S(2)}) collective-permute-start(bf16[12,128,128]{2,1,0:T(8,128)(2,1)S(1)} %get-tuple-element.49), channel_id=1, source_target_pairs={{1,0},{2,1},{3,2},{4,3},{5,4},{6,5},{7,6},{8,7},{9,8},{10,9},{11,1... | collective-permute-start | bytes 1179656 | tf_op jit(solution)/shard_map/ppermute | solution.py:354
  4.7 14.8 %collective-permute-start = (bf16[10,128,128]{2,1,0:T(8,128)(2,1)S(1)}, bf16[10,128,128]{2,1,0:T(8,128)(2,1)S(1)}, u32[]{:S(2)}, u32[]{:S(2)}) collective-permute-start(bf16[10,128,128]{2,1,0:T(8,128)(2,1)S(1)} %get-tuple-element.48), channel_id=1, source_target_pairs={{0,1},{1,2},{2,3},{3,4},{4,5},{5,6},{6,7},{7,8},{8,9},{9,10},{10,1... | collective-permute-start | bytes 983048 | tf_op jit(solution)/shard_map/ppermute | solution.py:353
  8.6 23.1 %collective-permute-start.3 = (bf16[12,128,128]{2,1,0:T(8,128)(2,1)S(1)}, bf16[12,128,128]{2,1,0:T(8,128)(2,1)S(1)}, u32[]{:S(2)}, u32[]{:S(2)}) collective-permute-start(bf16[12,128,128]{2,1,0:T(8,128)(2,1)S(1)} %get-tuple-element.52), channel_id=1, source_target_pairs={{1,0},{2,1},{3,2},{4,3},{5,4},{6,5},{7,6},{8,7},{9,8},{10,9},{11,1... | collective-permute-start | bytes 1179656 | tf_op jit(solution)/shard_map/ppermute | solution.py:354
  13.1 18.6 %collective-permute-start.2 = (bf16[10,128,128]{2,1,0:T(8,128)(2,1)S(1)}, bf16[10,128,128]{2,1,0:T(8,128)(2,1)S(1)}, u32[]{:S(2)}, u32[]{:S(2)}) collective-permute-start(bf16[10,128,128]{2,1,0:T(8,128)(2,1)S(1)} %get-tuple-element.51), channel_id=1, source_target_pairs={{0,1},{1,2},{2,3},{3,4},{4,5},{5,6},{6,7},{7,8},{8,9},{9,10},{10,1... | collective-permute-start | bytes 983048 | tf_op jit(solution)/shard_map/ppermute | solution.py:353
  16.0 1.7 %copy-start = (bf16[640,2048]{1,0:T(8,128)(2,1)S(1)}, bf16[640,2048]{1,0:T(8,128)(2,1)}, u32[]{:S(2)}) copy-start(bf16[640,2048]{1,0:T(8,128)(2,1)} %first_ref.1) | copy-start | bytes 7864324
  16.1 1.8 %copy-start.1 = (bf16[2048,128]{1,0:T(8,128)(2,1)S(1)}, bf16[2048,128]{1,0:T(8,128)(2,1)}, u32[]{:S(2)}) copy-start(bf16[2048,128]{1,0:T(8,128)(2,1)} %second_ref.1) | copy-start | bytes 1572868
  16.1 1.8 %copy-start.3 = (f32[128,128]{1,0:T(8,128)S(1)}, f32[128,128]{1,0:T(8,128)}, u32[]{:S(2)}) copy-start(f32[128,128]{1,0:T(8,128)} %remap_ref.1) | copy-start | bytes 196612
  16.1 1.8 %copy-start.4 = (f32[2048]{0:T(1024)S(1)}, f32[2048]{0:T(1024)}, u32[]{:S(2)}) copy-start(f32[2048]{0:T(1024)} %param.13) | copy-start | bytes 24580
  19.5 7.7 %copy-start.2 = (f32[8,256]{1,0:T(8,128)S(1)}, f32[8,256]{1,0:T(8,128)}, u32[]{:S(2)}) copy-start(f32[8,256]{1,0:T(8,128)} %refs_4_.7) | copy-start | bytes 24580
  19.5 7.7 %copy-start.5 = (s32[1,16]{1,0:T(1,128)S(1)}, s32[1,16]{1,0:T(1,128)}, u32[]{:S(2)}) copy-start(s32[1,16]{1,0:T(1,128)} %refs_0_.7) | copy-start | bytes 196
  20.7 23.4 %collective-permute-start.6 = (bf16[10,128,128]{2,1,0:T(8,128)(2,1)S(1)}, bf16[10,128,128]{2,1,0:T(8,128)(2,1)S(1)}, u32[]{:S(2)}, u32[]{:S(2)}) collective-permute-start(bf16[10,128,128]{2,1,0:T(8,128)(2,1)S(1)} %get-tuple-element.65), channel_id=1, source_target_pairs={{0,1},{1,2},{2,3},{3,4},{4,5},{5,6},{6,7},{7,8},{8,9},{9,10},{10,1... | collective-permute-start | bytes 983048 | tf_op jit(solution)/shard_map/ppermute | solution.py:363
  22.6 21.5 %collective-permute-start.7 = (bf16[10,128,128]{2,1,0:T(8,128)(2,1)S(1)}, bf16[10,128,128]{2,1,0:T(8,128)(2,1)S(1)}, u32[]{:S(2)}, u32[]{:S(2)}) collective-permute-start(bf16[10,128,128]{2,1,0:T(8,128)(2,1)S(1)} %get-tuple-element.66), channel_id=1, source_target_pairs={{1,0},{2,1},{3,2},{4,3},{5,4},{6,5},{7,6},{8,7},{9,8},{10,9},{11,1... | collective-permute-start | bytes 983048 | tf_op jit(solution)/shard_map/ppermute | solution.py:364
  32.9 16.7 %collective-permute-start.4 = (bf16[10,128,128]{2,1,0:T(8,128)(2,1)S(1)}, bf16[10,128,128]{2,1,0:T(8,128)(2,1)S(1)}, u32[]{:S(2)}, u32[]{:S(2)}) collective-permute-start(bf16[10,128,128]{2,1,0:T(8,128)(2,1)S(1)} %get-tuple-element.63), channel_id=1, source_target_pairs={{0,1},{1,2},{2,3},{3,4},{4,5},{5,6},{6,7},{7,8},{8,9},{9,10},{10,1... | collective-permute-start | bytes 983048 | tf_op jit(solution)/shard_map/ppermute | solution.py:363
  34.8 14.8 %collective-permute-start.5 = (bf16[10,128,128]{2,1,0:T(8,128)(2,1)S(1)}, bf16[10,128,128]{2,1,0:T(8,128)(2,1)S(1)}, u32[]{:S(2)}, u32[]{:S(2)}) collective-permute-start(bf16[10,128,128]{2,1,0:T(8,128)(2,1)S(1)} %get-tuple-element.64), channel_id=1, source_target_pairs={{1,0},{2,1},{3,2},{4,3},{5,4},{6,5},{7,6},{8,7},{9,8},{10,9},{11,1... | collective-permute-start | bytes 983048 | tf_op jit(solution)/shard_map/ppermute | solution.py:364

commit v4 on v3

--- a/solution.py
+++ b/solution.py
@@ -52,11 +52,20 @@
     return [q[j + 2] - (fluxes[j + 1] - fluxes[j]) for j in range(len(faces) - 1)]
 
 
+def is_even():
+    return lax.rem(lax.axis_index("lat"), 2) == 0
+
+
+def by_parity(body, near, far):
+    pl.when(is_even())(lambda: body(far, near))
+    pl.when(jnp.logical_not(is_even()))(lambda: body(near, far))
+
+
 def row_of(ref, start, count, rows):
     return ref[pl.ds(start, count, stride=rows), :]
 
 
-def pack_kernel(half, parts, state_hbm, wind_hbm, kept_ref, winds_ref, up_ref, down_ref, sems):
+def pack_kernel(half, parts, state_hbm, wind_hbm, kept_ref, winds_ref, near_ref, far_ref, sems):
     fields, levels, rows, lanes = kept_ref.shape
     size = levels // parts
     lon = pl.ds(half * lanes, lanes)
@@ -69,21 +78,23 @@
     winds = pltpu.make_async_copy(wind_hbm.at[:, :, lon], winds_ref, sems.at[parts])
     winds.start()
     flat = kept_ref.reshape(fields * levels * rows, lanes)
+    even = is_even()
     for p, made in enumerate(copies):
         made.wait()
         here = slice(p * size, (p + 1) * size)
         for f in range(fields):
             base = (f * levels + p * size) * rows
             for r in range(2):
-                first = row_of(flat, base + r, size, rows)
-                down_ref[r * fields + f, here] = first.astype(jnp.bfloat16)
-                last = row_of(flat, base + rows - 2 + r, size, rows)
-                up_ref[r * fields + f, here] = last.astype(jnp.bfloat16)
+                for ref, start in ((near_ref, jnp.where(even, rows - 2, 0)), (far_ref, jnp.where(even, 0, rows - 2))):
+                    value = row_of(flat, base + start + r, size, rows)
+                    ref[r * fields + f, here] = value.astype(jnp.bfloat16)
     winds.wait()
     speed = row_of(winds_ref.reshape(levels * rows, lanes), 0, levels, rows)
     high = speed.astype(jnp.bfloat16)
-    down_ref[2 * fields] = high
-    down_ref[2 * fields + 1] = (speed - high.astype(jnp.float32)).astype(jnp.bfloat16)
+    low = (speed - high.astype(jnp.float32)).astype(jnp.bfloat16)
+    for ref in (near_ref, far_ref):
+        ref[2 * fields] = high
+        ref[2 * fields + 1] = low
 
 
 def pack(half, state, wind):
@@ -94,7 +105,7 @@
         [
             array((fields, levels, rows, LANES)),
             array((levels, rows, LANES)),
-            array((2 * fields, levels, LANES), jnp.bfloat16),
+            array((2 * fields + 2, levels, LANES), jnp.bfloat16),
             array((2 * fields + 2, levels, LANES), jnp.bfloat16),
         ],
         (state, wind), ins=[HBM, HBM], scratch=[pltpu.SemaphoreType.DMA((parts + 1,))], moved=5_000_000)
@@ -124,39 +135,45 @@
         flops=50_000_000, moved=4_000_000)[0]
 
 
-def edge_kernel(kept_ref, winds_ref, above_ref, below_ref, out_ref, up_ref, down_ref):
+def edge_kernel(kept_ref, winds_ref, near_in, far_in, out_ref, near_out, far_out):
     fields, levels, rows, lanes = kept_ref.shape
     step = 16
     flat = kept_ref.reshape(fields * levels * rows, lanes)
     winds = winds_ref.reshape(levels * rows, lanes)
 
-    @pl.loop(0, levels // step)
-    def _(i):
-        base = i * (step * rows)
-        here = pl.ds(pl.multiple_of(i * step, step), step)
-        wide = lambda ref, index: ref[index, here, :].astype(jnp.float32)
-        speeds = {r: row_of(winds, base + r, step, rows) for r in (0, 1, 2, rows - 2, rows - 1)}
-        speeds[rows] = wide(below_ref, 2 * fields) + wide(below_ref, 2 * fields + 1)
-        for side, first in enumerate((0, rows - 2)):
-            faces = [face(speeds[first + j]) for j in range(3)]
-            for f in range(fields):
-                own = lambda r: row_of(flat, f * levels * rows + base + r, step, rows)
-                if side == 0:
-                    q = [wide(above_ref, f), wide(above_ref, fields + f)] + [own(r) for r in range(4)]
-                else:
-                    q = [own(r) for r in range(rows - 4, rows)] + [wide(below_ref, f), wide(below_ref, fields + f)]
-                sent = (down_ref, up_ref)[side]
-                for r, value in enumerate(rows_after(q, faces)):
-                    out_ref[2 * side + r, f, here, :] = value
-                    sent[r * fields + f, here, :] = value.astype(jnp.bfloat16)
-
-
-def edge(half, kept, winds, above, below):
+    def body(top, bottom):
+        above_ref, down_ref = top
+        below_ref, up_ref = bottom
+
+        @pl.loop(0, levels // step)
+        def _(i):
+            base = i * (step * rows)
+            here = pl.ds(pl.multiple_of(i * step, step), step)
+            wide = lambda ref, index: ref[index, here, :].astype(jnp.float32)
+            speeds = {r: row_of(winds, base + r, step, rows) for r in (0, 1, 2, rows - 2, rows - 1)}
+            speeds[rows] = wide(below_ref, 2 * fields) + wide(below_ref, 2 * fields + 1)
+            for side, first in enumerate((0, rows - 2)):
+                faces = [face(speeds[first + j]) for j in range(3)]
+                for f in range(fields):
+                    own = lambda r: row_of(flat, f * levels * rows + base + r, step, rows)
+                    if side == 0:
+                        q = [wide(above_ref, f), wide(above_ref, fields + f)] + [own(r) for r in range(4)]
+                    else:
+                        q = [own(r) for r in range(rows - 4, rows)] + [wide(below_ref, f), wide(below_ref, fields + f)]
+                    sent = (down_ref, up_ref)[side]
+                    for r, value in enumerate(rows_after(q, faces)):
+                        out_ref[2 * side + r, f, here, :] = value
+                        sent[r * fields + f, here, :] = value.astype(jnp.bfloat16)
+
+    by_parity(body, (near_in, near_out), (far_in, far_out))
+
+
+def edge(half, kept, winds, near, far):
     fields, levels, rows, lanes = kept.shape
     sent = array((2 * fields, levels, lanes), jnp.bfloat16)
     return call(
         edge_kernel, f"edge{half}", [array((4, fields, levels, lanes)), sent, sent],
-        (kept, winds, above, below), flops=50_000_000, moved=5_000_000)
+        (kept, winds, near, far), flops=50_000_000, moved=5_000_000)
 
 
 def weights_kernel(first_ref, bias_ref, second_ref, remap_ref, first_out, second_out, split_out):
@@ -216,14 +233,28 @@
 
 
 def finish_kernel(edges, half, halves, *refs):
-    if edges:
-        (days, mid, edg, wnd, sun, rcat, w1, w2, above, below, last, _, *refs) = refs
-        (out_hbm, out, a, x, rem, g, sems) = refs[-7:]
+    last_half = edges and half == halves - 1
+    if last_half:
+        (days, mid, edg, wnd, sun, rcat, w1, w2, near2, far2, near1, far1, _, *refs) = refs
+        *ready, out_hbm, out, a, x, rem, g, sems = refs
+    elif edges:
+        (days, mid, edg, wnd, sun, rcat, w1, w2, near2, far2, near1, far1, _, out, a, x, rem, g) = refs
     else:
         (days, mid, edg, wnd, sun, rcat, w1, w2, out, a, x, rem, g) = refs
     _, fields, levels, lanes = mid.shape
     rows = wnd.shape[1]
     inputs = fields * levels
+    most = pl.ds(1, fields - 1)
+    stores = []
+
+    def store(source, target):
+        made = pltpu.make_async_copy(source, target, sems.at[len(stores)])
+        made.start()
+        stores.append(made)
+
+    if last_half:
+        for h, source in enumerate(ready):
+            store(source, out_hbm.at[:, :, :, pl.ds(h * lanes, lanes)])
     row = lax.broadcasted_iota(jnp.int32, (x.shape[1] - inputs, x.shape[2]), 0)
     for u in range(2):
         x[u, inputs:, :] = jnp.where(row < 3, 1.0, 0.0).astype(jnp.bfloat16)
@@ -231,42 +262,51 @@
     step = 16
     winds = wnd.reshape(levels * rows, lanes)
 
-    @pl.loop(0, levels // step)
-    def _(i):
-        here = pl.ds(pl.multiple_of(i * step, step), step)
-        there = pl.ds(pl.multiple_of(levels + i * step, step), step)
-        base = i * (step * rows)
-        wide = lambda ref, index: ref[index, here, :].astype(jnp.float32)
-        if edges:
-            needed = (0, 1, 2, rows - 2, rows - 1)
-            speeds = {r: row_of(winds, base + r, step, rows) for r in needed}
-            speeds[rows] = wide(last, 2 * fields) + wide(last, 2 * fields + 1)
-            groups = ((0, 2), (rows - 2, 2))
-        else:
-            speeds = {r: row_of(winds, base + r, step, rows) for r in range(2, rows - 1)}
-            groups = ((2, 4),)
-        for first, many in groups:
-            faces = [face(speeds[first + j]) for j in range(many + 1)]
-            for f in range(fields):
-                kept = lambda r: (mid[r - 2, f, here, :] if 2 <= r < rows - 2 else
-                                  edg[r if r < 2 else r - rows + 4, f, here, :])
-                q = []
-                for r in range(first - 2, first + many + 2):
-                    if r < 0:
-                        q.append(wide(above, (r + 2) * fields + f))
-                    elif r >= rows:
-                        q.append(wide(below, (r - rows) * fields + f))
-                    else:
-                        q.append(kept(r))
-                for j, value in enumerate(rows_after(q, faces)):
-                    if edges:
-                        u, place = (0 if first == 0 else 1), j
-                    else:
-                        u, place = j // 2, j % 2
-                    cols = pl.ds(place * lanes, lanes)
-                    high = value.astype(jnp.bfloat16)
-                    a[u, f, here, cols] = high
-                    a[u, f, there, cols] = (value - high.astype(jnp.float32)).astype(jnp.bfloat16)
+    def advance(top, bottom):
+        above, _ = top
+        below, last = bottom
+
+        @pl.loop(0, levels // step)
+        def _(i):
+            here = pl.ds(pl.multiple_of(i * step, step), step)
+            there = pl.ds(pl.multiple_of(levels + i * step, step), step)
+            base = i * (step * rows)
+            wide = lambda ref, index: ref[index, here, :].astype(jnp.float32)
+            if edges:
+                needed = (0, 1, 2, rows - 2, rows - 1)
+                speeds = {r: row_of(winds, base + r, step, rows) for r in needed}
+                speeds[rows] = wide(last, 2 * fields) + wide(last, 2 * fields + 1)
+                groups = ((0, 2), (rows - 2, 2))
+            else:
+                speeds = {r: row_of(winds, base + r, step, rows) for r in range(2, rows - 1)}
+                groups = ((2, 4),)
+            for first, many in groups:
+                faces = [face(speeds[first + j]) for j in range(many + 1)]
+                for f in range(fields):
+                    kept = lambda r: (mid[r - 2, f, here, :] if 2 <= r < rows - 2 else
+                                      edg[r if r < 2 else r - rows + 4, f, here, :])
+                    q = []
+                    for r in range(first - 2, first + many + 2):
+                        if r < 0:
+                            q.append(wide(above, (r + 2) * fields + f))
+                        elif r >= rows:
+                            q.append(wide(below, (r - rows) * fields + f))
+                        else:
+                            q.append(kept(r))
+                    for j, value in enumerate(rows_after(q, faces)):
+                        if edges:
+                            u, place = (0 if first == 0 else 1), j
+                        else:
+                            u, place = j // 2, j % 2
+                        cols = pl.ds(place * lanes, lanes)
+                        high = value.astype(jnp.bfloat16)
+                        a[u, f, here, cols] = high
+                        a[u, f, there, cols] = (value - high.astype(jnp.float32)).astype(jnp.bfloat16)
+
+    if edges:
+        by_parity(advance, (near2, near1), (far2, far1))
+    else:
+        advance((None, None), (None, None))
 
     starts = (0, rows - 2) if edges else (2, 4)
     flat = out.reshape(fields * levels * rows, lanes)
@@ -284,13 +324,9 @@
             else:
                 for place in range(2):
                     put(f, u, place, value[:, place * lanes : (place + 1) * lanes])
-    stores = []
     lon = pl.ds(half * lanes, lanes)
-    if edges:
-        most = pl.ds(1, fields - 1)
-        made = pltpu.make_async_copy(out.at[most], out_hbm.at[most, :, :, lon], sems.at[0])
-        made.start()
-        stores.append(made)
+    if last_half:
+        store(out.at[most], out_hbm.at[most, :, :, lon])
     for u in range(2):
         net = network(x[u], w1, w2, g.at[u])
         for place in range(2):
@@ -301,10 +337,8 @@
             part = slice(place * lanes, (place + 1) * lanes)
             light = sun[r : r + 1, half * lanes : (half + 1) * lanes] * jnp.where(lit, 1.0, 0.0)
             put(0, u, place, rem[u, :, part] + net[:, part] * light)
-    if edges:
-        made = pltpu.make_async_copy(out.at[0], out_hbm.at[0, :, :, lon], sems.at[1])
-        made.start()
-        stores.append(made)
+    if last_half:
+        store(out.at[0], out_hbm.at[0, :, :, lon])
     for made in stores:
         made.wait()
 
@@ -322,15 +356,12 @@
     ins = [pl.BlockSpec(memory_space=pltpu.SMEM)] + [VMEM] * (len(operands) - 1)
     outs = [array((fields, levels, rows, lanes))]
     out_specs = [VMEM]
-    alias = {}
-    if edges:
-        scratch.append(pltpu.SemaphoreType.DMA((2,)))
+    alias = {12: 0} if edges else {}
+    if edges and half == halves - 1:
+        scratch.append(pltpu.SemaphoreType.DMA((halves + 1,)))
         outs = [array((fields, levels, rows, halves * lanes))] + outs
         out_specs = [HBM, VMEM]
-        alias = {11: 1}
-        if len(operands) > 12:
-            ins[12] = HBM
-            alias[12] = 0
+        alias = {12: 1}
     return call(
         functools.partial(finish_kernel, edges, half, halves), f"finish_{'edges' if edges else 'inner'}{half}", outs,
         operands, ins=ins, out_specs=out_specs, scratch=scratch, alias=alias,
@@ -340,39 +371,42 @@
 def shards(state, wind, sunlight, day_list, w_first, bias, w_second, remap):
     halves = state.shape[3] // LANES
     count = lax.axis_size("lat")
-    forward = [(i, i + 1) for i in range(count - 1)]
-    back = [(i + 1, i) for i in range(count - 1)]
+    near_route = [(i, i ^ 1) for i in range(count) if i ^ 1 < count]
+    far_route = [(i, j) for i in range(count) for j in ((i - 1) if i % 2 == 0 else (i + 1),) if 0 <= j < count]
     every = range(halves)
     state = pltpu.with_memory_space_constraint(state, pltpu.HBM)
     wind = pltpu.with_memory_space_constraint(wind, pltpu.HBM)
-    kept, winds, above, below, mid = [], [], [], [], []
+    kept, winds, near, far, mid = [], [], [], [], []
     for h in every:
-        k, w, up, down = pack(h, state, wind)
+        k, w, near_sent, far_sent = pack(h, state, wind)
         kept.append(k)
         winds.append(w)
-        above.append(lax.ppermute(up, "lat", forward))
-        below.append(lax.ppermute(down, "lat", back))
+        far.append(lax.ppermute(far_sent, "lat", far_route))
+        near.append(lax.ppermute(near_sent, "lat", near_route))
     for h in every:
         mid.append(inner(h, kept[h], winds[h]))
     w1, w2, rcat = weights(w_first, bias, w_second, remap)
-    mid, w1, w2, rcat, above[0], below[0] = lax.optimization_barrier((mid, w1, w2, rcat, above[0], below[0]))
-    edges, above2, below2, partial = [], [], [], []
+    mid, w1, w2, rcat, near[0], far[0] = lax.optimization_barrier((mid, w1, w2, rcat, near[0], far[0]))
+    edges, near2, far2, partial = [], [], [], []
     for h in every:
-        rows, up, down = edge(h, kept[h], winds[h], above[h], below[h])
+        rows, near_sent, far_sent = edge(h, kept[h], winds[h], near[h], far[h])
         edges.append(rows)
-        above2.append(lax.ppermute(up, "lat", forward))
-        below2.append(lax.ppermute(down, "lat", back))
+        far2.append(lax.ppermute(far_sent, "lat", far_route))
+        near2.append(lax.ppermute(near_sent, "lat", near_route))
         partial.append(finish(False, h, halves, day_list, mid[h], rows, winds[h], sunlight, rcat, w1, w2))
         if h + 1 < halves:
-            above[h + 1], below[h + 1], partial[h] = lax.optimization_barrier((above[h + 1], below[h + 1], partial[h]))
-    above2[0], below2[0], partial = lax.optimization_barrier((above2[0], below2[0], partial))
-    out = ()
+            near[h + 1], far[h + 1], partial[h] = lax.optimization_barrier((near[h + 1], far[h + 1], partial[h]))
+    near2[0], far2[0], partial = lax.optimization_barrier((near2[0], far2[0], partial))
+    ready = ()
     for h in every:
-        more = (above2[h], below2[h], below[h], partial[h]) + out
-        out = (finish(True, h, halves, day_list, mid[h], edges[h], winds[h], sunlight, rcat, w1, w2, *more),)
-        if h + 1 < halves:
-            above2[h + 1], below2[h + 1], out = lax.optimization_barrier((above2[h + 1], below2[h + 1], out))
-    return out[0]
+        more = (near2[h], far2[h], near[h], far[h], partial[h])
+        if h == halves - 1:
+            more += ready
+        done = finish(True, h, halves, day_list, mid[h], edges[h], winds[h], sunlight, rcat, w1, w2, *more)
+        if h == halves - 1:
+            return done
+        ready += (done,)
+        near2[h + 1], far2[h + 1], ready = lax.optimization_barrier((near2[h + 1], far2[h + 1], ready))
 
 
 def solution(mesh):

time: 55.6 us -> 50.4 us (0.906)
  the two profiles are of different devices: /device:TPU:10 before, /device:TPU:1 now
where the time goes in v4:
time: 50.4 us; the launch traced here: 50.2 us
  Pallas kernels  29.2 us (58%)
  starting transfers between devices  16.7 us (33%)
  waiting for transfers between devices  3.12 us (6%)
  local copies, waits for them, and re-layouts  0.84 us (2%)
    pallas_call x11, Pallas kernels, call(): pl.pallas_call(kernel, in_specs=ins or [VMEM] * len(operands), out_specs=...  29.2 us
    ppermute x2, starting transfers between devices, shards(): far2.append(lax.ppermute(far_sent, 'lat', far_route))  8.37 us
    ppermute x2, starting transfers between devices, shards(): far.append(lax.ppermute(far_sent, 'lat', far_route))  8.04 us
    ppermute x2, waiting for transfers between devices, shards(): far.append(lax.ppermute(far_sent, 'lat', far_route))  3.11 us
  transfers between devices with their start and end apart: 8, of which 1 were waited for; matrix products, arithmetic and copies ran while one was open for 0% of the time, Pallas kernels for 43%

profile of v4, /device:TPU:1, one launch (start us, length us, event | category | flops | bytes accessed | tf_op | source)
XLA Modules:
  0.0 50.2 jit_solution(5882708825994146988)
XLA Ops:
  0.0 1.9 %pack0.1 = (f32[5,128,8,128]{3,2,1,0:T(8,128)S(1)}, f32[128,8,128]{2,1,0:T(8,128)S(1)}, bf16[12,128,128]{2,1,0:T(8,128)(2,1)S(1)}, bf16[12,128,128]{2,1,0:T(8,128)(2,1)S(1)}) custom-call(f32[5,128,8,256]{3,2,1,0:T(8,128)} %state_hbm.3, f32[128,8,256]{2,1,0:T(8,128)} %wind_hbm.3), custom_call_target="tpu_custom_call" | custom-call | bytes 5000000 | tf_op jit(solution)/shard_map/pack0/pallas_call | solution.py:18
  1.9 0.1 collective-permute-start
  2.0 4.5 %collective-permute-start.1 = (bf16[12,128,128]{2,1,0:T(8,128)(2,1)S(1)}, bf16[12,128,128]{2,1,0:T(8,128)(2,1)S(1)}, u32[]{:S(2)}, u32[]{:S(2)}) collective-permute-start(bf16[12,128,128]{2,1,0:T(8,128)(2,1)S(1)} %get-tuple-element.48), channel_id=1, source_target_pairs={{1,2},{2,1},{3,4},{4,3},{5,6},{6,5},{7,8},{8,7},{9,10},{10,9},{11,... | collective-permute-start | bytes 1179656 | tf_op jit(solution)/shard_map/ppermute | solution.py:384
  6.6 1.9 %pack1.1 = (f32[5,128,8,128]{3,2,1,0:T(8,128)S(1)}, f32[128,8,128]{2,1,0:T(8,128)S(1)}, bf16[12,128,128]{2,1,0:T(8,128)(2,1)S(1)}, bf16[12,128,128]{2,1,0:T(8,128)(2,1)S(1)}) custom-call(f32[5,128,8,256]{3,2,1,0:T(8,128)} %state_hbm.3, f32[128,8,256]{2,1,0:T(8,128)} %wind_hbm.3), custom_call_target="tpu_custom_call" | custom-call | bytes 5000000 | tf_op jit(solution)/shard_map/pack1/pallas_call | solution.py:18
  8.5 0.1 collective-permute-start.2
  8.6 3.5 %collective-permute-start.3 = (bf16[12,128,128]{2,1,0:T(8,128)(2,1)S(1)}, bf16[12,128,128]{2,1,0:T(8,128)(2,1)S(1)}, u32[]{:S(2)}, u32[]{:S(2)}) collective-permute-start(bf16[12,128,128]{2,1,0:T(8,128)(2,1)S(1)} %get-tuple-element.51), channel_id=1, source_target_pairs={{1,2},{2,1},{3,4},{4,3},{5,6},{6,5},{7,8},{8,7},{9,10},{10,9},{11,... | collective-permute-start | bytes 1179656 | tf_op jit(solution)/shard_map/ppermute | solution.py:384
  12.1 1.0 %inner1.1.refs_1_ = f32[4,5,128,128]{3,2,1,0:T(8,128)S(1)} custom-call(f32[5,128,8,128]{3,2,1,0:T(8,128)S(1)} %get-tuple-element.42.kept_ref, f32[128,8,128]{2,1,0:T(8,128)S(1)} %get-tuple-element.43.winds_ref.refs_3_), custom_call_target="tpu_custom_call" | custom-call | flops 50000000 | bytes 4000000 | tf_op jit(solution)/shard_map/inner1/pallas_call | solution.py:18
  13.1 0.0 copy-start
  13.1 0.0 copy-start.1
  13.1 0.0 copy-start.3
  13.1 0.0 copy-start.4
  13.1 1.0 %inner0.1.refs_1_ = f32[4,5,128,128]{3,2,1,0:T(8,128)S(1)} custom-call(f32[5,128,8,128]{3,2,1,0:T(8,128)S(1)} %get-tuple-element.40.kept_ref, f32[128,8,128]{2,1,0:T(8,128)S(1)} %get-tuple-element.41.winds_ref.refs_3_), custom_call_target="tpu_custom_call" | custom-call | flops 50000000 | bytes 4000000 | tf_op jit(solution)/shard_map/inner0/pallas_call | solution.py:18
  14.1 0.7 %copy-done = bf16[640,2048]{1,0:T(8,128)(2,1)S(1)} copy-done((bf16[640,2048]{1,0:T(8,128)(2,1)S(1)}, bf16[640,2048]{1,0:T(8,128)(2,1)}, u32[]{:S(2)}) %copy-start) | copy-done | bytes 2621464
  14.8 0.1 copy-done.1
  14.9 0.0 copy-done.3
  14.9 0.0 copy-done.4
  14.9 1.6 %weights.1 = (bf16[2048,768]{1,0:T(8,128)(2,1)S(1)}, bf16[128,2048]{1,0:T(8,128)(2,1)S(1)}, bf16[256,256]{1,0:T(8,128)(2,1)S(1)}) custom-call(bf16[640,2048]{1,0:T(8,128)(2,1)S(1)} %copy-done, f32[1,2048]{1,0:T(1,128)S(1)} %bitcast.1, bf16[2048,128]{1,0:T(8,128)(2,1)S(1)} %copy-done.1, f32[128,128]{1,0:T(8,128)S(1)} %copy-done.3), custom_call_target="tpu_custom_call" | custom-call | flops 50000000 | bytes 7000000 | tf_op jit(solution)/shard_map/weights/pallas_call | solution.py:18
  16.5 0.0 copy-start.2
  16.6 0.0 copy-start.5
  16.6 0.0 collective-permute-done.near_in.refs_10_
  16.6 3.1 %collective-permute-done.1.far_in.refs_11_ = bf16[12,128,128]{2,1,0:T(8,128)(2,1)S(1)} collective-permute-done((bf16[12,128,128]{2,1,0:T(8,128)(2,1)S(1)}, bf16[12,128,128]{2,1,0:T(8,128)(2,1)S(1)}, u32[]{:S(2)}, u32[]{:S(2)}) %collective-permute-start.1) | collective-permute-done | bytes 393248 | tf_op jit(solution)/shard_map/ppermute | solution.py:384
  19.7 1.1 %edge0.1 = (f32[4,5,128,128]{3,2,1,0:T(8,128)S(1)}, bf16[10,128,128]{2,1,0:T(8,128)(2,1)S(1)}, bf16[10,128,128]{2,1,0:T(8,128)(2,1)S(1)}) custom-call(f32[5,128,8,128]{3,2,1,0:T(8,128)S(1)} %get-tuple-element.40.kept_ref, f32[128,8,128]{2,1,0:T(8,128)S(1)} %get-tuple-element.41.winds_ref.refs_3_, ...), custom_call_target="tpu_custom_call" | custom-call | flops 50000000 | bytes 5000000 | tf_op jit(solution)/shard_map/edge0/pallas_call | solution.py:18
  20.8 0.1 collective-permute-start.6
  20.9 4.4 %collective-permute-start.7 = (bf16[10,128,128]{2,1,0:T(8,128)(2,1)S(1)}, bf16[10,128,128]{2,1,0:T(8,128)(2,1)S(1)}, u32[]{:S(2)}, u32[]{:S(2)}) collective-permute-start(bf16[10,128,128]{2,1,0:T(8,128)(2,1)S(1)} %get-tuple-element.65), channel_id=1, source_target_pairs={{1,2},{2,1},{3,4},{4,3},{5,6},{6,5},{7,8},{8,7},{9,10},{10,9},{11,... | collective-permute-start | bytes 983048 | tf_op jit(solution)/shard_map/ppermute | solution.py:394
  25.3 0.0 copy-done.2
  25.3 0.0 copy-done.5
  25.3 4.5 %finish_inner0.1.refs_12_ = f32[5,128,8,128]{3,2,1,0:T(8,128)S(1)} custom-call(s32[1,16]{1,0:T(1,128)S(1)} %copy-done.5, f32[4,5,128,128]{3,2,1,0:T(8,128)S(1)} %inner0.1.refs_1_, f32[4,5,128,128]{3,2,1,0:T(8,128)S(1)} %get-tuple-element.55.refs_2_, f32[128,8,128]{2,1,0:T(8,128)S(1)} %get-tuple-element.41.winds_ref.refs_3_, f32[8,256]{1,0:T(8,128)S(1)} %copy-done.2, ...), custom_call_target="tpu_custom_call" | custom-call | flops 2000000000 | bytes 6000000 | tf_op jit(solution)/shard_map/finish_inner0/pallas_call | solution.py:18
  29.8 0.0 collective-permute-done.2.near_in.refs_10_
  29.9 0.0 collective-permute-done.3.far_in.refs_11_
  29.9 1.2 %edge1.1 = (f32[4,5,128,128]{3,2,1,0:T(8,128)S(1)}, bf16[10,128,128]{2,1,0:T(8,128)(2,1)S(1)}, bf16[10,128,128]{2,1,0:T(8,128)(2,1)S(1)}) custom-call(f32[5,128,8,128]{3,2,1,0:T(8,128)S(1)} %get-tuple-element.42.kept_ref, f32[128,8,128]{2,1,0:T(8,128)S(1)} %get-tuple-element.43.winds_ref.refs_3_, ...), custom_call_target="tpu_custom_call" | custom-call | flops 50000000 | bytes 5000000 | tf_op jit(solution)/shard_map/edge1/pallas_call | solution.py:18
  31.0 0.1 collective-permute-start.4
  31.1 4.0 %collective-permute-start.5 = (bf16[10,128,128]{2,1,0:T(8,128)(2,1)S(1)}, bf16[10,128,128]{2,1,0:T(8,128)(2,1)S(1)}, u32[]{:S(2)}, u32[]{:S(2)}) collective-permute-start(bf16[10,128,128]{2,1,0:T(8,128)(2,1)S(1)} %get-tuple-element.63), channel_id=1, source_target_pairs={{1,2},{2,1},{3,4},{4,3},{5,6},{6,5},{7,8},{8,7},{9,10},{10,9},{11,... | collective-permute-start | bytes 983048 | tf_op jit(solution)/shard_map/ppermute | solution.py:394
  35.1 4.5 %finish_inner1.1.refs_12_ = f32[5,128,8,128]{3,2,1,0:T(8,128)S(1)} custom-call(s32[1,16]{1,0:T(1,128)S(1)} %copy-done.5, f32[4,5,128,128]{3,2,1,0:T(8,128)S(1)} %inner1.1.refs_1_, f32[4,5,128,128]{3,2,1,0:T(8,128)S(1)} %get-tuple-element.61.refs_2_, f32[128,8,128]{2,1,0:T(8,128)S(1)} %get-tuple-element.43.winds_ref.refs_3_, f32[8,256]{1,0:T(8,128)S(1)} %copy-done.2, ...), custom_call_target="tpu_custom_call" | custom-call | flops 2000000000 | bytes 6000000 | tf_op jit(solution)/shard_map/finish_inner1/pallas_call | solution.py:18
  39.6 0.0 collective-permute-done.6.refs_8_
  39.6 0.0 collective-permute-done.7.refs_9_
  39.6 4.7 %finish_edges0.1.refs_13_ = f32[5,128,8,128]{3,2,1,0:T(8,128)S(1)} custom-call(s32[1,16]{1,0:T(1,128)S(1)} %copy-done.5, f32[4,5,128,128]{3,2,1,0:T(8,128)S(1)} %inner0.1.refs_1_, f32[4,5,128,128]{3,2,1,0:T(8,128)S(1)} %get-tuple-element.55.refs_2_, f32[128,8,128]{2,1,0:T(8,128)S(1)} %get-tuple-element.41.winds_ref.refs_3_, ...), custom_call_target="tpu_custom_call", output_to_operand_aliasing={{}: (12, {})} | custom-call | flops 2000000000 | bytes 6000000 | tf_op jit(solution)/shard_map/finish_edges0/pallas_call | solution.py:18
  44.3 0.0 collective-permute-done.4.refs_8_
  44.4 0.0 collective-permute-done.5.refs_9_
  44.4 5.7 %finish_edges1.1 = (f32[5,128,8,256]{3,2,1,0:T(8,128)}, f32[5,128,8,128]{3,2,1,0:T(8,128)S(1)}) custom-call(s32[1,16]{1,0:T(1,128)S(1)} %copy-done.5, f32[4,5,128,128]{3,2,1,0:T(8,128)S(1)} %inner1.1.refs_1_, f32[4,5,128,128]{3,2,1,0:T(8,128)S(1)} %get-tuple-element.61.refs_2_, ...), custom_call_target="tpu_custom_call", output_to_operand_aliasing={{1}: (12, {})} | custom-call | flops 2000000000 | bytes 6000000 | tf_op jit(solution)/shard_map/finish_edges1/pallas_call | solution.py:18
Async XLA Ops:
  1.9 14.6 %collective-permute-start = (bf16[12,128,128]{2,1,0:T(8,128)(2,1)S(1)}, bf16[12,128,128]{2,1,0:T(8,128)(2,1)S(1)}, u32[]{:S(2)}, u32[]{:S(2)}) collective-permute-start(bf16[12,128,128]{2,1,0:T(8,128)(2,1)S(1)} %get-tuple-element.47), channel_id=1, source_target_pairs={{0,1},{1,0},{2,3},{3,2},{4,5},{5,4},{6,7},{7,6},{8,9},{9,8},{10,11... | collective-permute-start | bytes 1179656 | tf_op jit(solution)/shard_map/ppermute | solution.py:385
  2.0 17.7 %collective-permute-start.1 = (bf16[12,128,128]{2,1,0:T(8,128)(2,1)S(1)}, bf16[12,128,128]{2,1,0:T(8,128)(2,1)S(1)}, u32[]{:S(2)}, u32[]{:S(2)}) collective-permute-start(bf16[12,128,128]{2,1,0:T(8,128)(2,1)S(1)} %get-tuple-element.48), channel_id=1, source_target_pairs={{1,2},{2,1},{3,4},{4,3},{5,6},{6,5},{7,8},{8,7},{9,10},{10,9},{11,... | collective-permute-start | bytes 1179656 | tf_op jit(solution)/shard_map/ppermute | solution.py:384
  8.5 21.3 %collective-permute-start.2 = (bf16[12,128,128]{2,1,0:T(8,128)(2,1)S(1)}, bf16[12,128,128]{2,1,0:T(8,128)(2,1)S(1)}, u32[]{:S(2)}, u32[]{:S(2)}) collective-permute-start(bf16[12,128,128]{2,1,0:T(8,128)(2,1)S(1)} %get-tuple-element.50), channel_id=1, source_target_pairs={{0,1},{1,0},{2,3},{3,2},{4,5},{5,4},{6,7},{7,6},{8,9},{9,8},{10,11... | collective-permute-start | bytes 1179656 | tf_op jit(solution)/shard_map/ppermute | solution.py:385
  8.6 21.3 %collective-permute-start.3 = (bf16[12,128,128]{2,1,0:T(8,128)(2,1)S(1)}, bf16[12,128,128]{2,1,0:T(8,128)(2,1)S(1)}, u32[]{:S(2)}, u32[]{:S(2)}) collective-permute-start(bf16[12,128,128]{2,1,0:T(8,128)(2,1)S(1)} %get-tuple-element.51), channel_id=1, source_target_pairs={{1,2},{2,1},{3,4},{4,3},{5,6},{6,5},{7,8},{8,7},{9,10},{10,9},{11,... | collective-permute-start | bytes 1179656 | tf_op jit(solution)/shard_map/ppermute | solution.py:384
  13.1 1.7 %copy-start = (bf16[640,2048]{1,0:T(8,128)(2,1)S(1)}, bf16[640,2048]{1,0:T(8,128)(2,1)}, u32[]{:S(2)}) copy-start(bf16[640,2048]{1,0:T(8,128)(2,1)} %first_ref.1) | copy-start | bytes 7864324
  13.1 1.8 %copy-start.1 = (bf16[2048,128]{1,0:T(8,128)(2,1)S(1)}, bf16[2048,128]{1,0:T(8,128)(2,1)}, u32[]{:S(2)}) copy-start(bf16[2048,128]{1,0:T(8,128)(2,1)} %second_ref.1) | copy-start | bytes 1572868
  13.1 1.8 %copy-start.3 = (f32[128,128]{1,0:T(8,128)S(1)}, f32[128,128]{1,0:T(8,128)}, u32[]{:S(2)}) copy-start(f32[128,128]{1,0:T(8,128)} %remap_ref.1) | copy-start | bytes 196612
  13.1 1.8 %copy-start.4 = (f32[2048]{0:T(1024)S(1)}, f32[2048]{0:T(1024)}, u32[]{:S(2)}) copy-start(f32[2048]{0:T(1024)} %param.13) | copy-start | bytes 24580
  16.5 8.8 %copy-start.2 = (f32[8,256]{1,0:T(8,128)S(1)}, f32[8,256]{1,0:T(8,128)}, u32[]{:S(2)}) copy-start(f32[8,256]{1,0:T(8,128)} %refs_4_.7) | copy-start | bytes 24580
  16.6 8.8 %copy-start.5 = (s32[1,16]{1,0:T(1,128)S(1)}, s32[1,16]{1,0:T(1,128)}, u32[]{:S(2)}) copy-start(s32[1,16]{1,0:T(1,128)} %refs_0_.7) | copy-start | bytes 196
  20.8 18.8 %collective-permute-start.6 = (bf16[10,128,128]{2,1,0:T(8,128)(2,1)S(1)}, bf16[10,128,128]{2,1,0:T(8,128)(2,1)S(1)}, u32[]{:S(2)}, u32[]{:S(2)}) collective-permute-start(bf16[10,128,128]{2,1,0:T(8,128)(2,1)S(1)} %get-tuple-element.64), channel_id=1, source_target_pairs={{0,1},{1,0},{2,3},{3,2},{4,5},{5,4},{6,7},{7,6},{8,9},{9,8},{10,11... | collective-permute-start | bytes 983048 | tf_op jit(solution)/shard_map/ppermute | solution.py:395
  20.9 18.7 %collective-permute-start.7 = (bf16[10,128,128]{2,1,0:T(8,128)(2,1)S(1)}, bf16[10,128,128]{2,1,0:T(8,128)(2,1)S(1)}, u32[]{:S(2)}, u32[]{:S(2)}) collective-permute-start(bf16[10,128,128]{2,1,0:T(8,128)(2,1)S(1)} %get-tuple-element.65), channel_id=1, source_target_pairs={{1,2},{2,1},{3,4},{4,3},{5,6},{6,5},{7,8},{8,7},{9,10},{10,9},{11,... | collective-permute-start | bytes 983048 | tf_op jit(solution)/shard_map/ppermute | solution.py:394
  31.0 13.3 %collective-permute-start.4 = (bf16[10,128,128]{2,1,0:T(8,128)(2,1)S(1)}, bf16[10,128,128]{2,1,0:T(8,128)(2,1)S(1)}, u32[]{:S(2)}, u32[]{:S(2)}) collective-permute-start(bf16[10,128,128]{2,1,0:T(8,128)(2,1)S(1)} %get-tuple-element.62), channel_id=1, source_target_pairs={{0,1},{1,0},{2,3},{3,2},{4,5},{5,4},{6,7},{7,6},{8,9},{9,8},{10,11... | collective-permute-start | bytes 983048 | tf_op jit(solution)/shard_map/ppermute | solution.py:395
  31.1 13.2 %collective-permute-start.5 = (bf16[10,128,128]{2,1,0:T(8,128)(2,1)S(1)}, bf16[10,128,128]{2,1,0:T(8,128)(2,1)S(1)}, u32[]{:S(2)}, u32[]{:S(2)}) collective-permute-start(bf16[10,128,128]{2,1,0:T(8,128)(2,1)S(1)} %get-tuple-element.63), channel_id=1, source_target_pairs={{1,2},{2,1},{3,4},{4,3},{5,6},{6,5},{7,8},{8,7},{9,10},{10,9},{11,... | collective-permute-start | bytes 983048 | tf_op jit(solution)/shard_map/ppermute | solution.py:394

commit v5 on v4

--- a/solution.py
+++ b/solution.py
@@ -374,19 +374,20 @@
     near_route = [(i, i ^ 1) for i in range(count) if i ^ 1 < count]
     far_route = [(i, j) for i in range(count) for j in ((i - 1) if i % 2 == 0 else (i + 1),) if 0 <= j < count]
     every = range(halves)
-    state = pltpu.with_memory_space_constraint(state, pltpu.HBM)
-    wind = pltpu.with_memory_space_constraint(wind, pltpu.HBM)
     kept, winds, near, far, mid = [], [], [], [], []
     for h in every:
-        k, w, near_sent, far_sent = pack(h, state, wind)
+        k, w, near_sent, far_sent = pack(
+            h, pltpu.with_memory_space_constraint(state, pltpu.HBM), pltpu.with_memory_space_constraint(wind, pltpu.HBM))
         kept.append(k)
         winds.append(w)
         far.append(lax.ppermute(far_sent, "lat", far_route))
         near.append(lax.ppermute(near_sent, "lat", near_route))
-    for h in every:
-        mid.append(inner(h, kept[h], winds[h]))
-    w1, w2, rcat = weights(w_first, bias, w_second, remap)
-    mid, w1, w2, rcat, near[0], far[0] = lax.optimization_barrier((mid, w1, w2, rcat, near[0], far[0]))
+        mid.append(inner(h, k, w))
+        if h == 0:
+            w1, w2, rcat = weights(w_first, bias, w_second, remap)
+            wind, w1, w2, rcat, mid[0] = lax.optimization_barrier((wind, w1, w2, rcat, mid[0]))
+        else:
+            near[0], far[0], near_sent, far_sent = lax.optimization_barrier((near[0], far[0], near_sent, far_sent))
     edges, near2, far2, partial = [], [], [], []
     for h in every:
         rows, near_sent, far_sent = edge(h, kept[h], winds[h], near[h], far[h])

time: 50.4 us -> 48.8 us (0.968)
  waiting for transfers between devices: 3.12 us -> 1.76 us
  local copies, waits for them, and re-layouts: 0.84 us -> 0.04 us
    ppermute x2, waiting for transfers between devices: 3.11 us -> 1.75 us  [shards(): far.append(lax.ppermute(far_sent, 'lat', far_route))]
    unnamed x12, local copies, waits for them, and re-layouts: 0.84 us -> 0.04 us
  transfers between devices with their start and end apart: 8 -> 8, of which waited for: 1 -> 1; matrix products, arithmetic and copies ran while one was open for 0% -> 0% of each run, Pallas kernels for 43% -> 44%
where the time goes in v5:
time: 48.8 us; the launch traced here: 48.6 us
  Pallas kernels  29.3 us (60%)
  starting transfers between devices  17.1 us (35%)
  waiting for transfers between devices  1.76 us (4%)
    pallas_call x11, Pallas kernels, call(): pl.pallas_call(kernel, in_specs=ins or [VMEM] * len(operands), out_specs=...  29.3 us
    ppermute x2, starting transfers between devices, shards(): far2.append(lax.ppermute(far_sent, 'lat', far_route))  8.48 us
    ppermute x2, starting transfers between devices, shards(): far.append(lax.ppermute(far_sent, 'lat', far_route))  8.3 us
    ppermute x2, waiting for transfers between devices, shards(): far.append(lax.ppermute(far_sent, 'lat', far_route))  1.75 us
  transfers between devices with their start and end apart: 8, of which 1 were waited for; matrix products, arithmetic and copies ran while one was open for 0% of the time, Pallas kernels for 44%

profile of v5, /device:TPU:1, one launch (start us, length us, event | category | flops | bytes accessed | tf_op | source)
XLA Modules:
  0.0 48.6 jit_solution(11465021694186360782)
XLA Ops:
  0.0 1.9 %pack0.1 = (f32[5,128,8,128]{3,2,1,0:T(8,128)S(1)}, f32[128,8,128]{2,1,0:T(8,128)S(1)}, bf16[12,128,128]{2,1,0:T(8,128)(2,1)S(1)}, bf16[12,128,128]{2,1,0:T(8,128)(2,1)S(1)}) custom-call(f32[5,128,8,256]{3,2,1,0:T(8,128)} %state_hbm.3, f32[128,8,256]{2,1,0:T(8,128)} %wind_hbm.2), custom_call_target="tpu_custom_call" | custom-call | bytes 5000000 | tf_op jit(solution)/shard_map/pack0/pallas_call | solution.py:18
  1.9 0.0 copy-start
  2.0 0.0 copy-start.1
  2.0 0.0 copy-start.3
  2.0 0.0 copy-start.4
  2.0 0.1 collective-permute-start.2
  2.1 4.8 %collective-permute-start.3 = (bf16[12,128,128]{2,1,0:T(8,128)(2,1)S(1)}, bf16[12,128,128]{2,1,0:T(8,128)(2,1)S(1)}, u32[]{:S(2)}, u32[]{:S(2)}) collective-permute-start(bf16[12,128,128]{2,1,0:T(8,128)(2,1)S(1)} %get-tuple-element.52), channel_id=1, source_target_pairs={{1,2},{2,1},{3,4},{4,3},{5,6},{6,5},{7,8},{8,7},{9,10},{10,9},{11,... | collective-permute-start | bytes 1179656 | tf_op jit(solution)/shard_map/ppermute | solution.py:383
  6.9 1.0 %inner0.1.refs_1_ = f32[4,5,128,128]{3,2,1,0:T(8,128)S(1)} custom-call(f32[5,128,8,128]{3,2,1,0:T(8,128)S(1)} %get-tuple-element.43.kept_ref, f32[128,8,128]{2,1,0:T(8,128)S(1)} %get-tuple-element.44.winds_ref.refs_3_), custom_call_target="tpu_custom_call" | custom-call | flops 50000000 | bytes 4000000 | tf_op jit(solution)/shard_map/inner0/pallas_call | solution.py:18
  7.8 0.0 copy-done
  7.9 0.0 copy-done.1
  7.9 0.0 copy-done.3
  7.9 0.0 copy-done.4
  7.9 1.6 %weights.1 = (bf16[2048,768]{1,0:T(8,128)(2,1)S(1)}, bf16[128,2048]{1,0:T(8,128)(2,1)S(1)}, bf16[256,256]{1,0:T(8,128)(2,1)S(1)}) custom-call(bf16[640,2048]{1,0:T(8,128)(2,1)S(1)} %copy-done, f32[1,2048]{1,0:T(1,128)S(1)} %bitcast.1, bf16[2048,128]{1,0:T(8,128)(2,1)S(1)} %copy-done.1, f32[128,128]{1,0:T(8,128)S(1)} %copy-done.3), custom_call_target="tpu_custom_call" | custom-call | flops 50000000 | bytes 7000000 | tf_op jit(solution)/shard_map/weights/pallas_call | solution.py:18
  9.5 1.9 %pack1.1 = (f32[5,128,8,128]{3,2,1,0:T(8,128)S(1)}, f32[128,8,128]{2,1,0:T(8,128)S(1)}, bf16[12,128,128]{2,1,0:T(8,128)(2,1)S(1)}, bf16[12,128,128]{2,1,0:T(8,128)(2,1)S(1)}) custom-call(f32[5,128,8,256]{3,2,1,0:T(8,128)} %state_hbm.3, f32[128,8,256]{2,1,0:T(8,128)} %wind_hbm.2), custom_call_target="tpu_custom_call" | custom-call | bytes 5000000 | tf_op jit(solution)/shard_map/pack1/pallas_call | solution.py:18
  11.4 0.1 collective-permute-start
  11.5 3.5 %collective-permute-start.1 = (bf16[12,128,128]{2,1,0:T(8,128)(2,1)S(1)}, bf16[12,128,128]{2,1,0:T(8,128)(2,1)S(1)}, u32[]{:S(2)}, u32[]{:S(2)}) collective-permute-start(bf16[12,128,128]{2,1,0:T(8,128)(2,1)S(1)} %get-tuple-element.49), channel_id=1, source_target_pairs={{1,2},{2,1},{3,4},{4,3},{5,6},{6,5},{7,8},{8,7},{9,10},{10,9},{11,... | collective-permute-start | bytes 1179656 | tf_op jit(solution)/shard_map/ppermute | solution.py:383
  15.0 1.0 %inner1.1.refs_1_ = f32[4,5,128,128]{3,2,1,0:T(8,128)S(1)} custom-call(f32[5,128,8,128]{3,2,1,0:T(8,128)S(1)} %get-tuple-element.46.kept_ref, f32[128,8,128]{2,1,0:T(8,128)S(1)} %get-tuple-element.47.winds_ref.refs_3_), custom_call_target="tpu_custom_call" | custom-call | flops 50000000 | bytes 4000000 | tf_op jit(solution)/shard_map/inner1/pallas_call | solution.py:18
  16.0 0.0 copy-start.2
  16.0 0.0 copy-start.5
  16.0 0.0 collective-permute-done.2.near_in.refs_10_
  16.1 0.0 collective-permute-done.3.far_in.refs_11_
  16.1 1.2 %edge0.1 = (f32[4,5,128,128]{3,2,1,0:T(8,128)S(1)}, bf16[10,128,128]{2,1,0:T(8,128)(2,1)S(1)}, bf16[10,128,128]{2,1,0:T(8,128)(2,1)S(1)}) custom-call(f32[5,128,8,128]{3,2,1,0:T(8,128)S(1)} %get-tuple-element.43.kept_ref, f32[128,8,128]{2,1,0:T(8,128)S(1)} %get-tuple-element.44.winds_ref.refs_3_, ...), custom_call_target="tpu_custom_call" | custom-call | flops 50000000 | bytes 5000000 | tf_op jit(solution)/shard_map/edge0/pallas_call | solution.py:18
  17.2 0.1 collective-permute-start.6
  17.3 4.1 %collective-permute-start.7 = (bf16[10,128,128]{2,1,0:T(8,128)(2,1)S(1)}, bf16[10,128,128]{2,1,0:T(8,128)(2,1)S(1)}, u32[]{:S(2)}, u32[]{:S(2)}) collective-permute-start(bf16[10,128,128]{2,1,0:T(8,128)(2,1)S(1)} %get-tuple-element.65), channel_id=1, source_target_pairs={{1,2},{2,1},{3,4},{4,3},{5,6},{6,5},{7,8},{8,7},{9,10},{10,9},{11,... | collective-permute-start | bytes 983048 | tf_op jit(solution)/shard_map/ppermute | solution.py:395
  21.4 0.0 copy-done.2
  21.4 0.0 copy-done.5
  21.4 4.5 %finish_inner0.1.refs_12_ = f32[5,128,8,128]{3,2,1,0:T(8,128)S(1)} custom-call(s32[1,16]{1,0:T(1,128)S(1)} %copy-done.5, f32[4,5,128,128]{3,2,1,0:T(8,128)S(1)} %inner0.1.refs_1_, f32[4,5,128,128]{3,2,1,0:T(8,128)S(1)} %get-tuple-element.55.refs_2_, f32[128,8,128]{2,1,0:T(8,128)S(1)} %get-tuple-element.44.winds_ref.refs_3_, f32[8,256]{1,0:T(8,128)S(1)} %copy-done.2, ...), custom_call_target="tpu_custom_call" | custom-call | flops 2000000000 | bytes 6000000 | tf_op jit(solution)/shard_map/finish_inner0/pallas_call | solution.py:18
  26.0 0.0 collective-permute-done.near_in.refs_10_
  26.0 1.7 %collective-permute-done.1.far_in.refs_11_ = bf16[12,128,128]{2,1,0:T(8,128)(2,1)S(1)} collective-permute-done((bf16[12,128,128]{2,1,0:T(8,128)(2,1)S(1)}, bf16[12,128,128]{2,1,0:T(8,128)(2,1)S(1)}, u32[]{:S(2)}, u32[]{:S(2)}) %collective-permute-start.1) | collective-permute-done | bytes 393248 | tf_op jit(solution)/shard_map/ppermute | solution.py:383
  27.7 1.1 %edge1.1 = (f32[4,5,128,128]{3,2,1,0:T(8,128)S(1)}, bf16[10,128,128]{2,1,0:T(8,128)(2,1)S(1)}, bf16[10,128,128]{2,1,0:T(8,128)(2,1)S(1)}) custom-call(f32[5,128,8,128]{3,2,1,0:T(8,128)S(1)} %get-tuple-element.46.kept_ref, f32[128,8,128]{2,1,0:T(8,128)S(1)} %get-tuple-element.47.winds_ref.refs_3_, ...), custom_call_target="tpu_custom_call" | custom-call | flops 50000000 | bytes 5000000 | tf_op jit(solution)/shard_map/edge1/pallas_call | solution.py:18
  28.9 0.1 collective-permute-start.4
  28.9 4.4 %collective-permute-start.5 = (bf16[10,128,128]{2,1,0:T(8,128)(2,1)S(1)}, bf16[10,128,128]{2,1,0:T(8,128)(2,1)S(1)}, u32[]{:S(2)}, u32[]{:S(2)}) collective-permute-start(bf16[10,128,128]{2,1,0:T(8,128)(2,1)S(1)} %get-tuple-element.63), channel_id=1, source_target_pairs={{1,2},{2,1},{3,4},{4,3},{5,6},{6,5},{7,8},{8,7},{9,10},{10,9},{11,... | collective-permute-start | bytes 983048 | tf_op jit(solution)/shard_map/ppermute | solution.py:395
  33.3 4.5 %finish_inner1.1.refs_12_ = f32[5,128,8,128]{3,2,1,0:T(8,128)S(1)} custom-call(s32[1,16]{1,0:T(1,128)S(1)} %copy-done.5, f32[4,5,128,128]{3,2,1,0:T(8,128)S(1)} %inner1.1.refs_1_, f32[4,5,128,128]{3,2,1,0:T(8,128)S(1)} %get-tuple-element.61.refs_2_, f32[128,8,128]{2,1,0:T(8,128)S(1)} %get-tuple-element.47.winds_ref.refs_3_, f32[8,256]{1,0:T(8,128)S(1)} %copy-done.2, ...), custom_call_target="tpu_custom_call" | custom-call | flops 2000000000 | bytes 6000000 | tf_op jit(solution)/shard_map/finish_inner1/pallas_call | solution.py:18
  37.9 0.0 collective-permute-done.6.refs_8_
  37.9 0.0 collective-permute-done.7.refs_9_
  37.9 4.7 %finish_edges0.1.refs_13_ = f32[5,128,8,128]{3,2,1,0:T(8,128)S(1)} custom-call(s32[1,16]{1,0:T(1,128)S(1)} %copy-done.5, f32[4,5,128,128]{3,2,1,0:T(8,128)S(1)} %inner0.1.refs_1_, f32[4,5,128,128]{3,2,1,0:T(8,128)S(1)} %get-tuple-element.55.refs_2_, f32[128,8,128]{2,1,0:T(8,128)S(1)} %get-tuple-element.44.winds_ref.refs_3_, ...), custom_call_target="tpu_custom_call", output_to_operand_aliasing={{}: (12, {})} | custom-call | flops 2000000000 | bytes 6000000 | tf_op jit(solution)/shard_map/finish_edges0/pallas_call | solution.py:18
  42.7 0.0 collective-permute-done.4.refs_8_
  42.7 0.0 collective-permute-done.5.refs_9_
  42.7 5.7 %finish_edges1.1 = (f32[5,128,8,256]{3,2,1,0:T(8,128)}, f32[5,128,8,128]{3,2,1,0:T(8,128)S(1)}) custom-call(s32[1,16]{1,0:T(1,128)S(1)} %copy-done.5, f32[4,5,128,128]{3,2,1,0:T(8,128)S(1)} %inner1.1.refs_1_, f32[4,5,128,128]{3,2,1,0:T(8,128)S(1)} %get-tuple-element.61.refs_2_, ...), custom_call_target="tpu_custom_call", output_to_operand_aliasing={{1}: (12, {})} | custom-call | flops 2000000000 | bytes 6000000 | tf_op jit(solution)/shard_map/finish_edges1/pallas_call | solution.py:18
Async XLA Ops:
  1.9 5.9 %copy-start = (bf16[640,2048]{1,0:T(8,128)(2,1)S(1)}, bf16[640,2048]{1,0:T(8,128)(2,1)}, u32[]{:S(2)}) copy-start(bf16[640,2048]{1,0:T(8,128)(2,1)} %first_ref.1) | copy-start | bytes 7864324
  2.0 5.9 %copy-start.1 = (bf16[2048,128]{1,0:T(8,128)(2,1)S(1)}, bf16[2048,128]{1,0:T(8,128)(2,1)}, u32[]{:S(2)}) copy-start(bf16[2048,128]{1,0:T(8,128)(2,1)} %second_ref.1) | copy-start | bytes 1572868
  2.0 5.9 %copy-start.3 = (f32[128,128]{1,0:T(8,128)S(1)}, f32[128,128]{1,0:T(8,128)}, u32[]{:S(2)}) copy-start(f32[128,128]{1,0:T(8,128)} %remap_ref.1) | copy-start | bytes 196612
  2.0 5.9 %copy-start.4 = (f32[2048]{0:T(1024)S(1)}, f32[2048]{0:T(1024)}, u32[]{:S(2)}) copy-start(f32[2048]{0:T(1024)} %param.13) | copy-start | bytes 24580
  2.0 14.1 %collective-permute-start.2 = (bf16[12,128,128]{2,1,0:T(8,128)(2,1)S(1)}, bf16[12,128,128]{2,1,0:T(8,128)(2,1)S(1)}, u32[]{:S(2)}, u32[]{:S(2)}) collective-permute-start(bf16[12,128,128]{2,1,0:T(8,128)(2,1)S(1)} %get-tuple-element.51), channel_id=1, source_target_pairs={{0,1},{1,0},{2,3},{3,2},{4,5},{5,4},{6,7},{7,6},{8,9},{9,8},{10,11... | collective-permute-start | bytes 1179656 | tf_op jit(solution)/shard_map/ppermute | solution.py:384
  2.1 14.0 %collective-permute-start.3 = (bf16[12,128,128]{2,1,0:T(8,128)(2,1)S(1)}, bf16[12,128,128]{2,1,0:T(8,128)(2,1)S(1)}, u32[]{:S(2)}, u32[]{:S(2)}) collective-permute-start(bf16[12,128,128]{2,1,0:T(8,128)(2,1)S(1)} %get-tuple-element.52), channel_id=1, source_target_pairs={{1,2},{2,1},{3,4},{4,3},{5,6},{6,5},{7,8},{8,7},{9,10},{10,9},{11,... | collective-permute-start | bytes 1179656 | tf_op jit(solution)/shard_map/ppermute | solution.py:383
  11.4 14.5 %collective-permute-start = (bf16[12,128,128]{2,1,0:T(8,128)(2,1)S(1)}, bf16[12,128,128]{2,1,0:T(8,128)(2,1)S(1)}, u32[]{:S(2)}, u32[]{:S(2)}) collective-permute-start(bf16[12,128,128]{2,1,0:T(8,128)(2,1)S(1)} %get-tuple-element.48), channel_id=1, source_target_pairs={{0,1},{1,0},{2,3},{3,2},{4,5},{5,4},{6,7},{7,6},{8,9},{9,8},{10,11... | collective-permute-start | bytes 1179656 | tf_op jit(solution)/shard_map/ppermute | solution.py:384
  11.5 16.2 %collective-permute-start.1 = (bf16[12,128,128]{2,1,0:T(8,128)(2,1)S(1)}, bf16[12,128,128]{2,1,0:T(8,128)(2,1)S(1)}, u32[]{:S(2)}, u32[]{:S(2)}) collective-permute-start(bf16[12,128,128]{2,1,0:T(8,128)(2,1)S(1)} %get-tuple-element.49), channel_id=1, source_target_pairs={{1,2},{2,1},{3,4},{4,3},{5,6},{6,5},{7,8},{8,7},{9,10},{10,9},{11,... | collective-permute-start | bytes 1179656 | tf_op jit(solution)/shard_map/ppermute | solution.py:383
  16.0 5.4 %copy-start.2 = (f32[8,256]{1,0:T(8,128)S(1)}, f32[8,256]{1,0:T(8,128)}, u32[]{:S(2)}) copy-start(f32[8,256]{1,0:T(8,128)} %refs_4_.7) | copy-start | bytes 24580
  16.0 5.4 %copy-start.5 = (s32[1,16]{1,0:T(1,128)S(1)}, s32[1,16]{1,0:T(1,128)}, u32[]{:S(2)}) copy-start(s32[1,16]{1,0:T(1,128)} %refs_0_.7) | copy-start | bytes 196
  17.2 20.6 %collective-permute-start.6 = (bf16[10,128,128]{2,1,0:T(8,128)(2,1)S(1)}, bf16[10,128,128]{2,1,0:T(8,128)(2,1)S(1)}, u32[]{:S(2)}, u32[]{:S(2)}) collective-permute-start(bf16[10,128,128]{2,1,0:T(8,128)(2,1)S(1)} %get-tuple-element.64), channel_id=1, source_target_pairs={{0,1},{1,0},{2,3},{3,2},{4,5},{5,4},{6,7},{7,6},{8,9},{9,8},{10,11... | collective-permute-start | bytes 983048 | tf_op jit(solution)/shard_map/ppermute | solution.py:396
  17.3 20.6 %collective-permute-start.7 = (bf16[10,128,128]{2,1,0:T(8,128)(2,1)S(1)}, bf16[10,128,128]{2,1,0:T(8,128)(2,1)S(1)}, u32[]{:S(2)}, u32[]{:S(2)}) collective-permute-start(bf16[10,128,128]{2,1,0:T(8,128)(2,1)S(1)} %get-tuple-element.65), channel_id=1, source_target_pairs={{1,2},{2,1},{3,4},{4,3},{5,6},{6,5},{7,8},{8,7},{9,10},{10,9},{11,... | collective-permute-start | bytes 983048 | tf_op jit(solution)/shard_map/ppermute | solution.py:395
  28.9 13.8 %collective-permute-start.4 = (bf16[10,128,128]{2,1,0:T(8,128)(2,1)S(1)}, bf16[10,128,128]{2,1,0:T(8,128)(2,1)S(1)}, u32[]{:S(2)}, u32[]{:S(2)}) collective-permute-start(bf16[10,128,128]{2,1,0:T(8,128)(2,1)S(1)} %get-tuple-element.62), channel_id=1, source_target_pairs={{0,1},{1,0},{2,3},{3,2},{4,5},{5,4},{6,7},{7,6},{8,9},{9,8},{10,11... | collective-permute-start | bytes 983048 | tf_op jit(solution)/shard_map/ppermute | solution.py:396
  28.9 13.7 %collective-permute-start.5 = (bf16[10,128,128]{2,1,0:T(8,128)(2,1)S(1)}, bf16[10,128,128]{2,1,0:T(8,128)(2,1)S(1)}, u32[]{:S(2)}, u32[]{:S(2)}) collective-permute-start(bf16[10,128,128]{2,1,0:T(8,128)(2,1)S(1)} %get-tuple-element.63), channel_id=1, source_target_pairs={{1,2},{2,1},{3,4},{4,3},{5,6},{6,5},{7,8},{8,7},{9,10},{10,9},{11,... | collective-permute-start | bytes 983048 | tf_op jit(solution)/shard_map/ppermute | solution.py:395

commit v6 on v5

--- a/solution.py
+++ b/solution.py
@@ -7,6 +7,7 @@
 from jax.sharding import PartitionSpec as P
 
 LANES = 128
+CODE = 80.0
 GELU_A = 0.7978845608028654
 GELU_B = 0.7978845608028654 * 0.044715
 HBM = pl.BlockSpec(memory_space=pltpu.HBM)
@@ -50,6 +51,16 @@
         slope = jnp.where(mask, slopes[j + 1], slopes[j + 2])
         fluxes.append(speed * edge + half * slope)
     return [q[j + 2] - (fluxes[j + 1] - fluxes[j]) for j in range(len(faces) - 1)]
+
+
+def encode(speed):
+    size = jnp.exp(CODE * jnp.abs(speed))
+    return jnp.where(speed < 0.0, -size, size).astype(jnp.bfloat16)
+
+
+def decode(code):
+    size = jnp.log(jnp.maximum(jnp.abs(code), 1.0)) * (1.0 / CODE)
+    return jnp.where(code < 0.0, -size, size)
 
 
 def is_even():
@@ -90,11 +101,9 @@
                     ref[r * fields + f, here] = value.astype(jnp.bfloat16)
     winds.wait()
     speed = row_of(winds_ref.reshape(levels * rows, lanes), 0, levels, rows)
-    high = speed.astype(jnp.bfloat16)
-    low = (speed - high.astype(jnp.float32)).astype(jnp.bfloat16)
+    code = encode(speed)
     for ref in (near_ref, far_ref):
-        ref[2 * fields] = high
-        ref[2 * fields + 1] = low
+        ref[2 * fields] = code
 
 
 def pack(half, state, wind):
@@ -105,8 +114,8 @@
         [
             array((fields, levels, rows, LANES)),
             array((levels, rows, LANES)),
-            array((2 * fields + 2, levels, LANES), jnp.bfloat16),
-            array((2 * fields + 2, levels, LANES), jnp.bfloat16),
+            array((2 * fields + 1, levels, LANES), jnp.bfloat16),
+            array((2 * fields + 1, levels, LANES), jnp.bfloat16),
         ],
         (state, wind), ins=[HBM, HBM], scratch=[pltpu.SemaphoreType.DMA((parts + 1,))], moved=5_000_000)
 
@@ -151,7 +160,7 @@
             here = pl.ds(pl.multiple_of(i * step, step), step)
             wide = lambda ref, index: ref[index, here, :].astype(jnp.float32)
             speeds = {r: row_of(winds, base + r, step, rows) for r in (0, 1, 2, rows - 2, rows - 1)}
-            speeds[rows] = wide(below_ref, 2 * fields) + wide(below_ref, 2 * fields + 1)
+            speeds[rows] = decode(wide(below_ref, 2 * fields))
             for side, first in enumerate((0, rows - 2)):
                 faces = [face(speeds[first + j]) for j in range(3)]
                 for f in range(fields):
@@ -275,7 +284,7 @@
             if edges:
                 needed = (0, 1, 2, rows - 2, rows - 1)
                 speeds = {r: row_of(winds, base + r, step, rows) for r in needed}
-                speeds[rows] = wide(last, 2 * fields) + wide(last, 2 * fields + 1)
+                speeds[rows] = decode(wide(last, 2 * fields))
                 groups = ((0, 2), (rows - 2, 2))
             else:
                 speeds = {r: row_of(winds, base + r, step, rows) for r in range(2, rows - 1)}
@@ -384,10 +393,11 @@
         near.append(lax.ppermute(near_sent, "lat", near_route))
         mid.append(inner(h, k, w))
         if h == 0:
-            w1, w2, rcat = weights(w_first, bias, w_second, remap)
-            wind, w1, w2, rcat, mid[0] = lax.optimization_barrier((wind, w1, w2, rcat, mid[0]))
-        else:
-            near[0], far[0], near_sent, far_sent = lax.optimization_barrier((near[0], far[0], near_sent, far_sent))
+            wind, mid[0] = lax.optimization_barrier((wind, mid[0]))
+        elif h == 1:
+            w_first, near_sent = lax.optimization_barrier((w_first, near_sent))
+    w1, w2, rcat = weights(w_first, bias, w_second, remap)
+    near[0], far[0], mid, w1, w2, rcat = lax.optimization_barrier((near[0], far[0], mid, w1, w2, rcat))
     edges, near2, far2, partial = [], [], [], []
     for h in every:
         rows, near_sent, far_sent = edge(h, kept[h], winds[h], near[h], far[h])

time: 48.8 us -> 49.6 us (1.016)
  starting transfers between devices: 17.1 us -> 19.2 us
  waiting for transfers between devices: 1.76 us -> 0.3 us
    ppermute x2, starting transfers between devices: 8.48 us -> 12 us  [shards(): far2.append(lax.ppermute(far_sent, 'lat', far_route))]
    ppermute x2, starting transfers between devices: 8.3 us -> 6.71 us  [shards(): far.append(lax.ppermute(far_sent, 'lat', far_route))]
    ppermute x2, waiting for transfers between devices: 1.75 us -> 0.28 us  [shards(): far.append(lax.ppermute(far_sent, 'lat', far_route))]
where the time goes in v6:
time: 49.6 us; the launch traced here: 49.4 us
  Pallas kernels  29.4 us (59%)
  starting transfers between devices  19.2 us (39%)
    pallas_call x11, Pallas kernels, call(): pl.pallas_call(kernel, in_specs=ins or [VMEM] * len(operands), out_specs=...  29.4 us
    ppermute x2, starting transfers between devices, shards(): far2.append(lax.ppermute(far_sent, 'lat', far_route))  12 us
    ppermute x2, starting transfers between devices, shards(): far.append(lax.ppermute(far_sent, 'lat', far_route))  6.71 us
  transfers between devices with their start and end apart: 8, of which 1 were waited for; matrix products, arithmetic and copies ran while one was open for 0% of the time, Pallas kernels for 44%

profile of v6, /device:TPU:1, one launch (start us, length us, event | category | flops | bytes accessed | tf_op | source)
XLA Modules:
  0.0 49.4 jit_solution(14340658635258461405)
XLA Ops:
  0.0 1.9 %pack0.1 = (f32[5,128,8,128]{3,2,1,0:T(8,128)S(1)}, f32[128,8,128]{2,1,0:T(8,128)S(1)}, bf16[11,128,128]{2,1,0:T(8,128)(2,1)S(1)}, bf16[11,128,128]{2,1,0:T(8,128)(2,1)S(1)}) custom-call(f32[5,128,8,256]{3,2,1,0:T(8,128)} %state_hbm.3, f32[128,8,256]{2,1,0:T(8,128)} %wind_hbm.2), custom_call_target="tpu_custom_call" | custom-call | bytes 5000000 | tf_op jit(solution)/shard_map/pack0/pallas_call | solution.py:19
  2.0 0.1 collective-permute-start
  2.0 4.5 %collective-permute-start.1 = (bf16[11,128,128]{2,1,0:T(8,128)(2,1)S(1)}, bf16[11,128,128]{2,1,0:T(8,128)(2,1)S(1)}, u32[]{:S(2)}, u32[]{:S(2)}) collective-permute-start(bf16[11,128,128]{2,1,0:T(8,128)(2,1)S(1)} %get-tuple-element.44), channel_id=1, source_target_pairs={{1,2},{2,1},{3,4},{4,3},{5,6},{6,5},{7,8},{8,7},{9,10},{10,9},{11,... | collective-permute-start | bytes 1081352 | tf_op jit(solution)/shard_map/ppermute | solution.py:392
  6.6 1.0 %inner0.1.refs_1_ = f32[4,5,128,128]{3,2,1,0:T(8,128)S(1)} custom-call(f32[5,128,8,128]{3,2,1,0:T(8,128)S(1)} %get-tuple-element.45.kept_ref, f32[128,8,128]{2,1,0:T(8,128)S(1)} %get-tuple-element.46.winds_ref.refs_3_), custom_call_target="tpu_custom_call" | custom-call | flops 50000000 | bytes 4000000 | tf_op jit(solution)/shard_map/inner0/pallas_call | solution.py:19
  7.5 2.0 %pack1.1 = (f32[5,128,8,128]{3,2,1,0:T(8,128)S(1)}, f32[128,8,128]{2,1,0:T(8,128)S(1)}, bf16[11,128,128]{2,1,0:T(8,128)(2,1)S(1)}, bf16[11,128,128]{2,1,0:T(8,128)(2,1)S(1)}) custom-call(f32[5,128,8,256]{3,2,1,0:T(8,128)} %state_hbm.3, f32[128,8,256]{2,1,0:T(8,128)} %wind_hbm.2), custom_call_target="tpu_custom_call" | custom-call | bytes 5000000 | tf_op jit(solution)/shard_map/pack1/pallas_call | solution.py:19
  9.5 0.0 copy-start
  9.5 0.0 copy-start.1
  9.5 0.0 copy-start.3
  9.5 0.0 copy-start.4
  9.6 2.2 %collective-permute-start.3 = (bf16[11,128,128]{2,1,0:T(8,128)(2,1)S(1)}, bf16[11,128,128]{2,1,0:T(8,128)(2,1)S(1)}, u32[]{:S(2)}, u32[]{:S(2)}) collective-permute-start(bf16[11,128,128]{2,1,0:T(8,128)(2,1)S(1)} %get-tuple-element.57), channel_id=1, source_target_pairs={{1,2},{2,1},{3,4},{4,3},{5,6},{6,5},{7,8},{8,7},{9,10},{10,9},{11,... | collective-permute-start | bytes 1081352 | tf_op jit(solution)/shard_map/ppermute | solution.py:392
  11.8 0.1 collective-permute-start.2
  11.8 1.0 %inner1.1.refs_1_ = f32[4,5,128,128]{3,2,1,0:T(8,128)S(1)} custom-call(f32[5,128,8,128]{3,2,1,0:T(8,128)S(1)} %get-tuple-element.49.kept_ref, f32[128,8,128]{2,1,0:T(8,128)S(1)} %get-tuple-element.50.winds_ref.refs_3_), custom_call_target="tpu_custom_call" | custom-call | flops 50000000 | bytes 4000000 | tf_op jit(solution)/shard_map/inner1/pallas_call | solution.py:19
  12.8 0.0 copy-done
  12.8 0.0 copy-done.1
  12.8 0.0 copy-done.3
  12.8 0.0 copy-done.4
  12.8 1.6 %weights.1 = (bf16[2048,768]{1,0:T(8,128)(2,1)S(1)}, bf16[128,2048]{1,0:T(8,128)(2,1)S(1)}, bf16[256,256]{1,0:T(8,128)(2,1)S(1)}) custom-call(bf16[640,2048]{1,0:T(8,128)(2,1)S(1)} %copy-done, f32[1,2048]{1,0:T(1,128)S(1)} %bitcast.1, bf16[2048,128]{1,0:T(8,128)(2,1)S(1)} %copy-done.1, f32[128,128]{1,0:T(8,128)S(1)} %copy-done.3), custom_call_target="tpu_custom_call" | custom-call | flops 50000000 | bytes 7000000 | tf_op jit(solution)/shard_map/weights/pallas_call | solution.py:19
  14.5 0.0 copy-start.2
  14.5 0.0 copy-start.5
  14.5 0.0 collective-permute-done.near_in.refs_10_
  14.5 0.3 collective-permute-done.1.far_in.refs_11_
  14.8 1.2 %edge0.1 = (f32[4,5,128,128]{3,2,1,0:T(8,128)S(1)}, bf16[10,128,128]{2,1,0:T(8,128)(2,1)S(1)}, bf16[10,128,128]{2,1,0:T(8,128)(2,1)S(1)}) custom-call(f32[5,128,8,128]{3,2,1,0:T(8,128)S(1)} %get-tuple-element.45.kept_ref, f32[128,8,128]{2,1,0:T(8,128)S(1)} %get-tuple-element.46.winds_ref.refs_3_, ...), custom_call_target="tpu_custom_call" | custom-call | flops 50000000 | bytes 5000000 | tf_op jit(solution)/shard_map/edge0/pallas_call | solution.py:19
  15.9 0.3 collective-permute-start.6
  16.2 4.5 %collective-permute-start.7 = (bf16[10,128,128]{2,1,0:T(8,128)(2,1)S(1)}, bf16[10,128,128]{2,1,0:T(8,128)(2,1)S(1)}, u32[]{:S(2)}, u32[]{:S(2)}) collective-permute-start(bf16[10,128,128]{2,1,0:T(8,128)(2,1)S(1)} %get-tuple-element.71), channel_id=1, source_target_pairs={{1,2},{2,1},{3,4},{4,3},{5,6},{6,5},{7,8},{8,7},{9,10},{10,9},{11,... | collective-permute-start | bytes 983048 | tf_op jit(solution)/shard_map/ppermute | solution.py:405
  20.8 0.0 copy-done.2
  20.8 0.0 copy-done.5
  20.8 4.5 %finish_inner0.1.refs_12_ = f32[5,128,8,128]{3,2,1,0:T(8,128)S(1)} custom-call(s32[1,16]{1,0:T(1,128)S(1)} %copy-done.5, f32[4,5,128,128]{3,2,1,0:T(8,128)S(1)} %inner0.1.refs_1_, f32[4,5,128,128]{3,2,1,0:T(8,128)S(1)} %get-tuple-element.61.refs_2_, f32[128,8,128]{2,1,0:T(8,128)S(1)} %get-tuple-element.46.winds_ref.refs_3_, f32[8,256]{1,0:T(8,128)S(1)} %copy-done.2, ...), custom_call_target="tpu_custom_call" | custom-call | flops 2000000000 | bytes 6000000 | tf_op jit(solution)/shard_map/finish_inner0/pallas_call | solution.py:19
  25.3 0.0 collective-permute-done.3.far_in.refs_11_
  25.4 0.0 collective-permute-done.2.near_in.refs_10_
  25.4 1.2 %edge1.1 = (f32[4,5,128,128]{3,2,1,0:T(8,128)S(1)}, bf16[10,128,128]{2,1,0:T(8,128)(2,1)S(1)}, bf16[10,128,128]{2,1,0:T(8,128)(2,1)S(1)}) custom-call(f32[5,128,8,128]{3,2,1,0:T(8,128)S(1)} %get-tuple-element.49.kept_ref, f32[128,8,128]{2,1,0:T(8,128)S(1)} %get-tuple-element.50.winds_ref.refs_3_, ...), custom_call_target="tpu_custom_call" | custom-call | flops 50000000 | bytes 5000000 | tf_op jit(solution)/shard_map/edge1/pallas_call | solution.py:19
  26.6 0.1 collective-permute-start.4
  26.6 7.5 %collective-permute-start.5 = (bf16[10,128,128]{2,1,0:T(8,128)(2,1)S(1)}, bf16[10,128,128]{2,1,0:T(8,128)(2,1)S(1)}, u32[]{:S(2)}, u32[]{:S(2)}) collective-permute-start(bf16[10,128,128]{2,1,0:T(8,128)(2,1)S(1)} %get-tuple-element.69), channel_id=1, source_target_pairs={{1,2},{2,1},{3,4},{4,3},{5,6},{6,5},{7,8},{8,7},{9,10},{10,9},{11,... | collective-permute-start | bytes 983048 | tf_op jit(solution)/shard_map/ppermute | solution.py:405
  34.1 4.5 %finish_inner1.1.refs_12_ = f32[5,128,8,128]{3,2,1,0:T(8,128)S(1)} custom-call(s32[1,16]{1,0:T(1,128)S(1)} %copy-done.5, f32[4,5,128,128]{3,2,1,0:T(8,128)S(1)} %inner1.1.refs_1_, f32[4,5,128,128]{3,2,1,0:T(8,128)S(1)} %get-tuple-element.67.refs_2_, f32[128,8,128]{2,1,0:T(8,128)S(1)} %get-tuple-element.50.winds_ref.refs_3_, f32[8,256]{1,0:T(8,128)S(1)} %copy-done.2, ...), custom_call_target="tpu_custom_call" | custom-call | flops 2000000000 | bytes 6000000 | tf_op jit(solution)/shard_map/finish_inner1/pallas_call | solution.py:19
  38.6 0.0 collective-permute-done.6.refs_8_
  38.6 0.0 collective-permute-done.7.refs_9_
  38.7 4.8 %finish_edges0.1.refs_13_ = f32[5,128,8,128]{3,2,1,0:T(8,128)S(1)} custom-call(s32[1,16]{1,0:T(1,128)S(1)} %copy-done.5, f32[4,5,128,128]{3,2,1,0:T(8,128)S(1)} %inner0.1.refs_1_, f32[4,5,128,128]{3,2,1,0:T(8,128)S(1)} %get-tuple-element.61.refs_2_, f32[128,8,128]{2,1,0:T(8,128)S(1)} %get-tuple-element.46.winds_ref.refs_3_, ...), custom_call_target="tpu_custom_call", output_to_operand_aliasing={{}: (12, {})} | custom-call | flops 2000000000 | bytes 6000000 | tf_op jit(solution)/shard_map/finish_edges0/pallas_call | solution.py:19
  43.4 0.0 collective-permute-done.4.refs_8_
  43.4 0.0 collective-permute-done.5.refs_9_
  43.4 5.8 %finish_edges1.1 = (f32[5,128,8,256]{3,2,1,0:T(8,128)}, f32[5,128,8,128]{3,2,1,0:T(8,128)S(1)}) custom-call(s32[1,16]{1,0:T(1,128)S(1)} %copy-done.5, f32[4,5,128,128]{3,2,1,0:T(8,128)S(1)} %inner1.1.refs_1_, f32[4,5,128,128]{3,2,1,0:T(8,128)S(1)} %get-tuple-element.67.refs_2_, ...), custom_call_target="tpu_custom_call", output_to_operand_aliasing={{1}: (12, {})} | custom-call | flops 2000000000 | bytes 6000000 | tf_op jit(solution)/shard_map/finish_edges1/pallas_call | solution.py:19
Async XLA Ops:
  2.0 12.5 %collective-permute-start = (bf16[11,128,128]{2,1,0:T(8,128)(2,1)S(1)}, bf16[11,128,128]{2,1,0:T(8,128)(2,1)S(1)}, u32[]{:S(2)}, u32[]{:S(2)}) collective-permute-start(bf16[11,128,128]{2,1,0:T(8,128)(2,1)S(1)} %get-tuple-element.43), channel_id=1, source_target_pairs={{0,1},{1,0},{2,3},{3,2},{4,5},{5,4},{6,7},{7,6},{8,9},{9,8},{10,11... | collective-permute-start | bytes 1081352 | tf_op jit(solution)/shard_map/ppermute | solution.py:393
  2.0 12.7 %collective-permute-start.1 = (bf16[11,128,128]{2,1,0:T(8,128)(2,1)S(1)}, bf16[11,128,128]{2,1,0:T(8,128)(2,1)S(1)}, u32[]{:S(2)}, u32[]{:S(2)}) collective-permute-start(bf16[11,128,128]{2,1,0:T(8,128)(2,1)S(1)} %get-tuple-element.44), channel_id=1, source_target_pairs={{1,2},{2,1},{3,4},{4,3},{5,6},{6,5},{7,8},{8,7},{9,10},{10,9},{11,... | collective-permute-start | bytes 1081352 | tf_op jit(solution)/shard_map/ppermute | solution.py:392
  9.5 3.3 %copy-start = (bf16[640,2048]{1,0:T(8,128)(2,1)S(1)}, bf16[640,2048]{1,0:T(8,128)(2,1)}, u32[]{:S(2)}) copy-start(bf16[640,2048]{1,0:T(8,128)(2,1)} %first_ref) | copy-start | bytes 7864324
  9.5 3.3 %copy-start.1 = (bf16[2048,128]{1,0:T(8,128)(2,1)S(1)}, bf16[2048,128]{1,0:T(8,128)(2,1)}, u32[]{:S(2)}) copy-start(bf16[2048,128]{1,0:T(8,128)(2,1)} %second_ref.1) | copy-start | bytes 1572868
  9.5 3.3 %copy-start.3 = (f32[128,128]{1,0:T(8,128)S(1)}, f32[128,128]{1,0:T(8,128)}, u32[]{:S(2)}) copy-start(f32[128,128]{1,0:T(8,128)} %remap_ref.1) | copy-start | bytes 196612
  9.5 3.3 %copy-start.4 = (f32[2048]{0:T(1024)S(1)}, f32[2048]{0:T(1024)}, u32[]{:S(2)}) copy-start(f32[2048]{0:T(1024)} %param.13) | copy-start | bytes 24580
  9.6 15.8 %collective-permute-start.3 = (bf16[11,128,128]{2,1,0:T(8,128)(2,1)S(1)}, bf16[11,128,128]{2,1,0:T(8,128)(2,1)S(1)}, u32[]{:S(2)}, u32[]{:S(2)}) collective-permute-start(bf16[11,128,128]{2,1,0:T(8,128)(2,1)S(1)} %get-tuple-element.57), channel_id=1, source_target_pairs={{1,2},{2,1},{3,4},{4,3},{5,6},{6,5},{7,8},{8,7},{9,10},{10,9},{11,... | collective-permute-start | bytes 1081352 | tf_op jit(solution)/shard_map/ppermute | solution.py:392
  11.8 13.6 %collective-permute-start.2 = (bf16[11,128,128]{2,1,0:T(8,128)(2,1)S(1)}, bf16[11,128,128]{2,1,0:T(8,128)(2,1)S(1)}, u32[]{:S(2)}, u32[]{:S(2)}) collective-permute-start(bf16[11,128,128]{2,1,0:T(8,128)(2,1)S(1)} %get-tuple-element.51), channel_id=1, source_target_pairs={{0,1},{1,0},{2,3},{3,2},{4,5},{5,4},{6,7},{7,6},{8,9},{9,8},{10,11... | collective-permute-start | bytes 1081352 | tf_op jit(solution)/shard_map/ppermute | solution.py:393
  14.5 6.3 %copy-start.2 = (f32[8,256]{1,0:T(8,128)S(1)}, f32[8,256]{1,0:T(8,128)}, u32[]{:S(2)}) copy-start(f32[8,256]{1,0:T(8,128)} %refs_4_.7) | copy-start | bytes 24580
  14.5 6.3 %copy-start.5 = (s32[1,16]{1,0:T(1,128)S(1)}, s32[1,16]{1,0:T(1,128)}, u32[]{:S(2)}) copy-start(s32[1,16]{1,0:T(1,128)} %refs_0_.7) | copy-start | bytes 196
  15.9 22.7 %collective-permute-start.6 = (bf16[10,128,128]{2,1,0:T(8,128)(2,1)S(1)}, bf16[10,128,128]{2,1,0:T(8,128)(2,1)S(1)}, u32[]{:S(2)}, u32[]{:S(2)}) collective-permute-start(bf16[10,128,128]{2,1,0:T(8,128)(2,1)S(1)} %get-tuple-element.70), channel_id=1, source_target_pairs={{0,1},{1,0},{2,3},{3,2},{4,5},{5,4},{6,7},{7,6},{8,9},{9,8},{10,11... | collective-permute-start | bytes 983048 | tf_op jit(solution)/shard_map/ppermute | solution.py:406
  16.2 22.4 %collective-permute-start.7 = (bf16[10,128,128]{2,1,0:T(8,128)(2,1)S(1)}, bf16[10,128,128]{2,1,0:T(8,128)(2,1)S(1)}, u32[]{:S(2)}, u32[]{:S(2)}) collective-permute-start(bf16[10,128,128]{2,1,0:T(8,128)(2,1)S(1)} %get-tuple-element.71), channel_id=1, source_target_pairs={{1,2},{2,1},{3,4},{4,3},{5,6},{6,5},{7,8},{8,7},{9,10},{10,9},{11,... | collective-permute-start | bytes 983048 | tf_op jit(solution)/shard_map/ppermute | solution.py:405
  26.6 16.9 %collective-permute-start.4 = (bf16[10,128,128]{2,1,0:T(8,128)(2,1)S(1)}, bf16[10,128,128]{2,1,0:T(8,128)(2,1)S(1)}, u32[]{:S(2)}, u32[]{:S(2)}) collective-permute-start(bf16[10,128,128]{2,1,0:T(8,128)(2,1)S(1)} %get-tuple-element.68), channel_id=1, source_target_pairs={{0,1},{1,0},{2,3},{3,2},{4,5},{5,4},{6,7},{7,6},{8,9},{9,8},{10,11... | collective-permute-start | bytes 983048 | tf_op jit(solution)/shard_map/ppermute | solution.py:406
  26.6 16.8 %collective-permute-start.5 = (bf16[10,128,128]{2,1,0:T(8,128)(2,1)S(1)}, bf16[10,128,128]{2,1,0:T(8,128)(2,1)S(1)}, u32[]{:S(2)}, u32[]{:S(2)}) collective-permute-start(bf16[10,128,128]{2,1,0:T(8,128)(2,1)S(1)} %get-tuple-element.69), channel_id=1, source_target_pairs={{1,2},{2,1},{3,4},{4,3},{5,6},{6,5},{7,8},{8,7},{9,10},{10,9},{11,... | collective-permute-start | bytes 983048 | tf_op jit(solution)/shard_map/ppermute | solution.py:405
